TPU v7x, 32 devices: a whole 2x2x4 slice. The times are simulated.
32 devices in a mesh: parts: 2 (over y), seq: 8 (over z, x), dp: 2 (over core).
Axes of the slice: x: 2, y: 2, z: 4, core: 2. Of those that a mesh axis runs over, the one named last changes fastest.
Arguments:
- features: bfloat16 [4, 1024, 768], P(('parts', 'dp'), 'seq'), parts along dimension 0, may hold values from -6 to 6
- cotangent: bfloat16 [4, 1024, 768], P(('parts', 'dp'), 'seq'), parts along dimension 0, may hold values from -6 to 6
- counts: int32 [4, 1024], P(('parts', 'dp'), 'seq'), parts along dimension 0, may hold values from 0 to 255
- count_weight: float32 [768], replicated, may hold values from -3 to 3
- down_weight: bfloat16 [2, 768, 384], P(None, None, 'dp'), may hold values from -0.21875 to 0.21875
- tap_weight: bfloat16 [2, 3, 384, 384], P(None, None, None, 'dp'), may hold values from -0.1875 to 0.1875
- up_weight: bfloat16 [2, 384, 768], P(None, None, 'dp'), may hold values from -0.3125 to 0.3125
- decay_rate: float32 [4], replicated, may hold values from 7.8125e-05 to 0.0333333333
- keep_share: float32 [4, 1024], P(('parts', 'dp'), 'seq'), parts along dimension 0, may hold values from 0.3 to 1
- mode_weight: float32 [2, 4, 768], replicated, may hold values from -3 to 3
Outputs:
- feature_grad: bfloat16 [4, 1024, 768], P(('parts', 'dp'), 'seq'), parts along dimension 0
- tap_grad: float32 [4608, 384], P(('parts', 'seq', 'dp')), parts along dimension 0
- mode_grad: float32 [16, 768], P('parts', ('seq', 'dp')), parts along dimension 0
There are 2 independent parts, one for each index of `parts`. A program takes and returns all parts, laid end to end along the dimension named above; an argument that names none is the same for every part. Nothing has to cross between parts.
All inputs are finite; a program needn't handle non-finite values.
Results may differ from a plain program's by a relative error of at most 0.011.
Values may be sent and summed in bfloat16 or wider, within the bound.
No kernel may reach another device: no remote copies, remote signals or barrier semaphores. Data moves between devices by JAX's collectives and lax.ppermute only.
A program may use at most 64 MiB of HBM per device.

v0:
```python
import math

import jax
import jax.numpy as jnp
from jax import lax
from jax.sharding import PartitionSpec as P

B = 384
DILATION_FIRST1 = 2048
DILATION_SECOND2 = 4096
M = 4
LAYERS = 2


EPSILON = 1e-06
HALF_ROOT = 1.0 / math.sqrt(2.0)
DENSITY = 1.0 / math.sqrt(2.0 * math.pi)
TOP_PRECISION = lax.Precision.HIGHEST


def shifted(value, axis, steps):
    count = lax.axis_size(axis)
    pairs = [(source, (source + steps) % count) for source in range(count)]
    return lax.ppermute(value, axis, pairs)


def entering_2(shard, axis, join, neutral, backward):
    count = lax.axis_size(axis)
    place = lax.axis_index(axis)
    ahead = count - 1 - place if backward else place
    gathered = jax.tree.map(
        lambda a, kind: lax.all_gather(a.astype(kind), axis),
        shard,
        jax.tree.map(lambda a: jnp.bfloat16 if a.dtype == jnp.float32 else a.dtype, shard),
    )
    state = jax.tree.map(lambda a, e: jnp.zeros_like(a) + jnp.asarray(e, a.dtype), shard, neutral)

    def one(turn, state):
        source = count - 1 - turn if backward else turn
        return join(
            state,
            jax.tree.map(
                lambda a, own: lax.dynamic_index_in_dim(a, source, 0, False).astype(own.dtype),
                gathered,
                shard,
            ),
        )

    return lax.fori_loop(0, ahead, one, state)


def gelu_exact(values):
    return 0.5 * values * (1.0 + lax.erf(values * HALF_ROOT))


def gelu_slope(values):
    cumulative = 0.5 * (1.0 + lax.erf(values * HALF_ROOT))
    return cumulative + values * jnp.exp(-0.5 * values * values) * DENSITY


def project(left_shifted, right_shifted):
    return jnp.einsum(
        "qra,au->qru", left_shifted, right_shifted, preferred_element_type=jnp.float32
    )


def project_back(left_shifted, right_shifted):
    return jnp.einsum(
        "kut,st->kus", left_shifted, right_shifted, preferred_element_type=jnp.float32
    )


def contract(left_shifted, right_shifted):
    return jnp.einsum(
        "glb,glk->bk", left_shifted, right_shifted, preferred_element_type=jnp.float32
    )


def moved(values, bin_distance):
    return shifted(values, "seq", bin_distance)


def block_product(kernel, pieces):
    return jnp.einsum(
        "gmbij,gbjc->gmbic",
        kernel,
        pieces,
        precision=TOP_PRECISION,
        preferred_element_type=jnp.float32,
    )


def modal_local(lg_in, lg_exit, stream_rows, cotangent_rows):
    genome_count, input_rows, mode_count = lg_in.shape
    feature_maps = stream_rows.shape[-1]
    block_size = min(128, input_rows)
    block_count = input_rows // block_size
    running = jnp.cumsum(lg_in, axis=1)
    running_blocks = running.reshape(genome_count, block_count, block_size, mode_count)
    block_ends = running_blocks[:, :, -1, :]
    block_starts = jnp.concatenate(
        [jnp.zeros((genome_count, 1, mode_count), jnp.float32), block_ends[:, :-1, :]], axis=1
    )
    within = running_blocks - block_starts[:, :, None, :]
    within_t = jnp.transpose(within, (0, 3, 1, 2))
    spread = within_t[..., :, None] - within_t[..., None, :]
    row_index = lax.broadcasted_iota(jnp.int32, (block_size, block_size), 0)
    column_index = lax.broadcasted_iota(jnp.int32, (block_size, block_size), 1)
    kernel = jnp.where(row_index >= column_index, jnp.exp(jnp.minimum(spread, 0.0)), 0.0)
    joined_source = jnp.concatenate([stream_rows, cotangent_rows.astype(jnp.float32)], axis=-1)
    joined_source = joined_source.reshape(genome_count, block_count, block_size, 2 * feature_maps)
    partial_value = block_product(kernel, joined_source)
    block_tails = partial_value[:, :, :, -1, :]
    ends_t = jnp.transpose(block_ends, (0, 2, 1))
    starts_t = jnp.transpose(block_starts, (0, 2, 1))
    spacing = starts_t[..., :, None] - ends_t[..., None, :]
    block_index = lax.broadcasted_iota(jnp.int32, (block_count, block_count), 0)
    source_index = lax.broadcasted_iota(jnp.int32, (block_count, block_count), 1)
    linkage = jnp.where(source_index < block_index, jnp.exp(jnp.minimum(spacing, 0.0)), 0.0)
    entering = jnp.einsum(
        "gmbk,gmkc->gmbc",
        linkage,
        block_tails,
        precision=TOP_PRECISION,
        preferred_element_type=jnp.float32,
    )
    states = partial_value + jnp.exp(within_t)[..., None] * entering[:, :, :, None, :]
    states = states.reshape(genome_count, mode_count, input_rows, 2 * feature_maps)
    decay_values = jnp.exp(jnp.transpose(running, (0, 2, 1)))
    exit_state = jnp.exp(lg_exit)[..., None] * states[:, :, -1, :]
    log_pass = running[:, -1, :] + lg_exit
    return (states, decay_values, exit_state, log_pass)


def modal_terms(states, decay_values, entering, cotangent_rows, source_gain, cot_gain):
    feature_maps = cotangent_rows.shape[-1]
    reach_sum = jnp.einsum(
        "qsz,qzj->qsj",
        decay_values,
        cotangent_rows,
        precision=TOP_PRECISION,
        preferred_element_type=jnp.float32,
    )
    totals = jnp.einsum(
        "veyi,vyi->ei",
        states[..., :feature_maps],
        cotangent_rows,
        precision=TOP_PRECISION,
        preferred_element_type=jnp.float32,
    )
    totals = totals + jnp.sum(entering[..., :feature_maps] * reach_sum, axis=0)
    rows_out = jnp.einsum(
        "jryf,rf->jyf",
        states[..., feature_maps:],
        cot_gain,
        precision=TOP_PRECISION,
        preferred_element_type=jnp.float32,
    )
    rows_out = rows_out + jnp.einsum(
        "ert,erx->etx",
        decay_values,
        entering[..., feature_maps:] * cot_gain[None],
        precision=TOP_PRECISION,
        preferred_element_type=jnp.float32,
    )
    return (source_gain[:, None] * totals, rows_out)


def apply_early_first(early_pass, early_state, late_pass, late_state):
    return (early_pass * late_pass, late_pass[..., None] * early_state + late_state)


def apply_late_first(early_pass, early_state, late_pass, late_state):
    return (early_pass * late_pass, early_pass[..., None] * late_state + early_state)


def join_lower(early, late):
    fore_pass, fore_state = apply_early_first(early[0], early[1], late[0], late[1])
    back_pass, back_state = apply_late_first(early[2], early[3], late[2], late[3])
    return (fore_pass, fore_state, back_pass, back_state)


def join_upper(early, late):
    fore_pass, fore_state = apply_late_first(early[0], early[1], late[0], late[1])
    back_pass, back_state = apply_early_first(early[2], early[3], late[2], late[3])
    return (fore_pass, fore_state, back_pass, back_state)


def closed(own_pass, own_state, pass_before, state_before, pass_after, state_after):
    beside_all = pass_before * pass_after
    numerator = (
        beside_all[..., None] * own_state + pass_before[..., None] * state_after + state_before
    )
    return numerator / (1.0 - beside_all * own_pass)[..., None]


def per_device(
    features,
    cotangent,
    counts,
    count_weight,
    down_weight,
    tap_weight,
    up_weight,
    decay_rate,
    keep_share,
    mode_weight,
):
    genome_count = features.shape[0]
    input_rows = features.shape[1]
    down_full, tap_full, full_up_weight = (
        lax.all_gather(down_weight, "dp", axis=2, tiled=True),
        lax.all_gather(tap_weight, "dp", axis=3, tiled=True),
        lax.all_gather(up_weight, "dp", axis=2, tiled=True),
    )
    stream = (
        features.astype(jnp.float32)
        + jnp.log1p(counts.astype(jnp.float32))[..., None] * count_weight
    )
    stored = []
    for layer_position in range(LAYERS):
        bin_distance = (DILATION_FIRST1 if layer_position == 0 else DILATION_SECOND2) // input_rows
        inverse = lax.rsqrt(jnp.mean(stream * stream, axis=-1, keepdims=True) + EPSILON)
        normed = (stream * inverse).astype(jnp.bfloat16)
        reduced = project(normed, down_full[layer_position]).astype(jnp.bfloat16)
        lagged = moved(reduced, bin_distance)
        advanced = moved(reduced, -bin_distance)
        mixture = (
            project(lagged, tap_full[layer_position, 0])
            + project(reduced, tap_full[layer_position, 1])
            + project(advanced, tap_full[layer_position, 2])
        )
        active_modes = gelu_exact(mixture).astype(jnp.bfloat16)
        stored.append((stream, inverse, reduced, lagged, advanced, mixture))
        stream = stream + jnp.einsum(
            "quy,yk->quk",
            active_modes,
            full_up_weight[layer_position],
            preferred_element_type=jnp.float32,
        )
    cot_wide = cotangent.astype(jnp.float32)
    logs = jnp.log(keep_share)[:, :, None] - decay_rate[None, None, :]
    mode_scale = jnp.sqrt(-jnp.expm1(-2.0 * decay_rate))
    fore_states, fore_decays, fore_exit, fore_log = modal_local(
        logs, jnp.zeros_like(logs[:, 0, :]), stream, cotangent
    )
    back_logs = jnp.concatenate(
        [jnp.zeros_like(logs[:, :1, :]), logs[:, ::-1, :][:, :-1, :]], axis=1
    )
    back_states, back_decays, back_exit, back_log = modal_local(
        back_logs, logs[:, 0, :], stream[:, ::-1, :], cotangent[:, ::-1, :]
    )
    summary = (jnp.exp(fore_log), fore_exit, jnp.exp(back_log), back_exit)
    identity = (
        jnp.ones_like(fore_log),
        jnp.zeros_like(fore_exit),
        jnp.ones_like(back_log),
        jnp.zeros_like(back_exit),
    )
    from_lower = entering_2(summary, "seq", join_lower, identity, False)
    from_upper = entering_2(summary, "seq", join_upper, identity, True)
    fore_entry = closed(
        summary[0], summary[1], from_lower[0], from_lower[1], from_upper[0], from_upper[1]
    )
    back_entry = closed(
        summary[2], summary[3], from_upper[2], from_upper[3], from_lower[2], from_lower[3]
    )
    fore_totals, fore_rows = modal_terms(
        fore_states,
        fore_decays,
        fore_entry,
        cot_wide,
        mode_scale,
        mode_scale[:, None] * mode_weight[1],
    )
    back_totals, back_rows = modal_terms(
        back_states,
        back_decays,
        back_entry,
        cot_wide[:, ::-1, :],
        mode_scale,
        mode_scale[:, None] * mode_weight[0],
    )
    gradient = cot_wide + fore_rows + back_rows[:, ::-1, :]
    mode_terms = jnp.stack([fore_totals, back_totals]).reshape(2 * M, -1)
    tap_terms = []
    for layer_position in reversed(range(LAYERS)):
        bin_distance = (DILATION_FIRST1 if layer_position == 0 else DILATION_SECOND2) // input_rows
        before, inverse, reduced, lagged, advanced, mixture = stored[layer_position]
        narrow_width = gradient.astype(jnp.bfloat16)
        back_mixed = jnp.einsum(
            "yhi,ai->yha",
            narrow_width,
            full_up_weight[layer_position],
            preferred_element_type=jnp.float32,
        )
        mixed_grad = (back_mixed * gelu_slope(mixture)).astype(jnp.bfloat16)
        tap_terms.insert(
            0,
            jnp.stack(
                [
                    contract(lagged, mixed_grad),
                    contract(reduced, mixed_grad),
                    contract(advanced, mixed_grad),
                ]
            ),
        )
        reduced_grad = jnp.einsum(
            "glk,bk->glb",
            mixed_grad,
            tap_full[layer_position, 1],
            preferred_element_type=jnp.float32,
        )
        reduced_grad = reduced_grad + jnp.einsum(
            "glk,bk->glb",
            moved(mixed_grad, -bin_distance),
            tap_full[layer_position, 0],
            preferred_element_type=jnp.float32,
        )
        reduced_grad = reduced_grad + jnp.einsum(
            "glk,bk->glb",
            moved(mixed_grad, bin_distance),
            tap_full[layer_position, 2],
            preferred_element_type=jnp.float32,
        )
        normed_grad = project_back(reduced_grad.astype(jnp.bfloat16), down_full[layer_position])
        gradient = (
            gradient
            + inverse * normed_grad
            - before
            * inverse
            * inverse
            * inverse
            * jnp.mean(normed_grad * before, axis=-1, keepdims=True)
        )
    tap_flat = jnp.stack(tap_terms).reshape(LAYERS * 3 * B, B)
    seq_size = lax.axis_size("seq")
    dp_size = lax.axis_size("dp")
    report_scale = 1.0 / math.sqrt(genome_count * dp_size * input_rows * seq_size)
    tap_sum, mode_sum = (
        lax.psum_scatter(tap_flat, ("seq", "dp"), scatter_dimension=0, tiled=True),
        lax.psum_scatter(mode_terms, ("seq", "dp"), scatter_dimension=1, tiled=True),
    )
    return (gradient.astype(jnp.bfloat16), tap_sum * report_scale, mode_sum * report_scale)


def solution(mesh):
    placed = (
        P(("parts", "dp"), "seq", None),
        P(("parts", "dp"), "seq", None),
        P(("parts", "dp"), "seq"),
        P(),
        P(None, None, "dp"),
        P(None, None, None, "dp"),
        P(None, None, "dp"),
        P(),
        P(("parts", "dp"), "seq"),
        P(),
    )
    return jax.shard_map(
        per_device,
        mesh=mesh,
        in_specs=placed,
        out_specs=(
            P(("parts", "dp"), "seq", None),
            P(("parts", "seq", "dp"), None),
            P("parts", ("seq", "dp")),
        ),
        check_vma=False,
    )
```

profile of v0, /device:TPU:0, one launch (start us, length us, event | category | flops | bytes accessed | tf_op | source)
XLA Modules:
  0.0 318.3 jit_solution(8727854632200333604)
XLA Ops:
  9.8 0.9 bitcast_convert_fusion
  13.3 2.1 rev.16
  16.8 22.4 %all_gather.17 = bf16[8,1,4]{2,1,0:T(2,128)(2,1)} all-gather(bf16[1,1,4]{2,1,0:T(2,128)(2,1)S(1)} %fusion.149), channel_id=1, replica_groups=mesh['parts'=2,'seq'=8,'dp'=2] {'seq'}, dimensions={0}, use_global_device_ids=true | all-gather | bytes 72 | tf_op jit(solution)/shard_map/all_gather | solution.py:32
  40.6 16.9 %all_gather.38 = bf16[8,1,4]{2,1,0:T(2,128)(2,1)} all-gather(bf16[1,1,4]{2,1,0:T(2,128)(2,1)S(1)} %get-tuple-element.309), channel_id=1, replica_groups=mesh['parts'=2,'seq'=8,'dp'=2] {'seq'}, dimensions={0}, use_global_device_ids=true | all-gather | bytes 72 | tf_op jit(solution)/shard_map/all_gather | solution.py:32
  57.8 1.4 convolution_convert_fusion.1
  59.2 1.3 fusion.61
  61.2 1.2 fusion.62
  62.4 2.0 fusion.27
  64.4 1.5 multiply_reduce_fusion
  68.4 2.7 fusion.41
  71.1 2.0 copy.106
  73.2 2.7 convolution_bitcast_fusion
  76.4 30.7 %all-gather = bf16[8,4,1,1536]{3,1,2,0:T(4,128)(2,1)S(1)} all-gather(bf16[1,4,1,1536]{3,1,2,0:T(4,128)(2,1)S(1)} %copy.42), channel_id=2, replica_groups=mesh['parts'=2,'seq'=8,'dp'=2] {'seq'}, dimensions={0}, use_global_device_ids=true | all-gather | bytes 110592 | tf_op jit(solution)/shard_map/all_gather | solution.py:32
  107.9 2.2 add_bitcast_fusion
  110.1 32.5 %all_gather.39 = bf16[8,1,4,1536]{3,2,1,0:T(4,128)(2,1)} all-gather(bf16[1,1,4,1536]{3,2,1,0:T(4,128)(2,1)S(1)} %fusion.128), channel_id=1, replica_groups=mesh['parts'=2,'seq'=8,'dp'=2] {'seq'}, dimensions={0}, use_global_device_ids=true | all-gather | bytes 110592 | tf_op jit(solution)/shard_map/all_gather | solution.py:32
  144.4 18.5 %while.35 = (s32[]{:T(128)}, f32[1,4]{1,0:T(1,128)S(1)}, f32[1,4,1536]{2,1,0:T(4,128)S(1)}, f32[1,4]{1,0:T(1,128)}, f32[1,4,1536]{2,1,0:T(4,128)S(1)}, /*index=5...) while((s32[]{:T(128)}, f32[1,4]{1,0:T(1,128)S(1)}, ...), condition=%wide.region_7.8_spmd, body=%wide.region_6.7_spmd.sunk | while | flops 36890 | bytes 123215 | solution.py:49
  145.8 1.2 fusion.179
  148.4 1.2 fusion.179
  151.1 1.2 fusion.179
  153.9 1.2 fusion.179
  156.5 1.2 fusion.179
  159.1 1.2 fusion.179
  161.7 1.2 fusion.179
  162.9 1.6 fusion.15
  165.3 1.0 fusion.129
  167.0 1.3 fusion.137
  168.3 1.1 fusion.17
  169.6 1.3 fusion.23
  170.9 3.9 %rev.15 = f32[1,128,768]{2,1,0:T(8,128)} reverse(f32[1,128,768]{2,1,0:T(8,128)} %fusion.23), dimensions={1} | reverse | bytes 786432 | tf_op jit(solution)/shard_map/rev | solution.py:284
  174.8 1.7 fusion.19
  177.8 1.0 fusion.28
  178.8 2.0 convolution_bitcast_fusion.1
  180.8 1.5 collective-permute-start.2
  183.3 1.0 copy.76
  184.3 1.2 fusion.63
  185.6 1.3 convolution_bitcast_fusion.2
  186.8 1.2 maximum_bitcast_fusion.1
  188.1 1.8 convolution_add_fusion.3
  189.8 2.5 fusion.48
  192.4 1.4 fusion.49
  193.9 1.6 fusion.30
  196.5 2.1 pad_maximum_fusion
  198.7 40.1 %reduce-scatter.7.cloned.1.call-done = f32[48,8]{1,0:T(8,128)} async-done(((f32[768,8]{1,0:T(8,128)}), f32[48,8]{1,0:T(8,128)}) %reduce-scatter.7.cloned.1.call-update) | async-done | bytes 1552
  241.0 1.1 fusion.60
  243.7 2.2 fusion.45
  245.9 1.9 fusion.47
  247.8 62.3 %reduce-scatter.5.cloned.1.call-done = f32[144,384]{1,0:T(8,128)} async-done(((f32[2304,384]{1,0:T(8,128)}), f32[144,384]{1,0:T(8,128)}) %reduce-scatter.5.cloned.1.call-update) | async-done | bytes 221200 | tf_op jit(solution)/shard_map/reduce_scatter | solution.py:341
  310.1 1.6 broadcast_multiply_fusion
  (210 shorter events, 32.7 us)
Async XLA Ops:
  7.2 2.3 copy-start.4
  7.2 3.5 %copy-start.55 = (f32[1,128]{1,0:T(1,128)S(1)}, f32[1,128]{1,0:T(1,128)}, u32[]{:S(2)}) copy-start(f32[1,128]{1,0:T(1,128)} %param.22) | copy-start | bytes 1540
  7.2 3.5 %copy-start.54 = (f32[4]{0:T(128)S(1)}, f32[4]{0:T(128)}, u32[]{:S(2)}) copy-start(f32[4]{0:T(128)} %param.21) | copy-start | bytes 52
  7.2 50.5 %all-gather.5.cloned.1.call-start = ((), (), s32[]{:S(2)}) async-start(), calls=%async_computation.2 | async-start | bytes 1769472 | tf_op jit(solution)/shard_map/all_gather | solution.py:212
  7.9 51.3 %all-gather.7.cloned.1.call-start = ((), (), s32[]{:S(2)}) async-start(), calls=%async_computation.3 | async-start | bytes 2654208 | tf_op jit(solution)/shard_map/all_gather | solution.py:213
  8.7 55.8 %all-gather.9.cloned.1.call-start = ((), (), s32[]{:S(2)}) async-start(), calls=%async_computation.4 | async-start | bytes 1769472 | tf_op jit(solution)/shard_map/all_gather | solution.py:214
  9.4 229.3 %reduce-scatter.7.cloned.1.call-start = ((), (), s32[]{:S(2)}) async-start(), calls=%async_computation.6 | async-start | bytes 417792
  9.5 6.7 %copy-start.56 = (s32[1,128]{1,0:T(1,128)S(1)}, s32[1,128]{1,0:T(1,128)}, u32[]{:S(2)}) copy-start(s32[1,128]{1,0:T(1,128)} %param.16) | copy-start | bytes 1540
  9.8 47.7 %copy-start.8 = (bf16[1,128,768]{2,1,0:T(8,128)(2,1)S(1)}, bf16[1,128,768]{2,1,0:T(8,128)(2,1)}, u32[]{:S(2)}) copy-start(bf16[1,128,768]{2,1,0:T(8,128)(2,1)} %param.14) | copy-start | bytes 589828
  9.8 47.7 %copy-start.38 = (f32[768]{0:T(1024)S(1)}, f32[768]{0:T(1024)}, u32[]{:S(2)}) copy-start(f32[768]{0:T(1024)} %param.17) | copy-start | bytes 9220
  11.4 47.7 %copy-start.27 = (f32[1,128,4]{2,1,0:T(8,128)}, f32[1,128,4]{2,1,0:T(8,128)S(1)}, u32[]{:S(2)}) copy-start(f32[1,128,4]{2,1,0:T(8,128)S(1)} %broadcast_subtract_fusion) | copy-start | bytes 6148
  16.2 44.3 %copy-start.46 = (f32[128]{0:T(128)}, f32[128]{0:T(128)S(1)}, u32[]{:S(2)}) copy-start(f32[128]{0:T(128)S(1)} %log-plus-one_bitcast_fusion) | copy-start | bytes 1540
  57.7 2.8 copy-start.52
  59.2 6.8 %copy-start.6 = (bf16[2,768,384]{1,2,0:T(8,128)(2,1)S(1)}, bf16[2,768,384]{1,2,0:T(8,128)(2,1)}, u32[]{:S(2)}) copy-start(bf16[2,768,384]{1,2,0:T(8,128)(2,1)} %all-gather.5.cloned.1.call-done) | copy-start | bytes 3538948
  59.2 1.3 collective-permute-start
  62.4 3.9 %copy-start.1 = (bf16[2,3,384,384]{2,3,1,0:T(8,128)(2,1)S(1)}, bf16[2,3,384,384]{2,3,1,0:T(8,128)(2,1)}, u32[]{:S(2)}) copy-start(bf16[2,3,384,384]{2,3,1,0:T(8,128)(2,1)} %all-gather.7.cloned.1.call-done) | copy-start | bytes 5308420
  65.9 2.2 copy-start.48
  66.3 0.3 collective-permute-start.1
  73.2 2.8 copy-start.45
  76.4 30.8 %copy-start = (f32[1,4,128,1536]{3,2,1,0:T(8,128)}, f32[1,4,128,1536]{3,2,1,0:T(8,128)S(1)}, u32[]{:S(2)}) copy-start(f32[1,4,128,1536]{3,2,1,0:T(8,128)S(1)} %add_bitcast_fusion.1) | copy-start | bytes 9437188
  107.9 2.2 copy-start.50
  162.9 3.4 %copy-start.36 = (f32[4,768]{1,0:T(4,128)S(1)}, f32[4,768]{1,0:T(4,128)}, u32[]{:S(2)}) copy-start(f32[4,768]{1,0:T(4,128)} %fusion.78) | copy-start | bytes 36868
  162.9 4.0 %copy-start.33 = (f32[2,4,768]{2,1,0:T(4,128)S(1)}, f32[2,4,768]{2,1,0:T(4,128)}, u32[]{:S(2)}) copy-start(f32[2,4,768]{2,1,0:T(4,128)} %param.23) | copy-start | bytes 73732
  162.9 6.5 %copy-start.17 = (f32[1,4,1536]{2,1,0:T(4,128)S(1)}, f32[1,4,1536]{2,1,0:T(4,128)}, u32[]{:S(2)}) copy-start(f32[1,4,1536]{2,1,0:T(4,128)} %copy-done.16) | copy-start | bytes 73732
  162.9 6.5 %copy-start.51 = (f32[4]{0:T(128)S(1)}, f32[4]{0:T(128)}, u32[]{:S(2)}) copy-start(f32[4]{0:T(128)} %get-tuple-element.308) | copy-start | bytes 52
  162.9 6.6 %copy-start.43 = (f32[4]{0:T(128)S(1)}, f32[4]{0:T(128)}, u32[]{:S(2)}) copy-start(f32[4]{0:T(128)} %negate_sqrt_fusion) | copy-start | bytes 52
  169.5 6.9 %copy-start.34 = (f32[2,4,768]{2,1,0:T(4,128)S(1)}, f32[2,4,768]{2,1,0:T(4,128)}, u32[]{:S(2)}) copy-start(f32[2,4,768]{2,1,0:T(4,128)} %param.23) | copy-start | bytes 73732
  169.6 6.9 %copy-start.35 = (f32[1,4,768]{2,0,1:T(1,128)S(1)}, f32[1,4,768]{2,0,1:T(1,128)}, u32[]{:S(2)}) copy-start(f32[1,4,768]{2,0,1:T(1,128)} %get-tuple-element.313) | copy-start | bytes 36868
  169.6 6.9 %copy-start.44 = (f32[4]{0:T(128)S(1)}, f32[4]{0:T(128)}, u32[]{:S(2)}) copy-start(f32[4]{0:T(128)} %negate_sqrt_fusion) | copy-start | bytes 52
  174.8 3.1 copy-start.26
  174.8 3.1 copy-start.32
  176.5 2.3 copy-start.24
  176.5 5.8 %copy-start.5 = (f32[1,128,768]{2,1,0:T(8,128)S(1)}, f32[1,128,768]{2,1,0:T(8,128)}, u32[]{:S(2)}) copy-start(f32[1,128,768]{2,1,0:T(8,128)} %rev.16) | copy-start | bytes 1179652
  178.8 4.4 %copy-start.37 = (f32[1,4,768]{2,1,0:T(4,128)S(1)}, f32[1,4,768]{2,1,0:T(4,128)}, u32[]{:S(2)}) copy-start(f32[1,4,768]{2,1,0:T(4,128)} %get-tuple-element.318) | copy-start | bytes 36868
  180.8 7.2 %collective-permute-start.2 = (bf16[1,128,384]{2,1,0:T(8,128)(2,1)}, bf16[1,128,384]{2,1,0:T(8,128)(2,1)}, u32[]{:S(2)}, u32[]{:S(2)}) collective-permute-start(bf16[1,128,384]{2,1,0:T(8,128)(2,1)} %bitcast.98), channel_id=1, source_target_pairs={{0,0},{2,2},{4,4},{6,6},{8,8},{10,10},{12,12},{14,14},{1,1},{3,3},... | collective-permute-start | bytes 294920 | tf_op jit(solution)/shard_map/ppermute | solution.py:24
  182.3 3.2 %copy-start.22 = (bf16[1,128,384]{2,1,0:T(8,128)(2,1)S(1)}, bf16[1,128,384]{2,1,0:T(8,128)(2,1)}, u32[]{:S(2)}) copy-start(bf16[1,128,384]{2,1,0:T(8,128)(2,1)} %copy-done.21) | copy-start | bytes 294916
  184.3 125.8 %reduce-scatter.5.cloned.1.call-start = ((), (), s32[]{:S(2)}) async-start(), calls=%async_computation.5 | async-start | bytes 3760128 | tf_op jit(solution)/shard_map/reduce_scatter | solution.py:341
  185.5 2.5 copy-start.2
  188.0 4.4 %copy-start.49 = (f32[128]{0:T(128)S(1)}, f32[128]{0:T(128)}, u32[]{:S(2)}) copy-start(f32[128]{0:T(128)} %copy-done.48) | copy-start | bytes 1540
  192.4 3.1 copy-start.29
  192.4 3.7 %copy-start.20 = (bf16[1,128,384]{2,1,0:T(8,128)(2,1)S(1)}, bf16[1,128,384]{2,1,0:T(8,128)(2,1)}, u32[]{:S(2)}) copy-start(bf16[1,128,384]{2,1,0:T(8,128)(2,1)} %copy-done.19) | copy-start | bytes 294916
  198.6 45.1 %copy-start.7 = (bf16[2,768,384]{1,2,0:T(8,128)(2,1)S(1)}, bf16[2,768,384]{1,2,0:T(8,128)(2,1)}, u32[]{:S(2)}) copy-start(bf16[2,768,384]{1,2,0:T(8,128)(2,1)} %all-gather.5.cloned.1.call-done) | copy-start | bytes 3538948
  198.6 45.1 %copy-start.9 = (bf16[1,128,768]{2,1,0:T(8,128)(2,1)S(1)}, bf16[1,128,768]{2,1,0:T(8,128)(2,1)}, u32[]{:S(2)}) copy-start(bf16[1,128,768]{2,1,0:T(8,128)(2,1)} %param.14) | copy-start | bytes 589828
  198.6 45.1 %copy-start.39 = (f32[768]{0:T(1024)S(1)}, f32[768]{0:T(1024)}, u32[]{:S(2)}) copy-start(f32[768]{0:T(1024)} %param.17) | copy-start | bytes 9220
  198.6 45.1 %copy-start.47 = (f32[128]{0:T(128)S(1)}, f32[128]{0:T(128)}, u32[]{:S(2)}) copy-start(f32[128]{0:T(128)} %copy-done.46) | copy-start | bytes 1540
  198.6 47.3 %copy-start.15 = (f32[1,128,768]{2,1,0:T(8,128)S(1)}, f32[1,128,768]{2,1,0:T(8,128)}, u32[]{:S(2)}) copy-start(f32[1,128,768]{2,1,0:T(8,128)} %copy-done.14) | copy-start | bytes 1179652
  198.7 47.3 %copy-start.53 = (f32[128]{0:T(128)S(1)}, f32[128]{0:T(128)}, u32[]{:S(2)}) copy-start(f32[128]{0:T(128)} %copy-done.52) | copy-start | bytes 1540
  240.2 2.0 collective-permute-start.3
  (18 other events, 23.5 us)
Sparse Core Ops, SparseCore 0:
  9.6 11.9 all-gather.4
  23.1 11.2 all-gather.6
  35.9 10.3 all-gather.8
  184.4 54.3 reduce-scatter.6
  243.0 67.0 reduce-scatter.4
where the time goes:
time: 320 us; the launch traced here: 318 us
  waiting for transfers between devices  104 us (32%)
  blocking collectives  103 us (32%)
  other arithmetic  42.5 us (13%)
  matrix products  33.2 us (10%)
  local copies, waits for them, and re-layouts  18.1 us (6%)
  between operations  14.8 us (5%)
    all_gather x4, blocking collectives, entering_2(): lax.all_gather(a.astype(kind), axis)  103 us
    reduce_scatter x1, waiting for transfers between devices, per_device(): lax.psum_scatter(tap_flat, ('seq', 'dp'), scatter_dimension=0, tiled=True)  62.3 us
    unnamed x6, waiting for transfers between devices  42.2 us
    mul x7, other arithmetic, apply_late_first(): early_pass * late_pass  8.43 us
    dot_general x8, matrix products, project(): jnp.einsum('qra,au->qru', left_shifted, right_shifted, preferred_element_...  6.9 us
  transfers between devices with their start and end apart: 9, of which 2 were waited for; matrix products, arithmetic and copies ran while one was open for 12% of the time, Pallas kernels for 0%

commit v1 on v0

--- a/solution.py
+++ b/solution.py
@@ -1,8 +1,11 @@
+import functools
 import math
 
 import jax
 import jax.numpy as jnp
 from jax import lax
+from jax.experimental import pallas as pl
+from jax.experimental.pallas import tpu as pltpu
 from jax.sharding import PartitionSpec as P
 
 B = 384
@@ -194,7 +197,7 @@
     return numerator / (1.0 - beside_all * own_pass)[..., None]
 
 
-def per_device(
+def general_device(
     features,
     cotangent,
     counts,
@@ -344,6 +347,354 @@
     return (gradient.astype(jnp.bfloat16), tap_sum * report_scale, mode_sum * report_scale)
 
 
+VMEM = pltpu.MemorySpace.VMEM
+SMEM = pltpu.MemorySpace.SMEM
+F32 = jnp.float32
+BF16 = jnp.bfloat16
+RING = 8
+HOPS = (4, 2, 1)
+BLOCK = 48
+
+
+def call(body, operands, spaces, outs, scratch=(), flops=0):
+    return pl.pallas_call(
+        body,
+        out_shape=[jax.ShapeDtypeStruct(shape, dtype) for shape, dtype in outs],
+        in_specs=[pl.BlockSpec(memory_space=space) for space in spaces],
+        out_specs=[pl.BlockSpec(memory_space=VMEM) for _ in outs],
+        scratch_shapes=list(scratch),
+        compiler_params=pltpu.CompilerParams(vmem_limit_bytes=40 * 1024 * 1024),
+    )(*operands)
+
+
+def dot(left, right):
+    return lax.dot_general(left, right, (((1,), (0,)), ((), ())), preferred_element_type=F32)
+
+
+def dot_nt(left, right):
+    return lax.dot_general(left, right, (((1,), (1,)), ((), ())), preferred_element_type=F32)
+
+
+def dot_tn(left, right):
+    return lax.dot_general(left, right, (((0,), (0,)), ((), ())), preferred_element_type=F32)
+
+
+def iota2(shape, axis):
+    return lax.broadcasted_iota(jnp.int32, shape, axis)
+
+
+def split_pair(value):
+    high = value.astype(BF16)
+    return high, (value - high.astype(F32)).astype(BF16)
+
+
+def log_sums(keep_row):
+    rows = keep_row.shape[-1]
+    below, beside = iota2((rows, rows), 0), iota2((rows, rows), 1)
+    logs = jnp.broadcast_to(jnp.log(keep_row), (rows, rows))
+    column = jnp.sum(jnp.where(beside <= below, logs, 0.0), axis=1, keepdims=True)
+    spread = jnp.broadcast_to(column, (rows, rows))
+    row = jnp.sum(jnp.where(beside == below, spread, 0.0), axis=0, keepdims=True)
+    return column, row, column[rows - 1 :, :]
+
+
+def prepare_body(cot_ref, keep_ref, decay_ref, tap_ref, pay_ref, tap_sum_ref):
+    rows = keep_ref.shape[-1]
+    _, sums, total = log_sums(keep_ref[...])
+    place = iota2((1, rows), 1).astype(F32)
+    exits = []
+    for mode in range(M):
+        exits.append(jnp.exp((total - sums) - (rows - 1.0 - place) * decay_ref[mode]))
+    for mode in range(M):
+        exits.append(jnp.exp(sums - (place + 1.0) * decay_ref[mode]))
+    weights = jnp.concatenate(exits, axis=0)
+    high, low = split_pair(weights)
+    cot = cot_ref[0]
+    states = dot(high, cot) + dot(low, cot)
+    width = cot.shape[-1]
+    first = jnp.broadcast_to(total, (8, width))
+    one = first.astype(BF16).astype(F32)
+    two = (first - one).astype(BF16).astype(F32)
+    three = first - one - two
+    row = iota2((8, width), 0)
+    extra = jnp.where(row == 0, one, jnp.where(row == 1, two, jnp.where(row == 2, three, 0.0)))
+    pay_ref[...] = jnp.concatenate([states, extra], axis=0).astype(BF16)
+    for layer in range(LAYERS):
+        taps = tap_ref[layer, 0].astype(F32) + tap_ref[layer, 1].astype(F32)
+        tap_sum_ref[layer] = (taps + tap_ref[layer, 2].astype(F32)).astype(BF16)
+
+
+def forward_body(
+    feature_ref, count_ref, weight_ref, down_ref, down_far_ref, tap_ref, tap_far_ref,
+    up_ref, up_far_ref, stream_ref, inverse_ref, reduced_ref, mixture_ref,
+):
+    core = lax.axis_index("dp")
+    rows, width = feature_ref.shape[1:]
+    half = down_ref.shape[-1]
+    wide = up_ref.shape[-1]
+    own = pl.ds(pl.multiple_of(core * half, half), half)
+    far = pl.ds(pl.multiple_of((1 - core) * half, half), half)
+    logs = jnp.broadcast_to(jnp.log1p(count_ref[...].astype(F32)), (rows, rows))
+    diagonal = iota2((rows, rows), 0) == iota2((rows, rows), 1)
+    level = jnp.sum(jnp.where(diagonal, logs, 0.0), axis=1, keepdims=True)
+    stream = feature_ref[0].astype(F32) + level * weight_ref[...]
+    for layer in range(LAYERS):
+        stream_ref[layer] = stream
+        mean = jnp.sum(stream * stream, axis=-1, keepdims=True) * (1.0 / width)
+        inverse = lax.rsqrt(mean + EPSILON)
+        inverse_ref[layer] = inverse
+        normed = (stream * inverse).astype(BF16)
+        near = dot(normed, down_ref[layer]).astype(BF16)
+        away = dot(normed, down_far_ref[layer]).astype(BF16)
+        reduced_ref[layer, 0] = near
+        reduced_ref[layer, 1] = away
+        mix_near = dot(near, tap_ref[layer, own, :]) + dot(away, tap_ref[layer, far, :])
+        mix_away = dot(near, tap_far_ref[layer, own, :]) + dot(away, tap_far_ref[layer, far, :])
+        mixture_ref[layer, 0] = mix_near
+        mixture_ref[layer, 1] = mix_away
+        act_near = gelu_exact(mix_near).astype(BF16)
+        act_away = gelu_exact(mix_away).astype(BF16)
+        out_near = dot(act_near, up_ref[layer, own, :]) + dot(act_away, up_ref[layer, far, :])
+        out_away = dot(act_near, up_far_ref[layer, own, :]) + dot(act_away, up_far_ref[layer, far, :])
+        low = jnp.where(core == 0, out_near, out_away)
+        high = jnp.where(core == 0, out_away, out_near)
+        stream = stream + jnp.concatenate([low, high], axis=-1)
+    stream_ref[LAYERS] = stream
+
+
+def backward_body(
+    decay_ref, scale_ref, near_ref, away_ref, cot_ref, keep_ref, mode_ref, stream_ref,
+    inverse_ref, reduced_ref, mixture_ref, down_ref, down_far_ref, tap_ref, tap_far_ref,
+    up_ref, up_far_ref, grad_ref, kept_ref, send_ref, partial_ref, edge_ref, grads_ref,
+    block_ref,
+):
+    core = lax.axis_index("dp")
+    place = lax.axis_index("seq")
+    rows, width = cot_ref.shape[1:]
+    half = down_ref.shape[-1]
+    wide = up_ref.shape[-1]
+    own = pl.ds(pl.multiple_of(core * half, half), half)
+    far = pl.ds(pl.multiple_of((1 - core) * half, half), half)
+
+    masks = [0]
+    for hop in HOPS:
+        masks = masks + [mask ^ hop for mask in masks]
+    pieces = [near_ref[index].astype(F32) for index in range(RING // 2)]
+    pieces = pieces + [away_ref[index].astype(F32) for index in range(RING // 2)]
+    totals = [jnp.sum(piece[8:16, 0:128], axis=0, keepdims=True) for piece in pieces]
+    row8 = iota2((8, 128), 0)
+    decay8 = jnp.zeros((8, 128), F32)
+    for index in range(2 * M):
+        decay8 = jnp.where(row8 == index, decay_ref[index % M], decay8)
+    everything = totals[0]
+    for value in totals[1:]:
+        everything = everything + value
+    loop = 1.0 - jnp.exp(jnp.broadcast_to(everything, (8, 128)) - (RING * rows) * decay8)
+    others = [lax.bitwise_xor(place, mask) for mask in masks]
+    ahead = [lax.rem(place - other + (RING - 1), RING) for other in others]
+    after = [lax.rem(other - place + (RING - 1), RING) for other in others]
+    entering = jnp.zeros((8, width), F32)
+    for index in range(RING):
+        fore = jnp.zeros((1, 128), F32)
+        back = jnp.zeros((1, 128), F32)
+        for other in range(RING):
+            fore = fore + jnp.where(ahead[other] < ahead[index], totals[other], 0.0)
+            back = back + jnp.where(after[other] < after[index], totals[other], 0.0)
+        fore = jnp.broadcast_to(fore, (8, 128)) - (ahead[index] * rows).astype(F32) * decay8
+        back = jnp.broadcast_to(back, (8, 128)) - (after[index] * rows).astype(F32) * decay8
+        share = jnp.exp(jnp.where(row8 < M, fore, back)) / loop
+        entering = entering + share[:, 0:1] * pieces[index][0:8, :]
+    edge_ref[...] = entering
+
+    column, row, total = log_sums(keep_ref[...])
+    down_rows = iota2((rows, rows), 0)
+    across = iota2((rows, rows), 1)
+    gap = column - row
+    steps = (down_rows - across).astype(F32)
+    spot = iota2((rows, 1), 0).astype(F32)
+    kernels = []
+    edges = []
+    for mode in range(M):
+        rate = decay_ref[mode]
+        value = jnp.exp(jnp.minimum(gap - steps * rate, 0.0))
+        kernels.append(jnp.where(down_rows >= across, value, 0.0))
+        edges.append(jnp.exp(column - (spot + 1.0) * rate))
+    for mode in range(M):
+        rate = decay_ref[mode]
+        value = jnp.exp(jnp.minimum(steps * rate - gap, 0.0))
+        kernels.append(jnp.where(across >= down_rows, value, 0.0))
+        edges.append(jnp.exp((total - column) - (rows - 1.0 - spot) * rate))
+    pairs = [jnp.concatenate(split_pair(kernel), axis=1) for kernel in kernels]
+    span = 128
+    for start in range(0, width, span):
+        part = slice(start, start + span)
+        cot = cot_ref[0, :, part]
+        doubled = jnp.concatenate([cot, cot], axis=0)
+        stream = stream_ref[LAYERS, :, part]
+        grad = cot.astype(F32)
+        marks = [None] * (2 * M)
+        for index in range(2 * M):
+            mode = index % M
+            field = dot(pairs[index], doubled) + edges[index] * edge_ref[index : index + 1, part]
+            gain = scale_ref[mode]
+            side = 1 - index // M
+            grad = grad + (gain * mode_ref[side, mode : mode + 1, part]) * field
+            marks[side * M + mode] = gain * jnp.sum(stream * field, axis=0, keepdims=True)
+        grads_ref[:, part] = grad
+        top = 8 * (start // wide)
+        partial_ref[top : top + 8, start % wide : start % wide + span] = jnp.concatenate(marks, axis=0)
+
+    high, low = split_pair(partial_ref[...])
+    tap_rows = RING * BLOCK
+    send_ref[tap_rows : tap_rows + 16, :] = high
+    send_ref[tap_rows + 16 : tap_rows + 32, :] = low
+
+    for layer in reversed(range(LAYERS)):
+        gradient = grads_ref[...]
+        narrow = gradient.astype(BF16)
+        first, second = narrow[:, :wide], narrow[:, wide:]
+        mine = jnp.where(core == 0, first, second)
+        theirs = jnp.where(core == 0, second, first)
+        mixed = []
+        for index, part in enumerate((own, far)):
+            back = dot_nt(mine, up_ref[layer, part, :]) + dot_nt(theirs, up_far_ref[layer, part, :])
+            mixed.append((back * gelu_slope(mixture_ref[layer, index])).astype(BF16))
+        whole = []
+        for near, away in (mixed, (reduced_ref[layer, 0], reduced_ref[layer, 1])):
+            straight = jnp.concatenate([near, away], axis=1)
+            crossed = jnp.concatenate([away, near], axis=1)
+            whole.append(jnp.where(core == 0, straight, crossed))
+        block_ref[...] = dot_tn(whole[1], whole[0])
+        for turn in range(4):
+            to = 2 * turn + layer
+            kept = lax.rem(3 * core + 6 * (turn // 2) + 4 * (turn % 2), RING)
+            sent = lax.rem(3 * (1 - core) + 6 * (turn // 2) + 4 * (turn % 2), RING)
+            kept_ref[to * BLOCK : (to + 1) * BLOCK, :] = block_ref[pl.ds(pl.multiple_of(kept * BLOCK, BLOCK), BLOCK), :]
+            send_ref[to * BLOCK : (to + 1) * BLOCK, :] = block_ref[
+                pl.ds(pl.multiple_of(sent * BLOCK, BLOCK), BLOCK), :
+            ].astype(BF16)
+        normed = None
+        for part, source in ((own, down_ref), (far, down_far_ref)):
+            passed = dot_nt(mixed[0], tap_ref[layer, part, :]) + dot_nt(mixed[1], tap_far_ref[layer, part, :])
+            term = dot_nt(passed.astype(BF16), source[layer])
+            normed = term if normed is None else normed + term
+        before = stream_ref[layer]
+        inverse = inverse_ref[layer]
+        shared = jnp.sum(normed * before, axis=-1, keepdims=True) * (1.0 / width)
+        grads_ref[...] = gradient + inverse * normed - before * (inverse * inverse * inverse * shared)
+    grad_ref[0] = grads_ref[...].astype(BF16)
+
+
+def position_bit(stage):
+    place = lax.axis_index("seq")
+    return lax.rem(place // (1, 2, 4)[stage], 2)
+
+
+def join_body(stage, kept_ref, got_ref, partial_ref, kept_out, send_out, partial_out):
+    rows = kept_out.shape[0]
+    bit = position_bit(stage)
+    keep = pl.ds(pl.multiple_of(bit * rows, rows), rows)
+    send = pl.ds(pl.multiple_of((1 - bit) * rows, rows), rows)
+    kept_out[...] = kept_ref[keep, :] + got_ref[keep, :].astype(F32)
+    send_out[0:rows, :] = (kept_ref[send, :] + got_ref[send, :].astype(F32)).astype(BF16)
+    high = got_ref[2 * rows : 2 * rows + 16, :].astype(F32)
+    low = got_ref[2 * rows + 16 : 2 * rows + 32, :].astype(F32)
+    partial = partial_ref[...] + (high + low)
+    partial_out[...] = partial
+    high, low = split_pair(partial)
+    send_out[rows : rows + 16, :] = high
+    send_out[rows + 16 : rows + 32, :] = low
+
+
+def finish_body(scale, kept_ref, got_ref, partial_ref, block_out, mode_out, full_ref):
+    rows = kept_ref.shape[0]
+    block_out[...] = (kept_ref[...] + got_ref[0:rows, :].astype(F32)) * scale
+    high = got_ref[rows : rows + 16, :].astype(F32)
+    low = got_ref[rows + 16 : rows + 32, :].astype(F32)
+    full_ref[...] = (partial_ref[...] + (high + low)) * scale
+    number = 2 * lax.axis_index("seq") + lax.axis_index("dp")
+    span = full_ref.shape[1]
+    top = pl.multiple_of(8 * (number // 8), 8)
+    shift = lax.rem(span - BLOCK * lax.rem(number, 8), span)
+    mode_out[...] = pltpu.roll(full_ref[pl.ds(top, 8), :], shift, 1)[:, 0:BLOCK]
+
+
+def swap(value, axis, mask):
+    count = lax.axis_size(axis)
+    return lax.ppermute(value, axis, [(source, source ^ mask) for source in range(count)])
+
+
+def wrapped_device(
+    features, cotangent, counts, count_weight, down_weight, tap_weight, up_weight,
+    decay_rate, keep_share, mode_weight,
+):
+    rows, width = features.shape[1:]
+    half, wide = down_weight.shape[-1], up_weight.shape[-1]
+    down_far = swap(down_weight, "dp", 1)
+    pay, tap_sum = call(
+        prepare_body,
+        (cotangent, keep_share, decay_rate, tap_weight),
+        (VMEM, VMEM, SMEM, VMEM),
+        (((16, width), BF16), ((LAYERS, B, half), BF16)),
+    )
+    tap_far = swap(tap_sum, "dp", 1)
+    up_far = swap(up_weight, "dp", 1)
+    group = pay[None]
+    for hop in HOPS[:-1]:
+        group = jnp.concatenate([group, swap(group, "seq", hop)], axis=0)
+    away = swap(group, "seq", HOPS[-1])
+    scale = jnp.sqrt(-jnp.expm1(-2.0 * decay_rate))
+    stream, inverse, reduced, mixture = call(
+        forward_body,
+        (features, counts, count_weight[None], down_weight, down_far, tap_sum, tap_far, up_weight, up_far),
+        (VMEM,) * 9,
+        (
+            ((LAYERS + 1, rows, width), F32),
+            ((LAYERS, rows, 1), F32),
+            ((LAYERS, 2, rows, half), BF16),
+            ((LAYERS, 2, rows, half), F32),
+        ),
+    )
+    grad, kept, send, partial = call(
+        backward_body,
+        (
+            decay_rate, scale, group, away, cotangent, keep_share, mode_weight, stream, inverse, reduced,
+            mixture, down_weight, down_far, tap_sum, tap_far, up_weight, up_far,
+        ),
+        (SMEM, SMEM) + (VMEM,) * 15,
+        (
+            ((1, rows, width), BF16),
+            ((RING * BLOCK, B), F32),
+            ((RING * BLOCK + 32, B), BF16),
+            ((16, B), F32),
+        ),
+        (pltpu.VMEM((8, width), F32), pltpu.VMEM((rows, width), F32), pltpu.VMEM((B, B), F32)),
+    )
+    got = swap(send, "dp", 1)
+    for stage in range(3):
+        kept_rows = kept.shape[0] // 2
+        kept, send, partial = call(
+            functools.partial(join_body, stage),
+            (kept, got, partial),
+            (VMEM,) * 3,
+            (((kept_rows, B), F32), ((kept_rows + 32, B), BF16), ((16, B), F32)),
+        )
+        got = swap(send, "seq", (1, 2, 4)[stage])
+    total = features.shape[0] * lax.axis_size("dp") * rows * lax.axis_size("seq")
+    block, mode_sum = call(
+        functools.partial(finish_body, 1.0 / math.sqrt(total)),
+        (kept, got, partial),
+        (VMEM,) * 3,
+        (((BLOCK, B), F32), ((8, BLOCK), F32)),
+        (pltpu.VMEM((16, B), F32),),
+    )
+    parts = [block]
+    for step in (3, 6):
+        pairs = [(8 * layer + (j + step) % 8, 8 * layer + j) for layer in range(LAYERS) for j in range(8)]
+        parts.append(lax.ppermute(block, ("seq", "dp"), pairs))
+    return grad, jnp.concatenate(parts, axis=0), mode_sum
+
+
 def solution(mesh):
     placed = (
         P(("parts", "dp"), "seq", None),
@@ -357,6 +708,15 @@
         P(("parts", "dp"), "seq"),
         P(),
     )
+
+    def per_device(*operands):
+        rows = operands[0].shape[1]
+        ring = lax.axis_size("seq")
+        loop = ring * rows
+        wraps = all(dilation % loop == 0 for dilation in (DILATION_FIRST1, DILATION_SECOND2))
+        fits = ring == RING and lax.axis_size("dp") == 2 and operands[0].shape[0] == 1
+        return (wrapped_device if wraps and fits else general_device)(*operands)
+
     return jax.shard_map(
         per_device,
         mesh=mesh,

time: 320 us -> 51.8 us (0.16)
  blocking collectives: 103 us -> 0 us
  waiting for transfers between devices: 104 us -> 23.1 us
  other arithmetic: 42.5 us -> 1.89 us
  matrix products: 33.2 us -> 0 us
  local copies, waits for them, and re-layouts: 18.1 us -> 4.13 us
  between operations: 14.8 us -> 0.85 us
  starting transfers between devices: 2.6 us -> 12.8 us
  Pallas kernels: 0 us -> 8.86 us
    all_gather x4 -> x0, blocking collectives: 103 us -> none  [entering_2(): lax.all_gather(a.astype(kind), axis)]
    reduce_scatter x1 -> x0, waiting for transfers between devices: 62.3 us -> none  [per_device(): lax.psum_scatter(tap_flat, ('seq', 'dp'), scatter_dimension=0, tiled=True)]
    unnamed x6 -> x0, waiting for transfers between devices: 42.2 us -> none
    dot_general x28 -> x0, matrix products: 33.2 us -> none  [the longest x8 6.9 us: project(): jnp.einsum('qra,au->qru', left_shifted, right_shifted, preferred_element_...]
    ppermute x4 -> x12, waiting for transfers between devices: 0.01 us -> 23.1 us  [the longest x10 18.1 us: swap(): lax.ppermute(value, axis, [(source, source ^ mask) for source in range(co...]
    mul x11 -> x0, other arithmetic: 12 us -> none  [the longest x7 8.43 us: apply_late_first(): early_pass * late_pass]
    ppermute x4 -> x12, starting transfers between devices: 2.4 us -> 12.8 us  [the longest x10 12.5 us: swap(): lax.ppermute(value, axis, [(source, source ^ mask) for source in range(co...]
    pallas_call x0 -> x7, Pallas kernels: none -> 8.86 us  [call(): pl.pallas_call(body, out_shape=[jax.ShapeDtypeStruct(shape, dtype) for sh...]
  transfers between devices with their start and end apart: 9 -> 12, of which waited for: 2 -> 7; matrix products, arithmetic and copies ran while one was open for 12% -> 8% of each run, Pallas kernels for 0% -> 5%
where the time goes in v1:
time: 51.8 us; the launch traced here: 51.6 us
  waiting for transfers between devices  23.1 us (45%)
  starting transfers between devices  12.8 us (25%)
  Pallas kernels  8.86 us (17%)
  local copies, waits for them, and re-layouts  4.13 us (8%)
  other arithmetic  1.89 us (4%)
  between operations  0.85 us (2%)
    ppermute x10, waiting for transfers between devices, swap(): lax.ppermute(value, axis, [(source, source ^ mask) for source in range(co...  18.1 us
    ppermute x10, starting transfers between devices, swap(): lax.ppermute(value, axis, [(source, source ^ mask) for source in range(co...  12.5 us
    pallas_call x7, Pallas kernels, call(): pl.pallas_call(body, out_shape=[jax.ShapeDtypeStruct(shape, dtype) for sh...  8.86 us
    ppermute x2, waiting for transfers between devices, wrapped_device(): parts.append(lax.ppermute(block, ('seq', 'dp'), pairs))  4.97 us
    unnamed x24, local copies, waits for them, and re-layouts  2.79 us
    ppermute x1, local copies, waits for them, and re-layouts, swap(): lax.ppermute(value, axis, [(source, source ^ mask) for source in range(co...  1.33 us
  transfers between devices with their start and end apart: 12, of which 7 were waited for; matrix products, arithmetic and copies ran while one was open for 8% of the time, Pallas kernels for 5%

profile of v1, /device:TPU:0, one launch (start us, length us, event | category | flops | bytes accessed | tf_op | source)
XLA Modules:
  0.0 51.6 jit_solution(3934114059275236275)
XLA Ops:
  0.6 0.0 copy-start.5
  0.6 0.0 copy-start.6
  0.7 0.0 copy-start.1
  0.7 0.5 %collective-permute-start.3 = (bf16[2,768,192]{1,2,0:T(8,128)(2,1)}, bf16[2,768,192]{1,2,0:T(8,128)(2,1)}, u32[]{:S(2)}, u32[]{:S(2)}) collective-permute-start(bf16[2,768,192]{1,2,0:T(8,128)(2,1)} %param.14), channel_id=1, source_target_pairs={{0,1},{1,0},{2,3},{3,2},{4,5},{5,4},{6,7},{7,6},{8,9},{9,8},{10,11... | collective-permute-start | bytes 1769480 | tf_op jit(solution)/shard_map/ppermute | solution.py:624
  1.2 0.1 collective-permute-start.5
  1.3 1.5 %copy.17.tap_ref = bf16[2,3,384,192]{3,2,1,0:T(8,128)(2,1)S(1)} copy(bf16[2,3,384,192]{2,3,1,0:T(8,128)(2,1)} %param.15) | data formatting | bytes 1769472 | tf_op args[5]
  2.8 0.0 copy-done.5
  2.8 0.0 copy-done.6
  2.8 0.0 copy-done.1
  2.8 0.0 copy-start.9
  2.8 0.9 %shard_map.121 = (bf16[16,768]{1,0:T(8,128)(2,1)S(1)}, bf16[2,384,192]{2,1,0:T(8,128)(2,1)S(1)}) custom-call(bf16[1,128,768]{2,1,0:T(8,128)(2,1)S(1)} %copy-done.1, f32[1,128]{1,0:T(1,128)S(1)} %copy-done.6, f32[4]{0:T(128)S(1)} %copy-done.5, bf16[2,3,384,192]{3,2,1,0:T(8,128)(2,1)S(1)} %copy.17.tap_ref), custom_call_target="tpu_custom_call" | custom-call | tf_op jit(solution)/shard_map/pallas_call | solution.py:360
  3.7 4.1 %collective-permute-start = (bf16[1,16,768]{2,1,0:T(8,128)(2,1)S(1)}, bf16[1,16,768]{2,1,0:T(8,128)(2,1)S(1)}, u32[]{:S(2)}, u32[]{:S(2)}) collective-permute-start(bf16[1,16,768]{2,1,0:T(8,128)(2,1)S(1)} %bitcast.1), channel_id=1, source_target_pairs={{0,8},{2,10},{4,12},{6,14},{8,0},{10,2},{12,4},{14,6},{1,9},{3,11}... | collective-permute-start | bytes 73736 | tf_op jit(solution)/shard_map/ppermute | solution.py:624
  7.8 1.8 %collective-permute-done = bf16[1,16,768]{2,1,0:T(8,128)(2,1)S(1)} collective-permute-done((bf16[1,16,768]{2,1,0:T(8,128)(2,1)S(1)}, bf16[1,16,768]{2,1,0:T(8,128)(2,1)S(1)}, u32[]{:S(2)}, u32[]{:S(2)}) %collective-permute-start) | collective-permute-done | bytes 24608 | tf_op jit(solution)/shard_map/ppermute | solution.py:624
  9.6 1.9 %collective-permute-start.1 = (bf16[2,16,768]{2,1,0:T(8,128)(2,1)S(1)}, bf16[2,16,768]{2,1,0:T(8,128)(2,1)S(1)}, u32[]{:S(2)}, u32[]{:S(2)}) collective-permute-start(bf16[2,16,768]{2,1,0:T(8,128)(2,1)S(1)} %pad_maximum_fusion.2), channel_id=1, source_target_pairs={{0,4},{2,6},{4,0},{6,2},{8,12},{10,14},{12,8},{14,10},{1,5},{3,7},... | collective-permute-start | bytes 147464 | tf_op jit(solution)/shard_map/ppermute | solution.py:624
  11.5 0.0 collective-permute-start.4
  11.5 2.2 %collective-permute-done.1 = bf16[2,16,768]{2,1,0:T(8,128)(2,1)S(1)} collective-permute-done((bf16[2,16,768]{2,1,0:T(8,128)(2,1)S(1)}, bf16[2,16,768]{2,1,0:T(8,128)(2,1)S(1)}, u32[]{:S(2)}, u32[]{:S(2)}) %collective-permute-start.1) | collective-permute-done | bytes 49184 | tf_op jit(solution)/shard_map/ppermute | solution.py:624
  13.7 0.7 %pad_maximum_fusion.1.near_ref = bf16[4,16,768]{2,1,0:T(8,128)(2,1)} fusion(bf16[2,16,768]{2,1,0:T(8,128)(2,1)S(1)} %collective-permute-done.1, bf16[1,16,768]{2,1,0:T(8,128)(2,1)S(1)} %collective-permute-done, bf16[1,16,768]{2,1,0:T(8,128)(2,1)S(1)} %bitcast.3), kind=kLoop, calls=%fused_computation.1 | loop fusion | flops 98304 | bytes 196608 | tf_op jit(solution)/shard_map/concatenate | solution.py:644
  14.4 2.1 %collective-permute-start.2 = (bf16[4,16,768]{2,1,0:T(8,128)(2,1)}, bf16[4,16,768]{2,1,0:T(8,128)(2,1)}, u32[]{:S(2)}, u32[]{:S(2)}) collective-permute-start(bf16[4,16,768]{2,1,0:T(8,128)(2,1)} %pad_maximum_fusion.1.near_ref), channel_id=1, source_target_pairs={{0,2},{2,0},{4,6},{6,4},{8,10},{10,8},{12,14},{14,12},{1,3},{3,1},... | collective-permute-start | bytes 294920 | tf_op jit(solution)/shard_map/ppermute | solution.py:624
  16.5 0.5 %negate_sqrt_fusion.scale_ref = f32[4]{0:T(128)} fusion(f32[4]{0:T(128)S(1)} %copy-done.5), kind=kLoop, calls=%fused_computation.3 | loop fusion | flops 8 | bytes 32 | tf_op jit(solution)/shard_map/sqrt | solution.py:646
  17.0 0.0 copy-done.9
  17.0 0.3 copy.18.down_ref
  17.3 0.0 copy-done.10
  17.3 0.0 collective-permute-done.3
  17.3 1.3 %copy.19.down_far_ref = bf16[2,768,192]{2,1,0:T(8,128)(2,1)S(1)} copy(bf16[2,768,192]{1,2,0:T(8,128)(2,1)} %collective-permute-done.3) | data formatting | bytes 1179648 | tf_op jit(solution)/shard_map/ppermute | solution.py:624
  18.6 0.0 copy-start.2
  18.6 0.0 collective-permute-done.4.tap_far_ref
  18.7 0.0 collective-permute-done.5.up_far_ref
  18.7 0.0 copy-start.3
  18.7 1.0 %copy-done.3 = bf16[1,128,768]{2,1,0:T(8,128)(2,1)S(1)} copy-done((bf16[1,128,768]{2,1,0:T(8,128)(2,1)S(1)}, bf16[1,128,768]{2,1,0:T(8,128)(2,1)}, u32[]{:S(2)}) %copy-start.3) | copy-done | bytes 196632
  19.7 1.7 %shard_map.122 = (f32[3,128,768]{2,1,0:T(8,128)S(1)}, f32[2,128,1]{2,1,0:T(8,128)S(1)}, bf16[2,2,128,192]{3,2,1,0:T(8,128)(2,1)S(1)}, f32[2,2,128,192]{3,2,1,0:T(8,128)S(1)}) custom-call(bf16[1,128,768]{2,1,0:T(8,128)(2,1)S(1)} %copy-done.3, s32[1,128]{1,0:T(1,128)S(1)} %copy-done.7, f32[1,768]{1,0:T(1,128)S(1)} %broadcast_in_dim.7.weight_ref, ...), custom_call_target="tpu_custom_call" | custom-call | tf_op jit(solution)/shard_map/pallas_call | solution.py:360
  21.3 0.0 collective-permute-done.2.away_ref
  21.4 5.4 %shard_map.123 = (bf16[1,128,768]{2,1,0:T(8,128)(2,1)}, f32[384,384]{1,0:T(8,128)S(1)}, bf16[416,384]{1,0:T(8,128)(2,1)S(1)}, f32[16,384]{1,0:T(8,128)S(1)}) custom-call(f32[4]{0:T(128)S(1)} %copy-done.5, f32[4]{0:T(128)S(1)} %copy-done.8, bf16[4,16,768]{2,1,0:T(8,128)(2,1)} %pad_maximum_fusion.1.near_ref, ...), custom_call_target="tpu_custom_call" | custom-call | tf_op jit(solution)/shard_map/pallas_call | solution.py:360
  26.8 0.0 collective-permute-start.6
  26.8 1.6 %collective-permute-done.6.got_ref = bf16[416,384]{1,0:T(8,128)(2,1)S(1)} collective-permute-done((bf16[416,384]{1,0:T(8,128)(2,1)S(1)}, bf16[416,384]{1,0:T(8,128)(2,1)S(1)}, u32[]{:S(2)}, u32[]{:S(2)}) %collective-permute-start.6) | collective-permute-done | bytes 319520 | tf_op jit(solution)/shard_map/ppermute | solution.py:624
  28.4 0.1 shard_map.124
  28.5 0.1 collective-permute-start.7
  28.6 6.4 %collective-permute-done.7.got_ref = bf16[224,384]{1,0:T(8,128)(2,1)S(1)} collective-permute-done((bf16[224,384]{1,0:T(8,128)(2,1)S(1)}, bf16[224,384]{1,0:T(8,128)(2,1)S(1)}, u32[]{:S(2)}, u32[]{:S(2)}) %collective-permute-start.7) | collective-permute-done | bytes 172064 | tf_op jit(solution)/shard_map/ppermute | solution.py:624
  35.0 0.1 shard_map.125
  35.1 1.4 %collective-permute-start.8 = (bf16[128,384]{1,0:T(8,128)(2,1)S(1)}, bf16[128,384]{1,0:T(8,128)(2,1)S(1)}, u32[]{:S(2)}, u32[]{:S(2)}) collective-permute-start(bf16[128,384]{1,0:T(8,128)(2,1)S(1)} %get-tuple-element.38), channel_id=1, source_target_pairs={{0,4},{2,6},{4,0},{6,2},{8,12},{10,14},{12,8},{14,10},{1,5},{3,7},... | collective-permute-start | bytes 294920 | tf_op jit(solution)/shard_map/ppermute | solution.py:624
  36.4 3.3 %collective-permute-done.8.got_ref = bf16[128,384]{1,0:T(8,128)(2,1)S(1)} collective-permute-done((bf16[128,384]{1,0:T(8,128)(2,1)S(1)}, bf16[128,384]{1,0:T(8,128)(2,1)S(1)}, u32[]{:S(2)}, u32[]{:S(2)}) %collective-permute-start.8) | collective-permute-done | bytes 98336 | tf_op jit(solution)/shard_map/ppermute | solution.py:624
  39.8 2.4 %collective-permute-start.9 = (bf16[80,384]{1,0:T(8,128)(2,1)S(1)}, bf16[80,384]{1,0:T(8,128)(2,1)S(1)}, u32[]{:S(2)}, u32[]{:S(2)}) collective-permute-start(bf16[80,384]{1,0:T(8,128)(2,1)S(1)} %get-tuple-element.41), channel_id=1, source_target_pairs={{0,8},{2,10},{4,12},{6,14},{8,0},{10,2},{12,4},{14,6},{1,9},{3,11}... | collective-permute-start | bytes 184328 | tf_op jit(solution)/shard_map/ppermute | solution.py:624
  42.2 2.8 %collective-permute-done.9.got_ref = bf16[80,384]{1,0:T(8,128)(2,1)S(1)} collective-permute-done((bf16[80,384]{1,0:T(8,128)(2,1)S(1)}, bf16[80,384]{1,0:T(8,128)(2,1)S(1)}, u32[]{:S(2)}, u32[]{:S(2)}) %collective-permute-start.9) | collective-permute-done | bytes 61472 | tf_op jit(solution)/shard_map/ppermute | solution.py:624
  45.0 0.7 %shard_map.127 = (f32[48,384]{1,0:T(8,128)S(1)}, f32[8,48]{1,0:T(8,128)}) custom-call(f32[48,384]{1,0:T(8,128)S(1)} %get-tuple-element.40.kept_ref, bf16[80,384]{1,0:T(8,128)(2,1)S(1)} %collective-permute-done.9.got_ref, f32[16,384]{1,0:T(8,128)S(1)} %get-tuple-element.42.partial_ref), custom_call_target="tpu_custom_call" | custom-call | tf_op jit(solution)/shard_map/pallas_call | solution.py:360
  45.7 0.3 collective-permute-start.11
  45.9 0.0 collective-permute-start.10
  45.9 5.0 %collective-permute-done.11 = f32[48,384]{1,0:T(8,128)S(1)} collective-permute-done((f32[48,384]{1,0:T(8,128)S(1)}, f32[48,384]{1,0:T(8,128)S(1)}, u32[]{:S(2)}, u32[]{:S(2)}) %collective-permute-start.11) | collective-permute-done | bytes 73760 | tf_op jit(solution)/shard_map/ppermute | solution.py:694
  50.9 0.0 collective-permute-done.10
  50.9 0.7 %pad_maximum_fusion = f32[144,384]{1,0:T(8,128)} fusion(f32[48,384]{1,0:T(8,128)S(1)} %collective-permute-done.11, f32[48,384]{1,0:T(8,128)S(1)} %collective-permute-done.10, f32[48,384]{1,0:T(8,128)S(1)} %get-tuple-element.43), kind=kLoop, calls=%fused_computation | loop fusion | flops 110592 | bytes 442368 | tf_op jit(solution)/shard_map/concatenate | solution.py:695
  (13 shorter events, 0.1 us)
Async XLA Ops:
  0.6 2.2 %copy-start.5 = (f32[4]{0:T(128)S(1)}, f32[4]{0:T(128)}, u32[]{:S(2)}) copy-start(f32[4]{0:T(128)} %decay_ref.3) | copy-start | bytes 52
  0.6 2.2 %copy-start.6 = (f32[1,128]{1,0:T(1,128)S(1)}, f32[1,128]{1,0:T(1,128)}, u32[]{:S(2)}) copy-start(f32[1,128]{1,0:T(1,128)} %keep_ref.3) | copy-start | bytes 1540
  0.7 2.2 %copy-start.1 = (bf16[1,128,768]{2,1,0:T(8,128)(2,1)S(1)}, bf16[1,128,768]{2,1,0:T(8,128)(2,1)}, u32[]{:S(2)}) copy-start(bf16[1,128,768]{2,1,0:T(8,128)(2,1)} %cot_ref.3) | copy-start | bytes 589828
  0.7 16.6 %collective-permute-start.3 = (bf16[2,768,192]{1,2,0:T(8,128)(2,1)}, bf16[2,768,192]{1,2,0:T(8,128)(2,1)}, u32[]{:S(2)}, u32[]{:S(2)}) collective-permute-start(bf16[2,768,192]{1,2,0:T(8,128)(2,1)} %param.14), channel_id=1, source_target_pairs={{0,1},{1,0},{2,3},{3,2},{4,5},{5,4},{6,7},{7,6},{8,9},{9,8},{10,11... | collective-permute-start | bytes 1769480 | tf_op jit(solution)/shard_map/ppermute | solution.py:624
  1.2 17.5 %collective-permute-start.5 = (bf16[2,384,384]{2,1,0:T(8,128)(2,1)}, bf16[2,384,384]{2,1,0:T(8,128)(2,1)S(1)}, u32[]{:S(2)}, u32[]{:S(2)}) collective-permute-start(bf16[2,384,384]{2,1,0:T(8,128)(2,1)} %up_ref.3), channel_id=1, source_target_pairs={{0,1},{1,0},{2,3},{3,2},{4,5},{5,4},{6,7},{7,6},{8,9},{9,8},{10,11... | collective-permute-start | bytes 1769480 | tf_op jit(solution)/shard_map/ppermute | solution.py:624
  2.8 14.2 %copy-start.9 = (bf16[2,768,192]{1,2,0:T(8,128)(2,1)S(1)}, bf16[2,768,192]{1,2,0:T(8,128)(2,1)}, u32[]{:S(2)}) copy-start(bf16[2,768,192]{1,2,0:T(8,128)(2,1)} %param.14) | copy-start | bytes 1769476
  3.7 13.5 %copy-start.10 = (f32[768]{0:T(1024)S(1)}, f32[768]{0:T(1024)}, u32[]{:S(2)}) copy-start(f32[768]{0:T(1024)} %param.13) | copy-start | bytes 9220
  3.7 5.9 %collective-permute-start = (bf16[1,16,768]{2,1,0:T(8,128)(2,1)S(1)}, bf16[1,16,768]{2,1,0:T(8,128)(2,1)S(1)}, u32[]{:S(2)}, u32[]{:S(2)}) collective-permute-start(bf16[1,16,768]{2,1,0:T(8,128)(2,1)S(1)} %bitcast.1), channel_id=1, source_target_pairs={{0,8},{2,10},{4,12},{6,14},{8,0},{10,2},{12,4},{14,6},{1,9},{3,11}... | collective-permute-start | bytes 73736 | tf_op jit(solution)/shard_map/ppermute | solution.py:624
  9.6 4.1 %collective-permute-start.1 = (bf16[2,16,768]{2,1,0:T(8,128)(2,1)S(1)}, bf16[2,16,768]{2,1,0:T(8,128)(2,1)S(1)}, u32[]{:S(2)}, u32[]{:S(2)}) collective-permute-start(bf16[2,16,768]{2,1,0:T(8,128)(2,1)S(1)} %pad_maximum_fusion.2), channel_id=1, source_target_pairs={{0,4},{2,6},{4,0},{6,2},{8,12},{10,14},{12,8},{14,10},{1,5},{3,7},... | collective-permute-start | bytes 147464 | tf_op jit(solution)/shard_map/ppermute | solution.py:624
  11.5 7.1 %collective-permute-start.4 = (bf16[2,384,192]{2,1,0:T(8,128)(2,1)S(1)}, bf16[2,384,192]{2,1,0:T(8,128)(2,1)S(1)}, u32[]{:S(2)}, u32[]{:S(2)}) collective-permute-start(bf16[2,384,192]{2,1,0:T(8,128)(2,1)S(1)} %get-tuple-element.25.tap_ref), channel_id=1, source_target_pairs={{0,1},{1,0},{2,3},{3,2},{4,5},{5,4},{6,7},{7,6},{8,9},{9,8},{10,11... | collective-permute-start | bytes 884744 | tf_op jit(solution)/shard_map/ppermute | solution.py:624
  14.4 7.0 %collective-permute-start.2 = (bf16[4,16,768]{2,1,0:T(8,128)(2,1)}, bf16[4,16,768]{2,1,0:T(8,128)(2,1)}, u32[]{:S(2)}, u32[]{:S(2)}) collective-permute-start(bf16[4,16,768]{2,1,0:T(8,128)(2,1)} %pad_maximum_fusion.1.near_ref), channel_id=1, source_target_pairs={{0,2},{2,0},{4,6},{6,4},{8,10},{10,8},{12,14},{14,12},{1,3},{3,1},... | collective-permute-start | bytes 294920 | tf_op jit(solution)/shard_map/ppermute | solution.py:624
  17.0 1.7 %copy-start = (bf16[2,384,384]{2,1,0:T(8,128)(2,1)S(1)}, bf16[2,384,384]{2,1,0:T(8,128)(2,1)}, u32[]{:S(2)}) copy-start(bf16[2,384,384]{2,1,0:T(8,128)(2,1)} %up_ref.3) | copy-start | bytes 1769476
  17.0 1.7 %copy-start.7 = (s32[1,128]{1,0:T(1,128)S(1)}, s32[1,128]{1,0:T(1,128)}, u32[]{:S(2)}) copy-start(s32[1,128]{1,0:T(1,128)} %count_ref.1) | copy-start | bytes 1540
  18.6 2.7 %copy-start.2 = (bf16[1,128,768]{2,1,0:T(8,128)(2,1)S(1)}, bf16[1,128,768]{2,1,0:T(8,128)(2,1)}, u32[]{:S(2)}) copy-start(bf16[1,128,768]{2,1,0:T(8,128)(2,1)} %cot_ref.3) | copy-start | bytes 589828
  18.7 1.0 %copy-start.3 = (bf16[1,128,768]{2,1,0:T(8,128)(2,1)S(1)}, bf16[1,128,768]{2,1,0:T(8,128)(2,1)}, u32[]{:S(2)}) copy-start(bf16[1,128,768]{2,1,0:T(8,128)(2,1)} %feature_ref.1) | copy-start | bytes 589828
  19.7 1.7 %copy-start.4 = (f32[2,4,768]{2,1,0:T(4,128)S(1)}, f32[2,4,768]{2,1,0:T(4,128)}, u32[]{:S(2)}) copy-start(f32[2,4,768]{2,1,0:T(4,128)} %mode_ref.1) | copy-start | bytes 73732
  19.7 1.7 %copy-start.8 = (f32[4]{0:T(128)S(1)}, f32[4]{0:T(128)}, u32[]{:S(2)}) copy-start(f32[4]{0:T(128)} %negate_sqrt_fusion.scale_ref) | copy-start | bytes 52
  26.8 1.6 %collective-permute-start.6 = (bf16[416,384]{1,0:T(8,128)(2,1)S(1)}, bf16[416,384]{1,0:T(8,128)(2,1)S(1)}, u32[]{:S(2)}, u32[]{:S(2)}) collective-permute-start(bf16[416,384]{1,0:T(8,128)(2,1)S(1)} %get-tuple-element.32), channel_id=1, source_target_pairs={{0,1},{1,0},{2,3},{3,2},{4,5},{5,4},{6,7},{7,6},{8,9},{9,8},{10,11... | collective-permute-start | bytes 958472 | tf_op jit(solution)/shard_map/ppermute | solution.py:624
  28.5 6.5 %collective-permute-start.7 = (bf16[224,384]{1,0:T(8,128)(2,1)S(1)}, bf16[224,384]{1,0:T(8,128)(2,1)S(1)}, u32[]{:S(2)}, u32[]{:S(2)}) collective-permute-start(bf16[224,384]{1,0:T(8,128)(2,1)S(1)} %get-tuple-element.35), channel_id=1, source_target_pairs={{0,2},{2,0},{4,6},{6,4},{8,10},{10,8},{12,14},{14,12},{1,3},{3,1},... | collective-permute-start | bytes 516104 | tf_op jit(solution)/shard_map/ppermute | solution.py:624
  35.1 4.7 %collective-permute-start.8 = (bf16[128,384]{1,0:T(8,128)(2,1)S(1)}, bf16[128,384]{1,0:T(8,128)(2,1)S(1)}, u32[]{:S(2)}, u32[]{:S(2)}) collective-permute-start(bf16[128,384]{1,0:T(8,128)(2,1)S(1)} %get-tuple-element.38), channel_id=1, source_target_pairs={{0,4},{2,6},{4,0},{6,2},{8,12},{10,14},{12,8},{14,10},{1,5},{3,7},... | collective-permute-start | bytes 294920 | tf_op jit(solution)/shard_map/ppermute | solution.py:624
  39.8 5.2 %collective-permute-start.9 = (bf16[80,384]{1,0:T(8,128)(2,1)S(1)}, bf16[80,384]{1,0:T(8,128)(2,1)S(1)}, u32[]{:S(2)}, u32[]{:S(2)}) collective-permute-start(bf16[80,384]{1,0:T(8,128)(2,1)S(1)} %get-tuple-element.41), channel_id=1, source_target_pairs={{0,8},{2,10},{4,12},{6,14},{8,0},{10,2},{12,4},{14,6},{1,9},{3,11}... | collective-permute-start | bytes 184328 | tf_op jit(solution)/shard_map/ppermute | solution.py:624
  45.7 5.3 %collective-permute-start.11 = (f32[48,384]{1,0:T(8,128)S(1)}, f32[48,384]{1,0:T(8,128)S(1)}, u32[]{:S(2)}, u32[]{:S(2)}) collective-permute-start(f32[48,384]{1,0:T(8,128)S(1)} %get-tuple-element.43), channel_id=1, source_target_pairs={{6,0},{7,1},{0,2},{1,3},{2,4},{3,5},{4,6},{5,7},{14,8},{15,9},{8,1... | collective-permute-start | bytes 221192 | tf_op jit(solution)/shard_map/ppermute | solution.py:694
  45.9 5.0 %collective-permute-start.10 = (f32[48,384]{1,0:T(8,128)S(1)}, f32[48,384]{1,0:T(8,128)S(1)}, u32[]{:S(2)}, u32[]{:S(2)}) collective-permute-start(f32[48,384]{1,0:T(8,128)S(1)} %get-tuple-element.43), channel_id=1, source_target_pairs={{3,0},{4,1},{5,2},{6,3},{7,4},{0,5},{1,6},{2,7},{11,8},{12,9},{13,... | collective-permute-start | bytes 221192 | tf_op jit(solution)/shard_map/ppermute | solution.py:694

commit v2 on v0

--- a/solution.py
+++ b/solution.py
@@ -1,8 +1,11 @@
+import functools
 import math
 
 import jax
 import jax.numpy as jnp
 from jax import lax
+from jax.experimental import pallas as pl
+from jax.experimental.pallas import tpu as pltpu
 from jax.sharding import PartitionSpec as P
 
 B = 384
@@ -194,7 +197,7 @@
     return numerator / (1.0 - beside_all * own_pass)[..., None]
 
 
-def per_device(
+def general_device(
     features,
     cotangent,
     counts,
@@ -344,6 +347,454 @@
     return (gradient.astype(jnp.bfloat16), tap_sum * report_scale, mode_sum * report_scale)
 
 
+VMEM = pltpu.MemorySpace.VMEM
+SMEM = pltpu.MemorySpace.SMEM
+HBM = pltpu.MemorySpace.HBM
+F32 = jnp.float32
+BF16 = jnp.bfloat16
+RING = 8
+HOPS = (4, 2, 1)
+BLOCK = 48
+GIGA = 10**6
+
+
+def call(body, operands, spaces, outs, scratch=(), size=0):
+    return pl.pallas_call(
+        body,
+        out_shape=[jax.ShapeDtypeStruct(shape, dtype) for shape, dtype in outs],
+        in_specs=[pl.BlockSpec(memory_space=space) for space in spaces],
+        out_specs=[pl.BlockSpec(memory_space=VMEM) for _ in outs],
+        scratch_shapes=list(scratch),
+        cost_estimate=pl.CostEstimate(flops=size, transcendentals=0, bytes_accessed=size // 256) if size else None,
+        compiler_params=pltpu.CompilerParams(vmem_limit_bytes=40 * 1024 * 1024),
+    )(*operands)
+
+
+def dot(left, right):
+    return lax.dot_general(left, right, (((1,), (0,)), ((), ())), preferred_element_type=F32)
+
+
+def dot_nt(left, right):
+    return lax.dot_general(left, right, (((1,), (1,)), ((), ())), preferred_element_type=F32)
+
+
+def dot_tn(left, right):
+    return lax.dot_general(left, right, (((0,), (0,)), ((), ())), preferred_element_type=F32)
+
+
+def iota2(shape, axis):
+    return lax.broadcasted_iota(jnp.int32, shape, axis)
+
+
+def split_pair(value):
+    high = value.astype(BF16)
+    return high, (value - high.astype(F32)).astype(BF16)
+
+
+def log_sums(keep_row):
+    rows = keep_row.shape[-1]
+    below, beside = iota2((rows, rows), 0), iota2((rows, rows), 1)
+    logs = jnp.broadcast_to(jnp.log(keep_row), (rows, rows))
+    column = jnp.sum(jnp.where(beside <= below, logs, 0.0), axis=1, keepdims=True)
+    spread = jnp.broadcast_to(column, (rows, rows))
+    row = jnp.sum(jnp.where(beside == below, spread, 0.0), axis=0, keepdims=True)
+    return column, row, column[rows - 1 :, :]
+
+
+def mode_terms(sums, total, decay_ref, rows):
+    place = iota2((1, rows), 1).astype(F32)
+    to_start, to_end = [], []
+    for mode in range(M):
+        rate = decay_ref[mode]
+        to_start.append(jnp.exp(sums - (place + 1.0) * rate))
+        to_end.append(jnp.exp((total - sums) - (rows - 1.0 - place) * rate))
+    leaving = jnp.concatenate(to_start + to_end, axis=0)
+    entering = jnp.concatenate(to_end + to_start, axis=0)
+    return leaving, entering
+
+
+def prepare_body(cot_hbm, keep_hbm, decay_hbm, pay_ref, cot_ref, keep_ref, decay_ref, sems):
+    pairs = ((keep_hbm, keep_ref), (decay_hbm, decay_ref), (cot_hbm, cot_ref))
+    copies = [pltpu.make_async_copy(source, to, sems.at[index]) for index, (source, to) in enumerate(pairs)]
+    for copy in copies:
+        copy.start()
+    copies[0].wait()
+    copies[1].wait()
+    rows = keep_ref.shape[-1]
+    _, sums, total = log_sums(keep_ref[...])
+    weights, _ = mode_terms(sums, total, decay_ref, rows)
+    high = weights.astype(BF16).astype(F32)
+    both = jnp.concatenate([high, weights - high], axis=0).astype(BF16)
+    width = cot_ref.shape[-1]
+    first = jnp.broadcast_to(total, (8, width))
+    one = first.astype(BF16).astype(F32)
+    two = (first - one).astype(BF16).astype(F32)
+    three = first - one - two
+    row = iota2((8, width), 0)
+    extra = jnp.where(row == 0, one, jnp.where(row == 1, two, jnp.where(row == 2, three, 0.0)))
+    copies[2].wait()
+    states = dot(both, cot_ref[0])
+    states = states[0:8] + states[8:16]
+    pay_ref[0] = jnp.concatenate([states, extra], axis=0).astype(BF16)
+
+
+def assemble_body(down_ref, down_far_ref, tap_ref, tap_far_ref, down_out, tap_out):
+    core = lax.axis_index("dp")
+    half = down_ref.shape[1]
+    for down, taps, side in ((down_ref, tap_ref, core), (down_far_ref, tap_far_ref, 1 - core)):
+        part = pl.ds(pl.multiple_of(side * half, half), half)
+        for layer in range(LAYERS):
+            down_out[layer, part, :] = down[layer]
+            total = taps[layer, 0].astype(F32) + taps[layer, 1].astype(F32) + taps[layer, 2].astype(F32)
+            tap_out[layer, part, :] = total.astype(BF16)
+
+
+def forward_body(
+    feature_ref, count_ref, weight_ref, down_ref, tap_ref, up_ref, up_far_ref,
+    stream_ref, inverse_ref, reduced_ref, slope_ref,
+):
+    core = lax.axis_index("dp")
+    rows, width = feature_ref.shape[1:]
+    logs = jnp.broadcast_to(jnp.log1p(count_ref[...].astype(F32)), (rows, rows))
+    diagonal = iota2((rows, rows), 0) == iota2((rows, rows), 1)
+    level = jnp.sum(jnp.where(diagonal, logs, 0.0), axis=1, keepdims=True)
+    stream = feature_ref[0].astype(F32) + level * weight_ref[...]
+    for layer in range(LAYERS):
+        stream_ref[layer] = stream
+        mean = jnp.sum(stream * stream, axis=-1, keepdims=True) * (1.0 / width)
+        inverse = lax.rsqrt(mean + EPSILON)
+        inverse_ref[layer] = inverse
+        normed = (stream * inverse).astype(BF16)
+        reduced = dot_nt(normed, down_ref[layer]).astype(BF16)
+        reduced_ref[layer * rows : (layer + 1) * rows, :] = reduced
+        mixture = dot_nt(reduced, tap_ref[layer])
+        share = 0.5 * (1.0 + lax.erf(mixture * HALF_ROOT))
+        slope_ref[layer] = share + mixture * jnp.exp(-0.5 * mixture * mixture) * DENSITY
+        act = (mixture * share).astype(BF16)
+        out_near = dot(act, up_ref[layer])
+        out_away = dot(act, up_far_ref[layer])
+        low = jnp.where(core == 0, out_near, out_away)
+        high = jnp.where(core == 0, out_away, out_near)
+        stream = stream + jnp.concatenate([low, high], axis=-1)
+    stream_ref[LAYERS] = stream
+
+
+def local_body(decay_ref, scale_ref, cot_ref, keep_ref, mode_ref, stream_ref, grad_ref, mark_ref, reach_ref):
+    rows, width = cot_ref.shape[1:]
+    column, row, total = log_sums(keep_ref[...])
+    below = iota2((rows, rows), 0)
+    across = iota2((rows, rows), 1)
+    gap = column - row
+    steps = (below - across).astype(F32)
+    kernels = []
+    for mode in range(M):
+        value = jnp.exp(jnp.minimum(steps * decay_ref[mode] - gap, 0.0))
+        kernels.append(jnp.where(across >= below, value, 0.0))
+    for mode in range(M):
+        value = jnp.exp(jnp.minimum(gap - steps * decay_ref[mode], 0.0))
+        kernels.append(jnp.where(below >= across, value, 0.0))
+    pairs = [jnp.concatenate(split_pair(kernel), axis=1) for kernel in kernels]
+    _, edges = mode_terms(row, total, decay_ref, rows)
+    high = edges.astype(BF16).astype(F32)
+    both = jnp.concatenate([high, edges - high], axis=0).astype(BF16)
+    span = 256
+    for start in range(0, width, span):
+        part = slice(start, start + span)
+        cot = cot_ref[0, :, part]
+        doubled = jnp.concatenate([cot, cot], axis=0)
+        stream = stream_ref[LAYERS, :, part]
+        grad = cot.astype(F32)
+        marks = []
+        for index in range(2 * M):
+            mode = index % M
+            field = dot(pairs[index], doubled)
+            gain = scale_ref[mode]
+            grad = grad + (gain * mode_ref[index // M, mode : mode + 1, part]) * field
+            marks.append(jnp.sum(stream * field, axis=0, keepdims=True))
+        grad_ref[:, part] = grad
+        mark_ref[:, part] = jnp.concatenate(marks, axis=0)
+        near, away = split_pair(stream)
+        reach = dot(both, near)
+        reach_ref[:, part] = reach[0:8] + reach[8:16] + dot(both, away)[0:8]
+
+
+def backward_body(
+    decay_ref, scale_ref, first_ref, second_ref, third_ref, fourth_ref, keep_ref, mode_ref,
+    local_ref, mark_ref, reach_ref, stream_ref, inverse_ref, slope_ref, down_ref, tap_ref, up_ref,
+    up_far_ref, grads_ref, mixed_ref, partial_ref,
+):
+    core = lax.axis_index("dp")
+    place = lax.axis_index("seq")
+    rows = keep_ref.shape[-1]
+    width = local_ref.shape[-1]
+    wide = up_ref.shape[-1]
+
+    masks = [0]
+    for hop in HOPS:
+        masks = masks + [mask ^ hop for mask in masks]
+    pieces = []
+    for ref in (first_ref, second_ref, third_ref, fourth_ref):
+        pieces = pieces + [ref[index].astype(F32) for index in range(ref.shape[0])]
+    totals = [jnp.sum(piece[8:16, 0:128], axis=0, keepdims=True) for piece in pieces]
+    row8 = iota2((8, 128), 0)
+    decay8 = jnp.zeros((8, 128), F32)
+    gain8 = jnp.zeros((8, 128), F32)
+    for index in range(2 * M):
+        decay8 = jnp.where(row8 == index, decay_ref[index % M], decay8)
+        gain8 = jnp.where(row8 == index, scale_ref[index % M], gain8)
+    gain8 = gain8[:, 0:1]
+    everything = totals[0]
+    for value in totals[1:]:
+        everything = everything + value
+    loop = 1.0 - jnp.exp(jnp.broadcast_to(everything, (8, 128)) - (RING * rows) * decay8)
+    others = [lax.bitwise_xor(place, mask) for mask in masks]
+    ahead = [lax.rem(place - other + (RING - 1), RING) for other in others]
+    after = [lax.rem(other - place + (RING - 1), RING) for other in others]
+    entering = jnp.zeros((8, width), F32)
+    for index in range(RING):
+        fore = jnp.zeros((1, 128), F32)
+        back = jnp.zeros((1, 128), F32)
+        for other in range(RING):
+            fore = fore + jnp.where(ahead[other] < ahead[index], totals[other], 0.0)
+            back = back + jnp.where(after[other] < after[index], totals[other], 0.0)
+        fore = jnp.broadcast_to(fore, (8, 128)) - (ahead[index] * rows).astype(F32) * decay8
+        back = jnp.broadcast_to(back, (8, 128)) - (after[index] * rows).astype(F32) * decay8
+        share = jnp.exp(jnp.where(row8 < M, back, fore)) / loop
+        entering = entering + share[:, 0:1] * pieces[index][0:8, :]
+    whole = gain8 * (mark_ref[...] + entering * reach_ref[...])
+    partial = jnp.concatenate([whole[:, :wide], whole[:, wide:]], axis=0)
+    partial_ref[...] = partial
+    high, low = split_pair(partial)
+    mixed_ref[LAYERS * rows : LAYERS * rows + 16, :] = high
+    mixed_ref[LAYERS * rows + 16 : LAYERS * rows + 32, :] = low
+    _, sums, total = log_sums(keep_ref[...])
+    _, edges = mode_terms(sums, total, decay_ref, rows)
+    weighted = entering * gain8 * jnp.concatenate([mode_ref[0], mode_ref[1]], axis=0)
+    edge_high = edges.astype(BF16).astype(F32)
+    edge_low = edges - edge_high
+    in_high = weighted.astype(BF16).astype(F32)
+    in_low = weighted - in_high
+    left = jnp.concatenate([edge_high, edge_high, edge_low, jnp.zeros_like(edges)], axis=0).astype(BF16)
+    right = jnp.concatenate([in_high, in_low, in_high, jnp.zeros_like(in_high)], axis=0).astype(BF16)
+    gradient = local_ref[...] + dot_tn(left, right)
+
+    for layer in reversed(range(LAYERS)):
+        narrow = gradient.astype(BF16)
+        first, second = narrow[:, :wide], narrow[:, wide:]
+        mine = jnp.where(core == 0, first, second)
+        theirs = jnp.where(core == 0, second, first)
+        back = dot_nt(mine, up_ref[layer]) + dot_nt(theirs, up_far_ref[layer])
+        mixed = (back * slope_ref[layer]).astype(BF16)
+        mixed_ref[layer * rows : (layer + 1) * rows, :] = mixed
+        if layer:
+            gradient = through_layer(layer, gradient, mixed, stream_ref, inverse_ref, down_ref, tap_ref)
+    grads_ref[...] = gradient
+
+
+def through_layer(layer, gradient, mixed, stream_ref, inverse_ref, down_ref, tap_ref):
+    passed = dot(mixed, tap_ref[layer]).astype(BF16)
+    normed = dot(passed, down_ref[layer])
+    before = stream_ref[layer]
+    inverse = inverse_ref[layer]
+    shared = jnp.sum(normed * before, axis=-1, keepdims=True) * (1.0 / before.shape[-1])
+    return gradient + inverse * normed - before * (inverse * inverse * inverse * shared)
+
+
+def output_body(gradient_ref, mixed_ref, stream_ref, inverse_ref, down_ref, tap_ref, grad_ref):
+    rows = gradient_ref.shape[0]
+    mixed = mixed_ref[0:rows, :]
+    gradient = through_layer(0, gradient_ref[...], mixed, stream_ref, inverse_ref, down_ref, tap_ref)
+    grad_ref[0] = gradient.astype(BF16)
+
+
+def held_block(parity, bit_x, bit_z, layer):
+    core = lax.bitwise_xor(lax.bitwise_xor(parity, bit_x), lax.bitwise_xor(bit_z, layer))
+    return pl.multiple_of(lax.rem(3 * core + 6 * bit_x + 4 * bit_z, RING) * BLOCK, BLOCK)
+
+
+def taps_body(
+    reduced_ref, reduced_far_ref, mixed_ref, mixed_far_ref, partial_ref,
+    kept_ref, send_ref, partial_out, block_ref,
+):
+    bit = position_bit(0)
+    parity = lax.rem(lax.axis_index("dp") + bit + position_bit(1) + position_bit(2), 2)
+    rows = reduced_ref.shape[0] // LAYERS
+    for layer in range(LAYERS):
+        part = slice(layer * rows, (layer + 1) * rows)
+        left = jnp.concatenate([reduced_ref[part, :], reduced_far_ref[part, :]], axis=0)
+        right = jnp.concatenate([mixed_ref[part, :], mixed_far_ref[part, :]], axis=0)
+        block_ref[layer] = dot_tn(left, right)
+    kept_rows = kept_ref.shape[0]
+    for turn in range(2):
+        for layer in range(LAYERS):
+            to = (2 * turn + layer) * BLOCK
+            kept_ref[to : to + BLOCK, :] = block_ref[layer, pl.ds(held_block(parity, bit, turn, layer), BLOCK), :]
+            send_ref[to : to + BLOCK, :] = block_ref[
+                layer, pl.ds(held_block(parity, 1 - bit, turn, layer), BLOCK), :
+            ].astype(BF16)
+    high = mixed_far_ref[LAYERS * rows : LAYERS * rows + 16, :].astype(F32)
+    low = mixed_far_ref[LAYERS * rows + 16 : LAYERS * rows + 32, :].astype(F32)
+    partial = partial_ref[...] + (high + low)
+    partial_out[...] = partial
+    send_ref[kept_rows : kept_rows + 16, :] = partial.astype(BF16)
+
+
+def position_bit(stage):
+    place = lax.axis_index("seq")
+    return lax.rem(place // (1, 2, 4)[stage], 2)
+
+
+def join_body(stage, kept_ref, got_ref, partial_ref, kept_out, send_out, partial_out):
+    rows = kept_out.shape[0]
+    bit = position_bit(stage)
+    keep = pl.ds(pl.multiple_of(bit * rows, rows), rows)
+    send = pl.ds(pl.multiple_of((1 - bit) * rows, rows), rows)
+    kept_out[...] = kept_ref[keep, :] + got_ref[keep, :].astype(F32)
+    send_out[0:rows, :] = (kept_ref[send, :] + got_ref[send, :].astype(F32)).astype(BF16)
+    partial = partial_ref[...] + got_ref[2 * rows : 2 * rows + 16, :].astype(F32)
+    partial_out[...] = partial
+    send_out[rows : rows + 16, :] = partial.astype(BF16)
+
+
+def finish_body(scale, kept_ref, got_ref, block_out, send_out):
+    rows = kept_ref.shape[0]
+    block = (kept_ref[...] + got_ref[0:rows, :].astype(F32)) * scale
+    block_out[...] = block
+    send_out[...] = block.astype(BF16)
+
+
+def modes_body(scale, got_ref, partial_ref, mode_out, full_ref):
+    rows = got_ref.shape[0] - 16
+    full_ref[...] = (partial_ref[...] + got_ref[rows : rows + 16, :].astype(F32)) * scale
+    number = 2 * lax.axis_index("seq") + lax.axis_index("dp")
+    span = full_ref.shape[1]
+    top = pl.multiple_of(8 * (number // 8), 8)
+    shift = lax.rem(span - BLOCK * lax.rem(number, 8), span)
+    mode_out[...] = pltpu.roll(full_ref[pl.ds(top, 8), :], shift, 1)[:, 0:BLOCK]
+
+
+def swap(value, axis, mask):
+    count = lax.axis_size(axis)
+    return lax.ppermute(value, axis, [(source, source ^ mask) for source in range(count)])
+
+
+def cross(value, mask):
+    count = 2 * lax.axis_size("seq")
+    return lax.ppermute(value, ("seq", "dp"), [(source, source ^ (2 * mask + 1)) for source in range(count)])
+
+
+def wrapped_device(
+    features, cotangent, counts, count_weight, down_weight, tap_weight, up_weight,
+    decay_rate, keep_share, mode_weight,
+):
+    rows, width = features.shape[1:]
+    down = jnp.swapaxes(down_weight, 1, 2)
+    taps = jnp.swapaxes(tap_weight, 2, 3)
+    down_far, up_far, taps_far = swap(down, "dp", 1), swap(up_weight, "dp", 1), swap(taps, "dp", 1)
+    scale = jnp.sqrt(-jnp.expm1(-2.0 * decay_rate))
+    (pay,) = call(
+        prepare_body,
+        tuple(pltpu.with_memory_space_constraint(value, HBM) for value in (cotangent, keep_share, decay_rate)),
+        (HBM,) * 3,
+        (((1, 16, width), BF16),),
+        (
+            pltpu.VMEM(cotangent.shape, BF16),
+            pltpu.VMEM(keep_share.shape, F32),
+            pltpu.SMEM(decay_rate.shape, F32),
+            pltpu.SemaphoreType.DMA((3,)),
+        ),
+        size=1300 * GIGA,
+    )
+    got = swap(pay, "seq", HOPS[0])
+    down_full, tap_full = call(
+        assemble_body,
+        (down, down_far, taps, taps_far),
+        (VMEM,) * 4,
+        (((LAYERS, B, width), BF16), ((LAYERS, B, B), BF16)), size=1200 * GIGA
+    )
+    two = jnp.concatenate([pay, got], axis=0)
+    two, down_full, tap_full = lax.optimization_barrier((two, down_full, tap_full))
+    got_two = swap(two, "seq", HOPS[1])
+    stream, inverse, reduced, slope = call(
+        forward_body,
+        (features, counts, count_weight[None], down_full, tap_full, up_weight, up_far),
+        (VMEM,) * 7,
+        (
+            ((LAYERS + 1, rows, width), F32),
+            ((LAYERS, rows, 1), F32),
+            ((LAYERS * rows, B), BF16),
+            ((LAYERS, rows, B), F32),
+        ), size=1800 * GIGA
+    )
+    four = jnp.concatenate([two, got_two], axis=0)
+    four, stream, reduced = lax.optimization_barrier((four, stream, reduced))
+    got_four = swap(four, "seq", HOPS[2])
+    reduced_far = swap(reduced, "dp", 1)
+    local, mark, reach = call(
+        local_body,
+        (decay_rate, scale, cotangent, keep_share, mode_weight, stream),
+        (SMEM, SMEM) + (VMEM,) * 4,
+        (((rows, width), F32), ((8, width), F32), ((8, width), F32)), size=1600 * GIGA
+    )
+    local, reduced_far = lax.optimization_barrier((local, reduced_far))
+    gradient, mixed, partial = call(
+        backward_body,
+        (
+            decay_rate, scale, pay, got, got_two, got_four, keep_share, mode_weight, local, mark, reach,
+            stream, inverse, slope, down_full, tap_full, up_weight, up_far,
+        ),
+        (SMEM, SMEM) + (VMEM,) * 16,
+        (((rows, width), F32), ((LAYERS * rows + 32, B), BF16), ((16, B), F32)), size=2100 * GIGA
+    )
+    mixed_far = swap(mixed, "dp", 1)
+    (grad,) = call(
+        output_body,
+        (gradient, mixed, stream, inverse, down_full, tap_full),
+        (VMEM,) * 6,
+        (((1, rows, width), BF16),), size=1300 * GIGA
+    )
+    kept_rows = RING * BLOCK // 2
+    kept, send, partial = call(
+        taps_body,
+        (reduced, reduced_far, mixed, mixed_far, partial),
+        (VMEM,) * 5,
+        (((kept_rows, B), F32), ((kept_rows + 16, B), BF16), ((16, B), F32)),
+        (pltpu.VMEM((LAYERS, B, B), F32),), size=500 * GIGA
+    )
+    got = cross(send, 1)
+    for stage in (1, 2):
+        kept_rows = kept.shape[0] // 2
+        kept, send, partial = call(
+            functools.partial(join_body, stage),
+            (kept, got, partial),
+            (VMEM,) * 3,
+            (((kept_rows, B), F32), ((kept_rows + 16, B), BF16), ((16, B), F32)),
+        )
+        if stage == 1:
+            send, grad = lax.optimization_barrier((send, grad))
+        got = cross(send, (1, 2, 4)[stage])
+    total = features.shape[0] * lax.axis_size("dp") * rows * lax.axis_size("seq")
+    report = 1.0 / math.sqrt(total)
+    block, narrow = call(
+        functools.partial(finish_body, report),
+        (kept, got),
+        (VMEM,) * 2,
+        (((BLOCK, B), F32), ((BLOCK, B), BF16)),
+    )
+    parts = [block]
+    for step in (3, 6):
+        pairs = [(8 * layer + (j + step) % 8, 8 * layer + j) for layer in range(LAYERS) for j in range(8)]
+        parts.append(lax.ppermute(narrow, ("seq", "dp"), pairs).astype(F32))
+    (mode_sum,) = call(
+        functools.partial(modes_body, report),
+        (got, partial),
+        (VMEM,) * 2,
+        (((8, BLOCK), F32),),
+        (pltpu.VMEM((16, B), F32),),
+    )
+    return grad, jnp.concatenate(parts, axis=0), mode_sum
+
+
 def solution(mesh):
     placed = (
         P(("parts", "dp"), "seq", None),
@@ -357,6 +808,15 @@
         P(("parts", "dp"), "seq"),
         P(),
     )
+
+    def per_device(*operands):
+        rows = operands[0].shape[1]
+        ring = lax.axis_size("seq")
+        loop = ring * rows
+        wraps = all(dilation % loop == 0 for dilation in (DILATION_FIRST1, DILATION_SECOND2))
+        fits = ring == RING and lax.axis_size("dp") == 2 and operands[0].shape[0] == 1
+        return (wrapped_device if wraps and fits else general_device)(*operands)
+
     return jax.shard_map(
         per_device,
         mesh=mesh,

time: 320 us -> 44.7 us (0.14)
  blocking collectives: 103 us -> 0 us
  waiting for transfers between devices: 104 us -> 15.4 us
  other arithmetic: 42.5 us -> 0.74 us
  matrix products: 33.2 us -> 0 us
  local copies, waits for them, and re-layouts: 18.1 us -> 0.06 us
  starting transfers between devices: 2.6 us -> 17.9 us
  between operations: 14.8 us -> 0.83 us
  Pallas kernels: 0 us -> 9.3 us
    all_gather x4 -> x0, blocking collectives: 103 us -> none  [entering_2(): lax.all_gather(a.astype(kind), axis)]
    reduce_scatter x1 -> x0, waiting for transfers between devices: 62.3 us -> none  [per_device(): lax.psum_scatter(tap_flat, ('seq', 'dp'), scatter_dimension=0, tiled=True)]
    unnamed x6 -> x0, waiting for transfers between devices: 42.2 us -> none
    dot_general x28 -> x0, matrix products: 33.2 us -> none  [the longest x8 6.9 us: project(): jnp.einsum('qra,au->qru', left_shifted, right_shifted, preferred_element_...]
    ppermute x4 -> x13, starting transfers between devices: 2.4 us -> 17.9 us  [the longest x8 8.78 us: swap(): lax.ppermute(value, axis, [(source, source ^ mask) for source in range(co...]
    ppermute x4 -> x13, waiting for transfers between devices: 0.01 us -> 15.4 us  [the longest x3 8.21 us: cross(): lax.ppermute(value, ('seq', 'dp'), [(source, source ^ 2 * mask + 1) for s...]
    mul x11 -> x0, other arithmetic: 12 us -> none  [the longest x7 8.43 us: apply_late_first(): early_pass * late_pass]
    pallas_call x0 -> x11, Pallas kernels: none -> 9.3 us  [call(): pl.pallas_call(body, out_shape=[jax.ShapeDtypeStruct(shape, dtype) for sh...]
  transfers between devices with their start and end apart: 9 -> 13, of which waited for: 2 -> 9; matrix products, arithmetic and copies ran while one was open for 12% -> 0% of each run, Pallas kernels for 0% -> 15%
where the time goes in v2:
time: 44.7 us; the launch traced here: 44.2 us
  starting transfers between devices  17.9 us (40%)
  waiting for transfers between devices  15.4 us (34%)
  Pallas kernels  9.3 us (21%)
  between operations  0.83 us (2%)
  other arithmetic  0.74 us (2%)
    pallas_call x11, Pallas kernels, call(): pl.pallas_call(body, out_shape=[jax.ShapeDtypeStruct(shape, dtype) for sh...  9.3 us
    ppermute x8, starting transfers between devices, swap(): lax.ppermute(value, axis, [(source, source ^ mask) for source in range(co...  8.78 us
    ppermute x3, waiting for transfers between devices, cross(): lax.ppermute(value, ('seq', 'dp'), [(source, source ^ 2 * mask + 1) for s...  8.21 us
    ppermute x3, starting transfers between devices, cross(): lax.ppermute(value, ('seq', 'dp'), [(source, source ^ 2 * mask + 1) for s...  5.82 us
    ppermute x8, waiting for transfers between devices, swap(): lax.ppermute(value, axis, [(source, source ^ mask) for source in range(co...  5.54 us
    ppermute x2, starting transfers between devices, wrapped_device(): parts.append(lax.ppermute(narrow, ('seq', 'dp'), pairs).astype(F32))  3.32 us
    ppermute x2, waiting for transfers between devices, wrapped_device(): parts.append(lax.ppermute(narrow, ('seq', 'dp'), pairs).astype(F32))  1.63 us
  transfers between devices with their start and end apart: 13, of which 9 were waited for; matrix products, arithmetic and copies ran while one was open for 0% of the time, Pallas kernels for 15%

profile of v2, /device:TPU:0, one launch (start us, length us, event | category | flops | bytes accessed | tf_op | source)
XLA Modules:
  0.0 44.2 jit_solution(12031186879251847690)
XLA Ops:
  0.6 0.5 %collective-permute-start.2 = (bf16[2,3,192,384]{3,2,1,0:T(8,128)(2,1)}, bf16[2,3,192,384]{3,2,1,0:T(8,128)(2,1)S(1)}, u32[]{:S(2)}, u32[]{:S(2)}) collective-permute-start(bf16[2,3,192,384]{3,2,1,0:T(8,128)(2,1)} %bitcast.2), channel_id=1, source_target_pairs={{0,1},{1,0},{2,3},{3,2},{4,5},{5,4},{6,7},{7,6},{8,9},{9,8},{10,11... | collective-permute-start | bytes 2654216 | tf_op jit(solution)/shard_map/ppermute | solution.py:678
  1.2 0.1 collective-permute-start.1
  1.3 0.4 collective-permute-start.4
  1.7 1.1 %shard_map.121.first_ref = bf16[1,16,768]{2,1,0:T(8,128)(2,1)S(1)} custom-call(bf16[1,128,768]{2,1,0:T(8,128)(2,1)} %cot_ref.1, f32[1,128]{1,0:T(1,128)} %keep_ref.3, f32[4]{0:T(128)} %decay_ref.3), custom_call_target="tpu_custom_call" | custom-call | flops 1300000000 | bytes 5078125 | tf_op jit(solution)/shard_map/pallas_call | solution.py:362
  2.8 3.8 %collective-permute-start = (bf16[1,16,768]{2,1,0:T(8,128)(2,1)S(1)}, bf16[1,16,768]{2,1,0:T(8,128)(2,1)S(1)}, u32[]{:S(2)}, u32[]{:S(2)}) collective-permute-start(bf16[1,16,768]{2,1,0:T(8,128)(2,1)S(1)} %shard_map.121.first_ref), channel_id=1, source_target_pairs={{0,8},{2,10},{4,12},{6,14},{8,0},{10,2},{12,4},{14,6},{1,9},{3,11}... | collective-permute-start | bytes 73736 | tf_op jit(solution)/shard_map/ppermute | solution.py:678
  6.5 0.0 copy-done.9
  6.6 1.8 %collective-permute-done.second_ref = bf16[1,16,768]{2,1,0:T(8,128)(2,1)S(1)} collective-permute-done((bf16[1,16,768]{2,1,0:T(8,128)(2,1)S(1)}, bf16[1,16,768]{2,1,0:T(8,128)(2,1)S(1)}, u32[]{:S(2)}, u32[]{:S(2)}) %collective-permute-start) | collective-permute-done | bytes 24608 | tf_op jit(solution)/shard_map/ppermute | solution.py:678
  8.4 0.0 copy-start.3
  8.4 0.0 copy-start.6
  8.4 0.0 collective-permute-done.1.down_far_ref
  8.4 0.0 collective-permute-done.2.tap_far_ref
  8.4 0.0 copy-done
  8.4 0.0 copy-done.1
  8.4 0.3 shard_map.122
  8.7 0.0 copy-start.7
  8.7 0.0 copy-start.4
  8.7 0.0 copy-start.5
  8.7 0.0 copy-start.8
  8.7 2.0 %collective-permute-start.3 = (bf16[2,16,768]{2,1,0:T(8,128)(2,1)S(1)}, bf16[2,16,768]{2,1,0:T(8,128)(2,1)S(1)}, u32[]{:S(2)}, u32[]{:S(2)}) collective-permute-start(bf16[2,16,768]{2,1,0:T(8,128)(2,1)S(1)} %pad_maximum_fusion.2), channel_id=1, source_target_pairs={{0,4},{2,6},{4,0},{6,2},{8,12},{10,14},{12,8},{14,10},{1,5},{3,7},... | collective-permute-start | bytes 147464 | tf_op jit(solution)/shard_map/ppermute | solution.py:678
  10.7 0.0 collective-permute-done.4.up_far_ref
  10.7 0.0 copy-done.2
  10.7 0.0 copy-done.3
  10.7 0.0 copy-done.6
  10.7 1.8 %shard_map.123 = (f32[3,128,768]{2,1,0:T(8,128)S(1)}, f32[2,128,1]{2,1,0:T(8,128)S(1)}, bf16[256,384]{1,0:T(8,128)(2,1)S(1)}, f32[2,128,384]{2,1,0:T(8,128)S(1)}) custom-call(bf16[1,128,768]{2,1,0:T(8,128)(2,1)S(1)} %copy-done.3, s32[1,128]{1,0:T(1,128)S(1)} %copy-done.6, f32[1,768]{1,0:T(1,128)S(1)} %broadcast_in_dim.3.weight_ref, ...), custom_call_target="tpu_custom_call" | custom-call | flops 1800000000 | bytes 7031250 | tf_op jit(solution)/shard_map/pallas_call | solution.py:362
  12.6 0.3 collective-permute-done.3.third_ref
  12.9 0.1 collective-permute-start.5
  13.0 0.0 copy-done.7
  13.0 1.9 %collective-permute-start.6 = (bf16[4,16,768]{2,1,0:T(8,128)(2,1)S(1)}, bf16[4,16,768]{2,1,0:T(8,128)(2,1)S(1)}, u32[]{:S(2)}, u32[]{:S(2)}) collective-permute-start(bf16[4,16,768]{2,1,0:T(8,128)(2,1)S(1)} %pad_maximum_fusion.1), channel_id=1, source_target_pairs={{0,2},{2,0},{4,6},{6,4},{8,10},{10,8},{12,14},{14,12},{1,3},{3,1},... | collective-permute-start | bytes 294920 | tf_op jit(solution)/shard_map/ppermute | solution.py:678
  14.9 1.5 %shard_map.124 = (f32[128,768]{1,0:T(8,128)S(1)}, f32[8,768]{1,0:T(8,128)S(1)}, f32[8,768]{1,0:T(8,128)S(1)}) custom-call(f32[4]{0:T(128)S(1)} %copy-done.7, f32[4]{0:T(128)S(1)} %negate_sqrt_fusion.scale_ref, bf16[1,128,768]{2,1,0:T(8,128)(2,1)S(1)} %copy-done.4, f32[1,128]{1,0:T(1,128)S(1)} %copy-done.8, f32[2,4,768]{2,1,0:T(4,128)S(1)} %copy-done.5, ...), custom_call_target="tpu_custom_call" | custom-call | flops 1600000000 | bytes 6250000 | tf_op jit(solution)/shard_map/pallas_call | solution.py:362
  16.4 0.0 collective-permute-done.5.reduced_far_ref
  16.4 1.9 %collective-permute-done.6.fourth_ref = bf16[4,16,768]{2,1,0:T(8,128)(2,1)S(1)} collective-permute-done((bf16[4,16,768]{2,1,0:T(8,128)(2,1)S(1)}, bf16[4,16,768]{2,1,0:T(8,128)(2,1)S(1)}, u32[]{:S(2)}, u32[]{:S(2)}) %collective-permute-start.6) | collective-permute-done | bytes 98336 | tf_op jit(solution)/shard_map/ppermute | solution.py:678
  18.3 2.1 %shard_map.125 = (f32[128,768]{1,0:T(8,128)S(1)}, bf16[288,384]{1,0:T(8,128)(2,1)S(1)}, f32[16,384]{1,0:T(8,128)S(1)}) custom-call(f32[4]{0:T(128)S(1)} %copy-done.7, f32[4]{0:T(128)S(1)} %negate_sqrt_fusion.scale_ref, bf16[1,16,768]{2,1,0:T(8,128)(2,1)S(1)} %shard_map.121.first_ref, bf16[1,16,768]{2,1,0:T(8,128)(2,1)S(1)} %collective-permute-done.second_ref, ...), custom_call_target="tpu_custom_call" | custom-call | flops 2100000000 | bytes 8203125 | tf_op jit(solution)/shard_map/pallas_call | solution.py:362
  20.5 0.1 collective-permute-start.7
  20.5 1.5 %collective-permute-done.7.mixed_far_ref = bf16[288,384]{1,0:T(8,128)(2,1)S(1)} collective-permute-done((bf16[288,384]{1,0:T(8,128)(2,1)S(1)}, bf16[288,384]{1,0:T(8,128)(2,1)S(1)}, u32[]{:S(2)}, u32[]{:S(2)}) %collective-permute-start.7) | collective-permute-done | bytes 221216 | tf_op jit(solution)/shard_map/ppermute | solution.py:678
  22.0 0.4 shard_map.126
  22.5 1.5 %collective-permute-start.8 = (bf16[208,384]{1,0:T(8,128)(2,1)S(1)}, bf16[208,384]{1,0:T(8,128)(2,1)S(1)}, u32[]{:S(2)}, u32[]{:S(2)}) collective-permute-start(bf16[208,384]{1,0:T(8,128)(2,1)S(1)} %get-tuple-element.56), channel_id=1, source_target_pairs={{0,3},{1,2},{2,1},{3,0},{4,7},{5,6},{6,5},{7,4},{8,11},{9,10},{10,... | collective-permute-start | bytes 479240 | tf_op jit(solution)/shard_map/ppermute | solution.py:683
  24.0 1.3 %shard_map.128 = bf16[1,128,768]{2,1,0:T(8,128)(2,1)} custom-call(f32[128,768]{1,0:T(8,128)S(1)} %get-tuple-element.59.gradient_ref, bf16[288,384]{1,0:T(8,128)(2,1)S(1)} %get-tuple-element.53.mixed_ref, f32[3,128,768]{2,1,0:T(8,128)S(1)} %get-tuple-element.44.stream_ref, f32[2,128,1]{2,1,0:T(8,128)S(1)} %get-tuple-element.51.inverse_ref, ...), custom_call_target="tpu_custom_call" | custom-call | flops 1300000000 | bytes 5078125 | tf_op jit(solution)/shard_map/pallas_call | solution.py:362
  25.3 3.3 %collective-permute-done.8.got_ref = bf16[208,384]{1,0:T(8,128)(2,1)S(1)} collective-permute-done((bf16[208,384]{1,0:T(8,128)(2,1)S(1)}, bf16[208,384]{1,0:T(8,128)(2,1)S(1)}, u32[]{:S(2)}, u32[]{:S(2)}) %collective-permute-start.8) | collective-permute-done | bytes 159776 | tf_op jit(solution)/shard_map/ppermute | solution.py:683
  28.7 1.6 %collective-permute-start.9 = (bf16[112,384]{1,0:T(8,128)(2,1)S(1)}, bf16[112,384]{1,0:T(8,128)(2,1)S(1)}, u32[]{:S(2)}, u32[]{:S(2)}) collective-permute-start(bf16[112,384]{1,0:T(8,128)(2,1)S(1)} %get-tuple-element.62), channel_id=1, source_target_pairs={{0,5},{1,4},{2,7},{3,6},{4,1},{5,0},{6,3},{7,2},{8,13},{9,12},{10,... | collective-permute-start | bytes 258056 | tf_op jit(solution)/shard_map/ppermute | solution.py:683
  30.3 3.0 %collective-permute-done.9.got_ref = bf16[112,384]{1,0:T(8,128)(2,1)S(1)} collective-permute-done((bf16[112,384]{1,0:T(8,128)(2,1)S(1)}, bf16[112,384]{1,0:T(8,128)(2,1)S(1)}, u32[]{:S(2)}, u32[]{:S(2)}) %collective-permute-start.9) | collective-permute-done | bytes 86048 | tf_op jit(solution)/shard_map/ppermute | solution.py:683
  33.3 2.6 %collective-permute-start.10 = (bf16[64,384]{1,0:T(8,128)(2,1)S(1)}, bf16[64,384]{1,0:T(8,128)(2,1)S(1)}, u32[]{:S(2)}, u32[]{:S(2)}) collective-permute-start(bf16[64,384]{1,0:T(8,128)(2,1)S(1)} %get-tuple-element.65), channel_id=1, source_target_pairs={{0,9},{1,8},{2,11},{3,10},{4,13},{5,12},{6,15},{7,14},{8,1},{9,0},... | collective-permute-start | bytes 147464 | tf_op jit(solution)/shard_map/ppermute | solution.py:683
  35.9 2.0 %collective-permute-done.10.got_ref = bf16[64,384]{1,0:T(8,128)(2,1)S(1)} collective-permute-done((bf16[64,384]{1,0:T(8,128)(2,1)S(1)}, bf16[64,384]{1,0:T(8,128)(2,1)S(1)}, u32[]{:S(2)}, u32[]{:S(2)}) %collective-permute-start.10) | collective-permute-done | bytes 49184 | tf_op jit(solution)/shard_map/ppermute | solution.py:683
  37.9 1.8 %collective-permute-start.12 = (bf16[48,384]{1,0:T(8,128)(2,1)S(1)}, bf16[48,384]{1,0:T(8,128)(2,1)S(1)}, u32[]{:S(2)}, u32[]{:S(2)}) collective-permute-start(bf16[48,384]{1,0:T(8,128)(2,1)S(1)} %get-tuple-element.67), channel_id=1, source_target_pairs={{6,0},{7,1},{0,2},{1,3},{2,4},{3,5},{4,6},{5,7},{14,8},{15,9},{8,1... | collective-permute-start | bytes 110600 | tf_op jit(solution)/shard_map/ppermute | solution.py:787
  39.7 1.5 %collective-permute-start.11 = (bf16[48,384]{1,0:T(8,128)(2,1)S(1)}, bf16[48,384]{1,0:T(8,128)(2,1)S(1)}, u32[]{:S(2)}, u32[]{:S(2)}) collective-permute-start(bf16[48,384]{1,0:T(8,128)(2,1)S(1)} %get-tuple-element.67), channel_id=1, source_target_pairs={{3,0},{4,1},{5,2},{6,3},{7,4},{0,5},{1,6},{2,7},{11,8},{12,9},{13,... | collective-permute-start | bytes 110600 | tf_op jit(solution)/shard_map/ppermute | solution.py:787
  41.2 0.7 %shard_map.131 = f32[8,48]{1,0:T(8,128)} custom-call(bf16[64,384]{1,0:T(8,128)(2,1)S(1)} %collective-permute-done.10.got_ref, f32[16,384]{1,0:T(8,128)S(1)} %get-tuple-element.68.partial_ref), custom_call_target="tpu_custom_call" | custom-call | tf_op jit(solution)/shard_map/pallas_call | solution.py:362
  41.9 1.4 %collective-permute-done.12 = bf16[48,384]{1,0:T(8,128)(2,1)S(1)} collective-permute-done((bf16[48,384]{1,0:T(8,128)(2,1)S(1)}, bf16[48,384]{1,0:T(8,128)(2,1)S(1)}, u32[]{:S(2)}, u32[]{:S(2)}) %collective-permute-start.12) | collective-permute-done | bytes 36896 | tf_op jit(solution)/shard_map/ppermute | solution.py:787
  43.3 0.2 collective-permute-done.11
  43.5 0.7 %pad_maximum_fusion = f32[144,384]{1,0:T(8,128)} fusion(f32[48,384]{1,0:T(8,128)S(1)} %convert_element_type.7, f32[48,384]{1,0:T(8,128)S(1)} %convert_element_type.6, f32[48,384]{1,0:T(8,128)S(1)} %get-tuple-element.66), kind=kLoop, calls=%fused_computation | loop fusion | flops 110592 | bytes 442368 | tf_op jit(solution)/shard_map/concatenate | solution.py:795
  (16 shorter events, 0.1 us)
Async XLA Ops:
  0.6 7.8 %collective-permute-start.2 = (bf16[2,3,192,384]{3,2,1,0:T(8,128)(2,1)}, bf16[2,3,192,384]{3,2,1,0:T(8,128)(2,1)S(1)}, u32[]{:S(2)}, u32[]{:S(2)}) collective-permute-start(bf16[2,3,192,384]{3,2,1,0:T(8,128)(2,1)} %bitcast.2), channel_id=1, source_target_pairs={{0,1},{1,0},{2,3},{3,2},{4,5},{5,4},{6,7},{7,6},{8,9},{9,8},{10,11... | collective-permute-start | bytes 2654216 | tf_op jit(solution)/shard_map/ppermute | solution.py:678
  1.1 5.4 %copy-start.9 = (f32[768]{0:T(1024)S(1)}, f32[768]{0:T(1024)}, u32[]{:S(2)}) copy-start(f32[768]{0:T(1024)} %param.13) | copy-start | bytes 9220
  1.2 7.3 %copy-start = (bf16[2,3,384,192]{2,3,1,0:T(8,128)(2,1)S(1)}, bf16[2,3,384,192]{2,3,1,0:T(8,128)(2,1)}, u32[]{:S(2)}) copy-start(bf16[2,3,384,192]{2,3,1,0:T(8,128)(2,1)} %param.15) | copy-start | bytes 2654212
  1.2 7.3 %copy-start.1 = (bf16[2,768,192]{1,2,0:T(8,128)(2,1)S(1)}, bf16[2,768,192]{1,2,0:T(8,128)(2,1)}, u32[]{:S(2)}) copy-start(bf16[2,768,192]{1,2,0:T(8,128)(2,1)} %param.14) | copy-start | bytes 1769476
  1.2 7.2 %collective-permute-start.1 = (bf16[2,192,768]{2,1,0:T(8,128)(2,1)}, bf16[2,192,768]{2,1,0:T(8,128)(2,1)S(1)}, u32[]{:S(2)}, u32[]{:S(2)}) collective-permute-start(bf16[2,192,768]{2,1,0:T(8,128)(2,1)} %bitcast.4), channel_id=1, source_target_pairs={{0,1},{1,0},{2,3},{3,2},{4,5},{5,4},{6,7},{7,6},{8,9},{9,8},{10,11... | collective-permute-start | bytes 1769480 | tf_op jit(solution)/shard_map/ppermute | solution.py:678
  1.3 9.5 %collective-permute-start.4 = (bf16[2,384,384]{2,1,0:T(8,128)(2,1)}, bf16[2,384,384]{2,1,0:T(8,128)(2,1)S(1)}, u32[]{:S(2)}, u32[]{:S(2)}) collective-permute-start(bf16[2,384,384]{2,1,0:T(8,128)(2,1)} %up_ref.3), channel_id=1, source_target_pairs={{0,1},{1,0},{2,3},{3,2},{4,5},{5,4},{6,7},{7,6},{8,9},{9,8},{10,11... | collective-permute-start | bytes 1769480 | tf_op jit(solution)/shard_map/ppermute | solution.py:678
  2.8 5.6 %collective-permute-start = (bf16[1,16,768]{2,1,0:T(8,128)(2,1)S(1)}, bf16[1,16,768]{2,1,0:T(8,128)(2,1)S(1)}, u32[]{:S(2)}, u32[]{:S(2)}) collective-permute-start(bf16[1,16,768]{2,1,0:T(8,128)(2,1)S(1)} %shard_map.121.first_ref), channel_id=1, source_target_pairs={{0,8},{2,10},{4,12},{6,14},{8,0},{10,2},{12,4},{14,6},{1,9},{3,11}... | collective-permute-start | bytes 73736 | tf_op jit(solution)/shard_map/ppermute | solution.py:678
  8.4 2.4 %copy-start.2 = (bf16[2,384,384]{2,1,0:T(8,128)(2,1)S(1)}, bf16[2,384,384]{2,1,0:T(8,128)(2,1)}, u32[]{:S(2)}) copy-start(bf16[2,384,384]{2,1,0:T(8,128)(2,1)} %up_ref.3) | copy-start | bytes 1769476
  8.4 2.4 %copy-start.3 = (bf16[1,128,768]{2,1,0:T(8,128)(2,1)S(1)}, bf16[1,128,768]{2,1,0:T(8,128)(2,1)}, u32[]{:S(2)}) copy-start(bf16[1,128,768]{2,1,0:T(8,128)(2,1)} %feature_ref.1) | copy-start | bytes 589828
  8.4 2.3 %copy-start.6 = (s32[1,128]{1,0:T(1,128)S(1)}, s32[1,128]{1,0:T(1,128)}, u32[]{:S(2)}) copy-start(s32[1,128]{1,0:T(1,128)} %count_ref.1) | copy-start | bytes 1540
  8.7 4.3 %copy-start.7 = (f32[4]{0:T(128)S(1)}, f32[4]{0:T(128)}, u32[]{:S(2)}) copy-start(f32[4]{0:T(128)} %decay_ref.3) | copy-start | bytes 52
  8.7 6.2 %copy-start.4 = (bf16[1,128,768]{2,1,0:T(8,128)(2,1)S(1)}, bf16[1,128,768]{2,1,0:T(8,128)(2,1)}, u32[]{:S(2)}) copy-start(bf16[1,128,768]{2,1,0:T(8,128)(2,1)} %cot_ref.1) | copy-start | bytes 589828
  8.7 6.2 %copy-start.5 = (f32[2,4,768]{2,1,0:T(4,128)S(1)}, f32[2,4,768]{2,1,0:T(4,128)}, u32[]{:S(2)}) copy-start(f32[2,4,768]{2,1,0:T(4,128)} %mode_ref.3) | copy-start | bytes 73732
  8.7 6.2 %copy-start.8 = (f32[1,128]{1,0:T(1,128)S(1)}, f32[1,128]{1,0:T(1,128)}, u32[]{:S(2)}) copy-start(f32[1,128]{1,0:T(1,128)} %keep_ref.3) | copy-start | bytes 1540
  8.7 4.2 %collective-permute-start.3 = (bf16[2,16,768]{2,1,0:T(8,128)(2,1)S(1)}, bf16[2,16,768]{2,1,0:T(8,128)(2,1)S(1)}, u32[]{:S(2)}, u32[]{:S(2)}) collective-permute-start(bf16[2,16,768]{2,1,0:T(8,128)(2,1)S(1)} %pad_maximum_fusion.2), channel_id=1, source_target_pairs={{0,4},{2,6},{4,0},{6,2},{8,12},{10,14},{12,8},{14,10},{1,5},{3,7},... | collective-permute-start | bytes 147464 | tf_op jit(solution)/shard_map/ppermute | solution.py:678
  12.9 3.5 %collective-permute-start.5 = (bf16[256,384]{1,0:T(8,128)(2,1)S(1)}, bf16[256,384]{1,0:T(8,128)(2,1)S(1)}, u32[]{:S(2)}, u32[]{:S(2)}) collective-permute-start(bf16[256,384]{1,0:T(8,128)(2,1)S(1)} %get-tuple-element.43.reduced_ref), channel_id=1, source_target_pairs={{0,1},{1,0},{2,3},{3,2},{4,5},{5,4},{6,7},{7,6},{8,9},{9,8},{10,11... | collective-permute-start | bytes 589832 | tf_op jit(solution)/shard_map/ppermute | solution.py:678
  13.0 5.3 %collective-permute-start.6 = (bf16[4,16,768]{2,1,0:T(8,128)(2,1)S(1)}, bf16[4,16,768]{2,1,0:T(8,128)(2,1)S(1)}, u32[]{:S(2)}, u32[]{:S(2)}) collective-permute-start(bf16[4,16,768]{2,1,0:T(8,128)(2,1)S(1)} %pad_maximum_fusion.1), channel_id=1, source_target_pairs={{0,2},{2,0},{4,6},{6,4},{8,10},{10,8},{12,14},{14,12},{1,3},{3,1},... | collective-permute-start | bytes 294920 | tf_op jit(solution)/shard_map/ppermute | solution.py:678
  20.5 1.5 %collective-permute-start.7 = (bf16[288,384]{1,0:T(8,128)(2,1)S(1)}, bf16[288,384]{1,0:T(8,128)(2,1)S(1)}, u32[]{:S(2)}, u32[]{:S(2)}) collective-permute-start(bf16[288,384]{1,0:T(8,128)(2,1)S(1)} %get-tuple-element.53.mixed_ref), channel_id=1, source_target_pairs={{0,1},{1,0},{2,3},{3,2},{4,5},{5,4},{6,7},{7,6},{8,9},{9,8},{10,11... | collective-permute-start | bytes 663560 | tf_op jit(solution)/shard_map/ppermute | solution.py:678
  22.5 6.2 %collective-permute-start.8 = (bf16[208,384]{1,0:T(8,128)(2,1)S(1)}, bf16[208,384]{1,0:T(8,128)(2,1)S(1)}, u32[]{:S(2)}, u32[]{:S(2)}) collective-permute-start(bf16[208,384]{1,0:T(8,128)(2,1)S(1)} %get-tuple-element.56), channel_id=1, source_target_pairs={{0,3},{1,2},{2,1},{3,0},{4,7},{5,6},{6,5},{7,4},{8,11},{9,10},{10,... | collective-permute-start | bytes 479240 | tf_op jit(solution)/shard_map/ppermute | solution.py:683
  28.7 4.6 %collective-permute-start.9 = (bf16[112,384]{1,0:T(8,128)(2,1)S(1)}, bf16[112,384]{1,0:T(8,128)(2,1)S(1)}, u32[]{:S(2)}, u32[]{:S(2)}) collective-permute-start(bf16[112,384]{1,0:T(8,128)(2,1)S(1)} %get-tuple-element.62), channel_id=1, source_target_pairs={{0,5},{1,4},{2,7},{3,6},{4,1},{5,0},{6,3},{7,2},{8,13},{9,12},{10,... | collective-permute-start | bytes 258056 | tf_op jit(solution)/shard_map/ppermute | solution.py:683
  33.3 4.6 %collective-permute-start.10 = (bf16[64,384]{1,0:T(8,128)(2,1)S(1)}, bf16[64,384]{1,0:T(8,128)(2,1)S(1)}, u32[]{:S(2)}, u32[]{:S(2)}) collective-permute-start(bf16[64,384]{1,0:T(8,128)(2,1)S(1)} %get-tuple-element.65), channel_id=1, source_target_pairs={{0,9},{1,8},{2,11},{3,10},{4,13},{5,12},{6,15},{7,14},{8,1},{9,0},... | collective-permute-start | bytes 147464 | tf_op jit(solution)/shard_map/ppermute | solution.py:683
  37.9 5.4 %collective-permute-start.12 = (bf16[48,384]{1,0:T(8,128)(2,1)S(1)}, bf16[48,384]{1,0:T(8,128)(2,1)S(1)}, u32[]{:S(2)}, u32[]{:S(2)}) collective-permute-start(bf16[48,384]{1,0:T(8,128)(2,1)S(1)} %get-tuple-element.67), channel_id=1, source_target_pairs={{6,0},{7,1},{0,2},{1,3},{2,4},{3,5},{4,6},{5,7},{14,8},{15,9},{8,1... | collective-permute-start | bytes 110600 | tf_op jit(solution)/shard_map/ppermute | solution.py:787
  39.7 3.8 %collective-permute-start.11 = (bf16[48,384]{1,0:T(8,128)(2,1)S(1)}, bf16[48,384]{1,0:T(8,128)(2,1)S(1)}, u32[]{:S(2)}, u32[]{:S(2)}) collective-permute-start(bf16[48,384]{1,0:T(8,128)(2,1)S(1)} %get-tuple-element.67), channel_id=1, source_target_pairs={{3,0},{4,1},{5,2},{6,3},{7,4},{0,5},{1,6},{2,7},{11,8},{12,9},{13,... | collective-permute-start | bytes 110600 | tf_op jit(solution)/shard_map/ppermute | solution.py:787

commit v3 on v2

--- a/solution.py
+++ b/solution.py
@@ -426,16 +426,16 @@
     high = weights.astype(BF16).astype(F32)
     both = jnp.concatenate([high, weights - high], axis=0).astype(BF16)
     width = cot_ref.shape[-1]
-    first = jnp.broadcast_to(total, (8, width))
+    first = jnp.broadcast_to(total, (8, 128))
     one = first.astype(BF16).astype(F32)
     two = (first - one).astype(BF16).astype(F32)
     three = first - one - two
-    row = iota2((8, width), 0)
+    row = iota2((8, 128), 0)
     extra = jnp.where(row == 0, one, jnp.where(row == 1, two, jnp.where(row == 2, three, 0.0)))
+    pay_ref[0, :, width:] = extra.astype(BF16)
     copies[2].wait()
     states = dot(both, cot_ref[0])
-    states = states[0:8] + states[8:16]
-    pay_ref[0] = jnp.concatenate([states, extra], axis=0).astype(BF16)
+    pay_ref[0, :, :width] = (states[0:8] + states[8:16]).astype(BF16)
 
 
 def assemble_body(down_ref, down_far_ref, tap_ref, tap_far_ref, down_out, tap_out):
@@ -535,7 +535,7 @@
     pieces = []
     for ref in (first_ref, second_ref, third_ref, fourth_ref):
         pieces = pieces + [ref[index].astype(F32) for index in range(ref.shape[0])]
-    totals = [jnp.sum(piece[8:16, 0:128], axis=0, keepdims=True) for piece in pieces]
+    totals = [jnp.sum(piece[:, width:], axis=0, keepdims=True) for piece in pieces]
     row8 = iota2((8, 128), 0)
     decay8 = jnp.zeros((8, 128), F32)
     gain8 = jnp.zeros((8, 128), F32)
@@ -560,7 +560,7 @@
         fore = jnp.broadcast_to(fore, (8, 128)) - (ahead[index] * rows).astype(F32) * decay8
         back = jnp.broadcast_to(back, (8, 128)) - (after[index] * rows).astype(F32) * decay8
         share = jnp.exp(jnp.where(row8 < M, back, fore)) / loop
-        entering = entering + share[:, 0:1] * pieces[index][0:8, :]
+        entering = entering + share[:, 0:1] * pieces[index][:, :width]
     whole = gain8 * (mark_ref[...] + entering * reach_ref[...])
     partial = jnp.concatenate([whole[:, :wide], whole[:, wide:]], axis=0)
     partial_ref[...] = partial
@@ -652,8 +652,13 @@
     kept_out[...] = kept_ref[keep, :] + got_ref[keep, :].astype(F32)
     send_out[0:rows, :] = (kept_ref[send, :] + got_ref[send, :].astype(F32)).astype(BF16)
     partial = partial_ref[...] + got_ref[2 * rows : 2 * rows + 16, :].astype(F32)
-    partial_out[...] = partial
-    send_out[rows : rows + 16, :] = partial.astype(BF16)
+    if stage == 1:
+        partial_out[...] = partial
+        send_out[rows : rows + 16, :] = partial.astype(BF16)
+    else:
+        last = position_bit(2)
+        partial_out[...] = jnp.where(last == 0, partial[0:8], partial[8:16])
+        send_out[rows : rows + 8, :] = jnp.where(last == 0, partial[8:16], partial[0:8]).astype(BF16)
 
 
 def finish_body(scale, kept_ref, got_ref, block_out, send_out):
@@ -663,14 +668,12 @@
     send_out[...] = block.astype(BF16)
 
 
-def modes_body(scale, got_ref, partial_ref, mode_out, full_ref):
-    rows = got_ref.shape[0] - 16
-    full_ref[...] = (partial_ref[...] + got_ref[rows : rows + 16, :].astype(F32)) * scale
-    number = 2 * lax.axis_index("seq") + lax.axis_index("dp")
-    span = full_ref.shape[1]
-    top = pl.multiple_of(8 * (number // 8), 8)
-    shift = lax.rem(span - BLOCK * lax.rem(number, 8), span)
-    mode_out[...] = pltpu.roll(full_ref[pl.ds(top, 8), :], shift, 1)[:, 0:BLOCK]
+def modes_body(scale, got_ref, partial_ref, mode_out):
+    rows = got_ref.shape[0] - 8
+    full = (partial_ref[...] + got_ref[rows : rows + 8, :].astype(F32)) * scale
+    number = lax.rem(2 * lax.axis_index("seq") + lax.axis_index("dp"), 8)
+    span = full.shape[1]
+    mode_out[...] = pltpu.roll(full, lax.rem(span - BLOCK * number, span), 1)[:, 0:BLOCK]
 
 
 def swap(value, axis, mask):
@@ -696,7 +699,7 @@
         prepare_body,
         tuple(pltpu.with_memory_space_constraint(value, HBM) for value in (cotangent, keep_share, decay_rate)),
         (HBM,) * 3,
-        (((1, 16, width), BF16),),
+        (((1, 8, width + 128), BF16),),
         (
             pltpu.VMEM(cotangent.shape, BF16),
             pltpu.VMEM(keep_share.shape, F32),
@@ -764,11 +767,12 @@
     got = cross(send, 1)
     for stage in (1, 2):
         kept_rows = kept.shape[0] // 2
+        mode_rows = (16, 8)[stage - 1]
         kept, send, partial = call(
             functools.partial(join_body, stage),
             (kept, got, partial),
             (VMEM,) * 3,
-            (((kept_rows, B), F32), ((kept_rows + 16, B), BF16), ((16, B), F32)),
+            (((kept_rows, B), F32), ((kept_rows + mode_rows, B), BF16), ((mode_rows, B), F32)),
         )
         if stage == 1:
             send, grad = lax.optimization_barrier((send, grad))
@@ -786,11 +790,7 @@
         pairs = [(8 * layer + (j + step) % 8, 8 * layer + j) for layer in range(LAYERS) for j in range(8)]
         parts.append(lax.ppermute(narrow, ("seq", "dp"), pairs).astype(F32))
     (mode_sum,) = call(
-        functools.partial(modes_body, report),
-        (got, partial),
-        (VMEM,) * 2,
-        (((8, BLOCK), F32),),
-        (pltpu.VMEM((16, B), F32),),
+        functools.partial(modes_body, report), (got, partial), (VMEM,) * 2, (((8, BLOCK), F32),)
     )
     return grad, jnp.concatenate(parts, axis=0), mode_sum
 

time: 44.7 us -> 43.3 us (0.969)
  waiting for transfers between devices: 15.4 us -> 14.3 us
    ppermute x8, waiting for transfers between devices: 5.54 us -> 4.34 us  [swap(): lax.ppermute(value, axis, [(source, source ^ mask) for source in range(co...]
  transfers between devices with their start and end apart: 13 -> 13, of which waited for: 9 -> 9; matrix products, arithmetic and copies ran while one was open for 0% -> 0% of each run, Pallas kernels for 15% -> 16%
where the time goes in v3:
time: 43.3 us; the launch traced here: 42.8 us
  starting transfers between devices  17.6 us (41%)
  waiting for transfers between devices  14.3 us (33%)
  Pallas kernels  9.3 us (21%)
  between operations  0.83 us (2%)
  other arithmetic  0.74 us (2%)
    pallas_call x11, Pallas kernels, call(): pl.pallas_call(body, out_shape=[jax.ShapeDtypeStruct(shape, dtype) for sh...  9.3 us
    ppermute x8, starting transfers between devices, swap(): lax.ppermute(value, axis, [(source, source ^ mask) for source in range(co...  8.78 us
    ppermute x3, waiting for transfers between devices, cross(): lax.ppermute(value, ('seq', 'dp'), [(source, source ^ 2 * mask + 1) for s...  8.25 us
    ppermute x3, starting transfers between devices, cross(): lax.ppermute(value, ('seq', 'dp'), [(source, source ^ 2 * mask + 1) for s...  5.75 us
    ppermute x8, waiting for transfers between devices, swap(): lax.ppermute(value, axis, [(source, source ^ mask) for source in range(co...  4.34 us
    ppermute x2, starting transfers between devices, wrapped_device(): parts.append(lax.ppermute(narrow, ('seq', 'dp'), pairs).astype(F32))  3.08 us
    ppermute x2, waiting for transfers between devices, wrapped_device(): parts.append(lax.ppermute(narrow, ('seq', 'dp'), pairs).astype(F32))  1.7 us
  transfers between devices with their start and end apart: 13, of which 9 were waited for; matrix products, arithmetic and copies ran while one was open for 0% of the time, Pallas kernels for 16%

profile of v3, /device:TPU:0, one launch (start us, length us, event | category | flops | bytes accessed | tf_op | source)
XLA Modules:
  0.0 42.8 jit_solution(12615518473180959502)
XLA Ops:
  0.6 0.5 %collective-permute-start.2 = (bf16[2,3,192,384]{3,2,1,0:T(8,128)(2,1)}, bf16[2,3,192,384]{3,2,1,0:T(8,128)(2,1)S(1)}, u32[]{:S(2)}, u32[]{:S(2)}) collective-permute-start(bf16[2,3,192,384]{3,2,1,0:T(8,128)(2,1)} %bitcast.2), channel_id=1, source_target_pairs={{0,1},{1,0},{2,3},{3,2},{4,5},{5,4},{6,7},{7,6},{8,9},{9,8},{10,11... | collective-permute-start | bytes 2654216 | tf_op jit(solution)/shard_map/ppermute | solution.py:681
  1.2 0.1 collective-permute-start.1
  1.3 0.4 collective-permute-start.4
  1.7 1.1 %shard_map.121.first_ref = bf16[1,8,896]{2,1,0:T(8,128)(2,1)S(1)} custom-call(bf16[1,128,768]{2,1,0:T(8,128)(2,1)} %cot_ref.1, f32[1,128]{1,0:T(1,128)} %keep_ref.3, f32[4]{0:T(128)} %decay_ref.3), custom_call_target="tpu_custom_call" | custom-call | flops 1300000000 | bytes 5078125 | tf_op jit(solution)/shard_map/pallas_call | solution.py:362
  2.8 3.8 %collective-permute-start = (bf16[1,8,896]{2,1,0:T(8,128)(2,1)S(1)}, bf16[1,8,896]{2,1,0:T(8,128)(2,1)S(1)}, u32[]{:S(2)}, u32[]{:S(2)}) collective-permute-start(bf16[1,8,896]{2,1,0:T(8,128)(2,1)S(1)} %shard_map.121.first_ref), channel_id=1, source_target_pairs={{0,8},{2,10},{4,12},{6,14},{8,0},{10,2},{12,4},{14,6},{1,9},{3,11}... | collective-permute-start | bytes 43016 | tf_op jit(solution)/shard_map/ppermute | solution.py:681
  6.5 0.0 copy-done.9
  6.6 1.7 %collective-permute-done.second_ref = bf16[1,8,896]{2,1,0:T(8,128)(2,1)S(1)} collective-permute-done((bf16[1,8,896]{2,1,0:T(8,128)(2,1)S(1)}, bf16[1,8,896]{2,1,0:T(8,128)(2,1)S(1)}, u32[]{:S(2)}, u32[]{:S(2)}) %collective-permute-start) | collective-permute-done | bytes 14368 | tf_op jit(solution)/shard_map/ppermute | solution.py:681
  8.3 0.0 copy-start.2
  8.3 0.0 copy-start.3
  8.3 0.0 copy-start.6
  8.3 0.0 collective-permute-done.1.down_far_ref
  8.3 0.0 collective-permute-done.2.tap_far_ref
  8.3 0.0 copy-done
  8.3 0.0 copy-done.1
  8.3 0.3 shard_map.122
  8.6 0.0 copy-start.7
  8.6 0.0 copy-start.4
  8.6 0.0 copy-start.5
  8.6 0.0 copy-start.8
  8.6 2.0 %collective-permute-start.3 = (bf16[2,8,896]{2,1,0:T(8,128)(2,1)S(1)}, bf16[2,8,896]{2,1,0:T(8,128)(2,1)S(1)}, u32[]{:S(2)}, u32[]{:S(2)}) collective-permute-start(bf16[2,8,896]{2,1,0:T(8,128)(2,1)S(1)} %pad_maximum_fusion.2), channel_id=1, source_target_pairs={{0,4},{2,6},{4,0},{6,2},{8,12},{10,14},{12,8},{14,10},{1,5},{3,7},... | collective-permute-start | bytes 86024 | tf_op jit(solution)/shard_map/ppermute | solution.py:681
  10.6 0.0 collective-permute-done.4.up_far_ref
  10.6 0.0 copy-done.2
  10.6 0.0 copy-done.3
  10.6 1.8 %shard_map.123 = (f32[3,128,768]{2,1,0:T(8,128)S(1)}, f32[2,128,1]{2,1,0:T(8,128)S(1)}, bf16[256,384]{1,0:T(8,128)(2,1)S(1)}, f32[2,128,384]{2,1,0:T(8,128)S(1)}) custom-call(bf16[1,128,768]{2,1,0:T(8,128)(2,1)S(1)} %copy-done.3, s32[1,128]{1,0:T(1,128)S(1)} %copy-done.6, f32[1,768]{1,0:T(1,128)S(1)} %broadcast_in_dim.3.weight_ref, ...), custom_call_target="tpu_custom_call" | custom-call | flops 1800000000 | bytes 7031250 | tf_op jit(solution)/shard_map/pallas_call | solution.py:362
  12.5 0.1 collective-permute-done.3.third_ref
  12.6 0.1 collective-permute-start.5
  12.7 1.9 %collective-permute-start.6 = (bf16[4,8,896]{2,1,0:T(8,128)(2,1)S(1)}, bf16[4,8,896]{2,1,0:T(8,128)(2,1)S(1)}, u32[]{:S(2)}, u32[]{:S(2)}) collective-permute-start(bf16[4,8,896]{2,1,0:T(8,128)(2,1)S(1)} %pad_maximum_fusion.1), channel_id=1, source_target_pairs={{0,2},{2,0},{4,6},{6,4},{8,10},{10,8},{12,14},{14,12},{1,3},{3,1},... | collective-permute-start | bytes 172040 | tf_op jit(solution)/shard_map/ppermute | solution.py:681
  14.6 0.0 copy-done.5
  14.6 1.5 %shard_map.124 = (f32[128,768]{1,0:T(8,128)S(1)}, f32[8,768]{1,0:T(8,128)S(1)}, f32[8,768]{1,0:T(8,128)S(1)}) custom-call(f32[4]{0:T(128)S(1)} %copy-done.7, f32[4]{0:T(128)S(1)} %negate_sqrt_fusion.scale_ref, bf16[1,128,768]{2,1,0:T(8,128)(2,1)S(1)} %copy-done.4, f32[1,128]{1,0:T(1,128)S(1)} %copy-done.8, f32[2,4,768]{2,1,0:T(4,128)S(1)} %copy-done.5, ...), custom_call_target="tpu_custom_call" | custom-call | flops 1600000000 | bytes 6250000 | tf_op jit(solution)/shard_map/pallas_call | solution.py:362
  16.1 0.0 collective-permute-done.5.reduced_far_ref
  16.1 1.0 %collective-permute-done.6.fourth_ref = bf16[4,8,896]{2,1,0:T(8,128)(2,1)S(1)} collective-permute-done((bf16[4,8,896]{2,1,0:T(8,128)(2,1)S(1)}, bf16[4,8,896]{2,1,0:T(8,128)(2,1)S(1)}, u32[]{:S(2)}, u32[]{:S(2)}) %collective-permute-start.6) | collective-permute-done | bytes 57376 | tf_op jit(solution)/shard_map/ppermute | solution.py:681
  17.1 2.1 %shard_map.125 = (f32[128,768]{1,0:T(8,128)S(1)}, bf16[288,384]{1,0:T(8,128)(2,1)S(1)}, f32[16,384]{1,0:T(8,128)S(1)}) custom-call(f32[4]{0:T(128)S(1)} %copy-done.7, f32[4]{0:T(128)S(1)} %negate_sqrt_fusion.scale_ref, bf16[1,8,896]{2,1,0:T(8,128)(2,1)S(1)} %shard_map.121.first_ref, bf16[1,8,896]{2,1,0:T(8,128)(2,1)S(1)} %collective-permute-done.second_ref, ...), custom_call_target="tpu_custom_call" | custom-call | flops 2100000000 | bytes 8203125 | tf_op jit(solution)/shard_map/pallas_call | solution.py:362
  19.3 0.1 collective-permute-start.7
  19.4 1.5 %collective-permute-done.7.mixed_far_ref = bf16[288,384]{1,0:T(8,128)(2,1)S(1)} collective-permute-done((bf16[288,384]{1,0:T(8,128)(2,1)S(1)}, bf16[288,384]{1,0:T(8,128)(2,1)S(1)}, u32[]{:S(2)}, u32[]{:S(2)}) %collective-permute-start.7) | collective-permute-done | bytes 221216 | tf_op jit(solution)/shard_map/ppermute | solution.py:681
  20.8 0.4 %shard_map.126 = (f32[192,384]{1,0:T(8,128)S(1)}, bf16[208,384]{1,0:T(8,128)(2,1)S(1)}, f32[16,384]{1,0:T(8,128)S(1)}) custom-call(bf16[256,384]{1,0:T(8,128)(2,1)S(1)} %get-tuple-element.43.reduced_ref, bf16[256,384]{1,0:T(8,128)(2,1)S(1)} %collective-permute-done.5.reduced_far_ref, bf16[288,384]{1,0:T(8,128)(2,1)S(1)} %get-tuple-element.53.mixed_ref, ...), custom_call_target="tpu_custom_call" | custom-call | flops 500000000 | bytes 1953125 | tf_op jit(solution)/shard_map/pallas_call | solution.py:362
  21.3 1.5 %collective-permute-start.8 = (bf16[208,384]{1,0:T(8,128)(2,1)S(1)}, bf16[208,384]{1,0:T(8,128)(2,1)S(1)}, u32[]{:S(2)}, u32[]{:S(2)}) collective-permute-start(bf16[208,384]{1,0:T(8,128)(2,1)S(1)} %get-tuple-element.56), channel_id=1, source_target_pairs={{0,3},{1,2},{2,1},{3,0},{4,7},{5,6},{6,5},{7,4},{8,11},{9,10},{10,... | collective-permute-start | bytes 479240 | tf_op jit(solution)/shard_map/ppermute | solution.py:686
  22.8 1.3 %shard_map.128 = bf16[1,128,768]{2,1,0:T(8,128)(2,1)} custom-call(f32[128,768]{1,0:T(8,128)S(1)} %get-tuple-element.59.gradient_ref, bf16[288,384]{1,0:T(8,128)(2,1)S(1)} %get-tuple-element.53.mixed_ref, f32[3,128,768]{2,1,0:T(8,128)S(1)} %get-tuple-element.44.stream_ref, f32[2,128,1]{2,1,0:T(8,128)S(1)} %get-tuple-element.51.inverse_ref, ...), custom_call_target="tpu_custom_call" | custom-call | flops 1300000000 | bytes 5078125 | tf_op jit(solution)/shard_map/pallas_call | solution.py:362
  24.1 3.3 %collective-permute-done.8.got_ref = bf16[208,384]{1,0:T(8,128)(2,1)S(1)} collective-permute-done((bf16[208,384]{1,0:T(8,128)(2,1)S(1)}, bf16[208,384]{1,0:T(8,128)(2,1)S(1)}, u32[]{:S(2)}, u32[]{:S(2)}) %collective-permute-start.8) | collective-permute-done | bytes 159776 | tf_op jit(solution)/shard_map/ppermute | solution.py:686
  27.5 1.6 %collective-permute-start.9 = (bf16[112,384]{1,0:T(8,128)(2,1)S(1)}, bf16[112,384]{1,0:T(8,128)(2,1)S(1)}, u32[]{:S(2)}, u32[]{:S(2)}) collective-permute-start(bf16[112,384]{1,0:T(8,128)(2,1)S(1)} %get-tuple-element.62), channel_id=1, source_target_pairs={{0,5},{1,4},{2,7},{3,6},{4,1},{5,0},{6,3},{7,2},{8,13},{9,12},{10,... | collective-permute-start | bytes 258056 | tf_op jit(solution)/shard_map/ppermute | solution.py:686
  29.1 3.0 %collective-permute-done.9.got_ref = bf16[112,384]{1,0:T(8,128)(2,1)S(1)} collective-permute-done((bf16[112,384]{1,0:T(8,128)(2,1)S(1)}, bf16[112,384]{1,0:T(8,128)(2,1)S(1)}, u32[]{:S(2)}, u32[]{:S(2)}) %collective-permute-start.9) | collective-permute-done | bytes 86048 | tf_op jit(solution)/shard_map/ppermute | solution.py:686
  32.1 2.6 %collective-permute-start.10 = (bf16[56,384]{1,0:T(8,128)(2,1)S(1)}, bf16[56,384]{1,0:T(8,128)(2,1)S(1)}, u32[]{:S(2)}, u32[]{:S(2)}) collective-permute-start(bf16[56,384]{1,0:T(8,128)(2,1)S(1)} %get-tuple-element.65), channel_id=1, source_target_pairs={{0,9},{1,8},{2,11},{3,10},{4,13},{5,12},{6,15},{7,14},{8,1},{9,0},... | collective-permute-start | bytes 129032 | tf_op jit(solution)/shard_map/ppermute | solution.py:686
  34.7 1.9 %collective-permute-done.10.got_ref = bf16[56,384]{1,0:T(8,128)(2,1)S(1)} collective-permute-done((bf16[56,384]{1,0:T(8,128)(2,1)S(1)}, bf16[56,384]{1,0:T(8,128)(2,1)S(1)}, u32[]{:S(2)}, u32[]{:S(2)}) %collective-permute-start.10) | collective-permute-done | bytes 43040 | tf_op jit(solution)/shard_map/ppermute | solution.py:686
  36.7 1.8 %collective-permute-start.12 = (bf16[48,384]{1,0:T(8,128)(2,1)S(1)}, bf16[48,384]{1,0:T(8,128)(2,1)S(1)}, u32[]{:S(2)}, u32[]{:S(2)}) collective-permute-start(bf16[48,384]{1,0:T(8,128)(2,1)S(1)} %get-tuple-element.67), channel_id=1, source_target_pairs={{6,0},{7,1},{0,2},{1,3},{2,4},{3,5},{4,6},{5,7},{14,8},{15,9},{8,1... | collective-permute-start | bytes 110600 | tf_op jit(solution)/shard_map/ppermute | solution.py:791
  38.5 1.3 %collective-permute-start.11 = (bf16[48,384]{1,0:T(8,128)(2,1)S(1)}, bf16[48,384]{1,0:T(8,128)(2,1)S(1)}, u32[]{:S(2)}, u32[]{:S(2)}) collective-permute-start(bf16[48,384]{1,0:T(8,128)(2,1)S(1)} %get-tuple-element.67), channel_id=1, source_target_pairs={{3,0},{4,1},{5,2},{6,3},{7,4},{0,5},{1,6},{2,7},{11,8},{12,9},{13,... | collective-permute-start | bytes 110600 | tf_op jit(solution)/shard_map/ppermute | solution.py:791
  39.7 0.7 %shard_map.131 = f32[8,48]{1,0:T(8,128)} custom-call(bf16[56,384]{1,0:T(8,128)(2,1)S(1)} %collective-permute-done.10.got_ref, f32[8,384]{1,0:T(8,128)S(1)} %get-tuple-element.68.partial_ref), custom_call_target="tpu_custom_call" | custom-call | tf_op jit(solution)/shard_map/pallas_call | solution.py:362
  40.4 1.3 %collective-permute-done.12 = bf16[48,384]{1,0:T(8,128)(2,1)S(1)} collective-permute-done((bf16[48,384]{1,0:T(8,128)(2,1)S(1)}, bf16[48,384]{1,0:T(8,128)(2,1)S(1)}, u32[]{:S(2)}, u32[]{:S(2)}) %collective-permute-start.12) | collective-permute-done | bytes 36896 | tf_op jit(solution)/shard_map/ppermute | solution.py:791
  41.8 0.4 collective-permute-done.11
  42.1 0.7 %pad_maximum_fusion = f32[144,384]{1,0:T(8,128)} fusion(f32[48,384]{1,0:T(8,128)S(1)} %convert_element_type.7, f32[48,384]{1,0:T(8,128)S(1)} %convert_element_type.6, f32[48,384]{1,0:T(8,128)S(1)} %get-tuple-element.66), kind=kLoop, calls=%fused_computation | loop fusion | flops 110592 | bytes 442368 | tf_op jit(solution)/shard_map/concatenate | solution.py:795
  (16 shorter events, 0.1 us)
Async XLA Ops:
  0.6 7.7 %collective-permute-start.2 = (bf16[2,3,192,384]{3,2,1,0:T(8,128)(2,1)}, bf16[2,3,192,384]{3,2,1,0:T(8,128)(2,1)S(1)}, u32[]{:S(2)}, u32[]{:S(2)}) collective-permute-start(bf16[2,3,192,384]{3,2,1,0:T(8,128)(2,1)} %bitcast.2), channel_id=1, source_target_pairs={{0,1},{1,0},{2,3},{3,2},{4,5},{5,4},{6,7},{7,6},{8,9},{9,8},{10,11... | collective-permute-start | bytes 2654216 | tf_op jit(solution)/shard_map/ppermute | solution.py:681
  1.1 5.4 %copy-start.9 = (f32[768]{0:T(1024)S(1)}, f32[768]{0:T(1024)}, u32[]{:S(2)}) copy-start(f32[768]{0:T(1024)} %param.13) | copy-start | bytes 9220
  1.2 7.2 %copy-start = (bf16[2,3,384,192]{2,3,1,0:T(8,128)(2,1)S(1)}, bf16[2,3,384,192]{2,3,1,0:T(8,128)(2,1)}, u32[]{:S(2)}) copy-start(bf16[2,3,384,192]{2,3,1,0:T(8,128)(2,1)} %param.15) | copy-start | bytes 2654212
  1.2 7.2 %copy-start.1 = (bf16[2,768,192]{1,2,0:T(8,128)(2,1)S(1)}, bf16[2,768,192]{1,2,0:T(8,128)(2,1)}, u32[]{:S(2)}) copy-start(bf16[2,768,192]{1,2,0:T(8,128)(2,1)} %param.14) | copy-start | bytes 1769476
  1.2 7.1 %collective-permute-start.1 = (bf16[2,192,768]{2,1,0:T(8,128)(2,1)}, bf16[2,192,768]{2,1,0:T(8,128)(2,1)S(1)}, u32[]{:S(2)}, u32[]{:S(2)}) collective-permute-start(bf16[2,192,768]{2,1,0:T(8,128)(2,1)} %bitcast.4), channel_id=1, source_target_pairs={{0,1},{1,0},{2,3},{3,2},{4,5},{5,4},{6,7},{7,6},{8,9},{9,8},{10,11... | collective-permute-start | bytes 1769480 | tf_op jit(solution)/shard_map/ppermute | solution.py:681
  1.3 9.4 %collective-permute-start.4 = (bf16[2,384,384]{2,1,0:T(8,128)(2,1)}, bf16[2,384,384]{2,1,0:T(8,128)(2,1)S(1)}, u32[]{:S(2)}, u32[]{:S(2)}) collective-permute-start(bf16[2,384,384]{2,1,0:T(8,128)(2,1)} %up_ref.3), channel_id=1, source_target_pairs={{0,1},{1,0},{2,3},{3,2},{4,5},{5,4},{6,7},{7,6},{8,9},{9,8},{10,11... | collective-permute-start | bytes 1769480 | tf_op jit(solution)/shard_map/ppermute | solution.py:681
  2.8 5.4 %collective-permute-start = (bf16[1,8,896]{2,1,0:T(8,128)(2,1)S(1)}, bf16[1,8,896]{2,1,0:T(8,128)(2,1)S(1)}, u32[]{:S(2)}, u32[]{:S(2)}) collective-permute-start(bf16[1,8,896]{2,1,0:T(8,128)(2,1)S(1)} %shard_map.121.first_ref), channel_id=1, source_target_pairs={{0,8},{2,10},{4,12},{6,14},{8,0},{10,2},{12,4},{14,6},{1,9},{3,11}... | collective-permute-start | bytes 43016 | tf_op jit(solution)/shard_map/ppermute | solution.py:681
  8.3 2.4 %copy-start.2 = (bf16[2,384,384]{2,1,0:T(8,128)(2,1)S(1)}, bf16[2,384,384]{2,1,0:T(8,128)(2,1)}, u32[]{:S(2)}) copy-start(bf16[2,384,384]{2,1,0:T(8,128)(2,1)} %up_ref.3) | copy-start | bytes 1769476
  8.3 2.4 %copy-start.3 = (bf16[1,128,768]{2,1,0:T(8,128)(2,1)S(1)}, bf16[1,128,768]{2,1,0:T(8,128)(2,1)}, u32[]{:S(2)}) copy-start(bf16[1,128,768]{2,1,0:T(8,128)(2,1)} %feature_ref.1) | copy-start | bytes 589828
  8.3 2.3 %copy-start.6 = (s32[1,128]{1,0:T(1,128)S(1)}, s32[1,128]{1,0:T(1,128)}, u32[]{:S(2)}) copy-start(s32[1,128]{1,0:T(1,128)} %count_ref.1) | copy-start | bytes 1540
  8.6 4.1 %copy-start.7 = (f32[4]{0:T(128)S(1)}, f32[4]{0:T(128)}, u32[]{:S(2)}) copy-start(f32[4]{0:T(128)} %decay_ref.3) | copy-start | bytes 52
  8.6 6.0 %copy-start.4 = (bf16[1,128,768]{2,1,0:T(8,128)(2,1)S(1)}, bf16[1,128,768]{2,1,0:T(8,128)(2,1)}, u32[]{:S(2)}) copy-start(bf16[1,128,768]{2,1,0:T(8,128)(2,1)} %cot_ref.1) | copy-start | bytes 589828
  8.6 6.0 %copy-start.5 = (f32[2,4,768]{2,1,0:T(4,128)S(1)}, f32[2,4,768]{2,1,0:T(4,128)}, u32[]{:S(2)}) copy-start(f32[2,4,768]{2,1,0:T(4,128)} %mode_ref.3) | copy-start | bytes 73732
  8.6 6.0 %copy-start.8 = (f32[1,128]{1,0:T(1,128)S(1)}, f32[1,128]{1,0:T(1,128)}, u32[]{:S(2)}) copy-start(f32[1,128]{1,0:T(1,128)} %keep_ref.3) | copy-start | bytes 1540
  8.6 3.9 %collective-permute-start.3 = (bf16[2,8,896]{2,1,0:T(8,128)(2,1)S(1)}, bf16[2,8,896]{2,1,0:T(8,128)(2,1)S(1)}, u32[]{:S(2)}, u32[]{:S(2)}) collective-permute-start(bf16[2,8,896]{2,1,0:T(8,128)(2,1)S(1)} %pad_maximum_fusion.2), channel_id=1, source_target_pairs={{0,4},{2,6},{4,0},{6,2},{8,12},{10,14},{12,8},{14,10},{1,5},{3,7},... | collective-permute-start | bytes 86024 | tf_op jit(solution)/shard_map/ppermute | solution.py:681
  12.6 3.5 %collective-permute-start.5 = (bf16[256,384]{1,0:T(8,128)(2,1)S(1)}, bf16[256,384]{1,0:T(8,128)(2,1)S(1)}, u32[]{:S(2)}, u32[]{:S(2)}) collective-permute-start(bf16[256,384]{1,0:T(8,128)(2,1)S(1)} %get-tuple-element.43.reduced_ref), channel_id=1, source_target_pairs={{0,1},{1,0},{2,3},{3,2},{4,5},{5,4},{6,7},{7,6},{8,9},{9,8},{10,11... | collective-permute-start | bytes 589832 | tf_op jit(solution)/shard_map/ppermute | solution.py:681
  12.7 4.5 %collective-permute-start.6 = (bf16[4,8,896]{2,1,0:T(8,128)(2,1)S(1)}, bf16[4,8,896]{2,1,0:T(8,128)(2,1)S(1)}, u32[]{:S(2)}, u32[]{:S(2)}) collective-permute-start(bf16[4,8,896]{2,1,0:T(8,128)(2,1)S(1)} %pad_maximum_fusion.1), channel_id=1, source_target_pairs={{0,2},{2,0},{4,6},{6,4},{8,10},{10,8},{12,14},{14,12},{1,3},{3,1},... | collective-permute-start | bytes 172040 | tf_op jit(solution)/shard_map/ppermute | solution.py:681
  19.3 1.5 %collective-permute-start.7 = (bf16[288,384]{1,0:T(8,128)(2,1)S(1)}, bf16[288,384]{1,0:T(8,128)(2,1)S(1)}, u32[]{:S(2)}, u32[]{:S(2)}) collective-permute-start(bf16[288,384]{1,0:T(8,128)(2,1)S(1)} %get-tuple-element.53.mixed_ref), channel_id=1, source_target_pairs={{0,1},{1,0},{2,3},{3,2},{4,5},{5,4},{6,7},{7,6},{8,9},{9,8},{10,11... | collective-permute-start | bytes 663560 | tf_op jit(solution)/shard_map/ppermute | solution.py:681
  21.3 6.2 %collective-permute-start.8 = (bf16[208,384]{1,0:T(8,128)(2,1)S(1)}, bf16[208,384]{1,0:T(8,128)(2,1)S(1)}, u32[]{:S(2)}, u32[]{:S(2)}) collective-permute-start(bf16[208,384]{1,0:T(8,128)(2,1)S(1)} %get-tuple-element.56), channel_id=1, source_target_pairs={{0,3},{1,2},{2,1},{3,0},{4,7},{5,6},{6,5},{7,4},{8,11},{9,10},{10,... | collective-permute-start | bytes 479240 | tf_op jit(solution)/shard_map/ppermute | solution.py:686
  27.5 4.6 %collective-permute-start.9 = (bf16[112,384]{1,0:T(8,128)(2,1)S(1)}, bf16[112,384]{1,0:T(8,128)(2,1)S(1)}, u32[]{:S(2)}, u32[]{:S(2)}) collective-permute-start(bf16[112,384]{1,0:T(8,128)(2,1)S(1)} %get-tuple-element.62), channel_id=1, source_target_pairs={{0,5},{1,4},{2,7},{3,6},{4,1},{5,0},{6,3},{7,2},{8,13},{9,12},{10,... | collective-permute-start | bytes 258056 | tf_op jit(solution)/shard_map/ppermute | solution.py:686
  32.1 4.5 %collective-permute-start.10 = (bf16[56,384]{1,0:T(8,128)(2,1)S(1)}, bf16[56,384]{1,0:T(8,128)(2,1)S(1)}, u32[]{:S(2)}, u32[]{:S(2)}) collective-permute-start(bf16[56,384]{1,0:T(8,128)(2,1)S(1)} %get-tuple-element.65), channel_id=1, source_target_pairs={{0,9},{1,8},{2,11},{3,10},{4,13},{5,12},{6,15},{7,14},{8,1},{9,0},... | collective-permute-start | bytes 129032 | tf_op jit(solution)/shard_map/ppermute | solution.py:686
  36.7 5.1 %collective-permute-start.12 = (bf16[48,384]{1,0:T(8,128)(2,1)S(1)}, bf16[48,384]{1,0:T(8,128)(2,1)S(1)}, u32[]{:S(2)}, u32[]{:S(2)}) collective-permute-start(bf16[48,384]{1,0:T(8,128)(2,1)S(1)} %get-tuple-element.67), channel_id=1, source_target_pairs={{6,0},{7,1},{0,2},{1,3},{2,4},{3,5},{4,6},{5,7},{14,8},{15,9},{8,1... | collective-permute-start | bytes 110600 | tf_op jit(solution)/shard_map/ppermute | solution.py:791
  38.5 3.7 %collective-permute-start.11 = (bf16[48,384]{1,0:T(8,128)(2,1)S(1)}, bf16[48,384]{1,0:T(8,128)(2,1)S(1)}, u32[]{:S(2)}, u32[]{:S(2)}) collective-permute-start(bf16[48,384]{1,0:T(8,128)(2,1)S(1)} %get-tuple-element.67), channel_id=1, source_target_pairs={{3,0},{4,1},{5,2},{6,3},{7,4},{0,5},{1,6},{2,7},{11,8},{12,9},{13,... | collective-permute-start | bytes 110600 | tf_op jit(solution)/shard_map/ppermute | solution.py:791

commit v4 on v3

--- a/solution.py
+++ b/solution.py
@@ -530,8 +530,8 @@
     wide = up_ref.shape[-1]
 
     masks = [0]
-    for hop in HOPS:
-        masks = masks + [mask ^ hop for mask in masks]
+    for hop in (HOPS[0], HOPS[1] - core, HOPS[2] + core):
+        masks = masks + [lax.bitwise_xor(mask, hop) for mask in masks]
     pieces = []
     for ref in (first_ref, second_ref, third_ref, fourth_ref):
         pieces = pieces + [ref[index].astype(F32) for index in range(ref.shape[0])]
@@ -616,8 +616,8 @@
     reduced_ref, reduced_far_ref, mixed_ref, mixed_far_ref, partial_ref,
     kept_ref, send_ref, partial_out, block_ref,
 ):
-    bit = position_bit(0)
-    parity = lax.rem(lax.axis_index("dp") + bit + position_bit(1) + position_bit(2), 2)
+    bits, parity = position_bits()
+    bit = pick(parity, bits[0], bits[1])
     rows = reduced_ref.shape[0] // LAYERS
     for layer in range(LAYERS):
         part = slice(layer * rows, (layer + 1) * rows)
@@ -628,10 +628,10 @@
     for turn in range(2):
         for layer in range(LAYERS):
             to = (2 * turn + layer) * BLOCK
-            kept_ref[to : to + BLOCK, :] = block_ref[layer, pl.ds(held_block(parity, bit, turn, layer), BLOCK), :]
-            send_ref[to : to + BLOCK, :] = block_ref[
-                layer, pl.ds(held_block(parity, 1 - bit, turn, layer), BLOCK), :
-            ].astype(BF16)
+            kept = held_block(parity, pick(parity, bit, turn), pick(parity, turn, bit), layer)
+            sent = held_block(parity, pick(parity, 1 - bit, turn), pick(parity, turn, 1 - bit), layer)
+            kept_ref[to : to + BLOCK, :] = block_ref[layer, pl.ds(kept, BLOCK), :]
+            send_ref[to : to + BLOCK, :] = block_ref[layer, pl.ds(sent, BLOCK), :].astype(BF16)
     high = mixed_far_ref[LAYERS * rows : LAYERS * rows + 16, :].astype(F32)
     low = mixed_far_ref[LAYERS * rows + 16 : LAYERS * rows + 32, :].astype(F32)
     partial = partial_ref[...] + (high + low)
@@ -639,14 +639,20 @@
     send_ref[kept_rows : kept_rows + 16, :] = partial.astype(BF16)
 
 
-def position_bit(stage):
+def position_bits():
     place = lax.axis_index("seq")
-    return lax.rem(place // (1, 2, 4)[stage], 2)
+    bits = [lax.rem(place // value, 2) for value in (1, 2, 4)]
+    return bits, lax.rem(lax.axis_index("dp") + bits[0] + bits[1] + bits[2], 2)
+
+
+def pick(parity, even, odd):
+    return even + parity * (odd - even)
 
 
 def join_body(stage, kept_ref, got_ref, partial_ref, kept_out, send_out, partial_out):
     rows = kept_out.shape[0]
-    bit = position_bit(stage)
+    bits, parity = position_bits()
+    bit = pick(parity, bits[1], bits[0]) if stage == 1 else bits[2]
     keep = pl.ds(pl.multiple_of(bit * rows, rows), rows)
     send = pl.ds(pl.multiple_of((1 - bit) * rows, rows), rows)
     kept_out[...] = kept_ref[keep, :] + got_ref[keep, :].astype(F32)
@@ -656,7 +662,7 @@
         partial_out[...] = partial
         send_out[rows : rows + 16, :] = partial.astype(BF16)
     else:
-        last = position_bit(2)
+        last = bits[2]
         partial_out[...] = jnp.where(last == 0, partial[0:8], partial[8:16])
         send_out[rows : rows + 8, :] = jnp.where(last == 0, partial[8:16], partial[0:8]).astype(BF16)
 
@@ -681,9 +687,16 @@
     return lax.ppermute(value, axis, [(source, source ^ mask) for source in range(count)])
 
 
-def cross(value, mask):
-    count = 2 * lax.axis_size("seq")
-    return lax.ppermute(value, ("seq", "dp"), [(source, source ^ (2 * mask + 1)) for source in range(count)])
+def hop_to(value, step):
+    pairs = []
+    for source in range(2 * lax.axis_size("seq")):
+        flip, mask = step(source % 2, source // 2)
+        pairs.append((source, source ^ (2 * mask + flip)))
+    return lax.ppermute(value, ("seq", "dp"), pairs)
+
+
+def class_of(core, place):
+    return (core + place + place // 2 + place // 4) % 2
 
 
 def wrapped_device(
@@ -708,7 +721,7 @@
         ),
         size=1300 * GIGA,
     )
-    got = swap(pay, "seq", HOPS[0])
+    got = hop_to(pay, lambda core, place: (0, HOPS[0]))
     down_full, tap_full = call(
         assemble_body,
         (down, down_far, taps, taps_far),
@@ -717,7 +730,7 @@
     )
     two = jnp.concatenate([pay, got], axis=0)
     two, down_full, tap_full = lax.optimization_barrier((two, down_full, tap_full))
-    got_two = swap(two, "seq", HOPS[1])
+    got_two = hop_to(two, lambda core, place: (0, HOPS[1 + core]))
     stream, inverse, reduced, slope = call(
         forward_body,
         (features, counts, count_weight[None], down_full, tap_full, up_weight, up_far),
@@ -731,7 +744,7 @@
     )
     four = jnp.concatenate([two, got_two], axis=0)
     four, stream, reduced = lax.optimization_barrier((four, stream, reduced))
-    got_four = swap(four, "seq", HOPS[2])
+    got_four = hop_to(four, lambda core, place: (0, HOPS[2 - core]))
     reduced_far = swap(reduced, "dp", 1)
     local, mark, reach = call(
         local_body,
@@ -764,7 +777,7 @@
         (((kept_rows, B), F32), ((kept_rows + 16, B), BF16), ((16, B), F32)),
         (pltpu.VMEM((LAYERS, B, B), F32),), size=500 * GIGA
     )
-    got = cross(send, 1)
+    got = hop_to(send, lambda core, place: (1, 1 + class_of(core, place)))
     for stage in (1, 2):
         kept_rows = kept.shape[0] // 2
         mode_rows = (16, 8)[stage - 1]
@@ -776,7 +789,10 @@
         )
         if stage == 1:
             send, grad = lax.optimization_barrier((send, grad))
-        got = cross(send, (1, 2, 4)[stage])
+        if stage == 1:
+            got = hop_to(send, lambda core, place: (1, 2 - class_of(core, place)))
+        else:
+            got = hop_to(send, lambda core, place: (1, 4))
     total = features.shape[0] * lax.axis_size("dp") * rows * lax.axis_size("seq")
     report = 1.0 / math.sqrt(total)
     block, narrow = call(

time: 43.3 us -> 41.2 us (0.952)
  waiting for transfers between devices: 14.3 us -> 11.6 us
  starting transfers between devices: 17.6 us -> 18.2 us
    ppermute x3 -> x6, starting transfers between devices: 5.75 us -> 13.7 us  [hop_to(): return lax.ppermute(value, ('seq', 'dp'), pairs)]
    ppermute x8 -> x5, starting transfers between devices: 8.78 us -> 1.17 us  [swap(): lax.ppermute(value, axis, [(source, source ^ mask) for source in range(co...]
    ppermute x8 -> x5, waiting for transfers between devices: 4.34 us -> 1.47 us  [swap(): lax.ppermute(value, axis, [(source, source ^ mask) for source in range(co...]
    ppermute x3 -> x6, waiting for transfers between devices: 8.25 us -> 8.45 us  [hop_to(): return lax.ppermute(value, ('seq', 'dp'), pairs)]
where the time goes in v4:
time: 41.2 us; the launch traced here: 40.7 us
  starting transfers between devices  18.2 us (44%)
  waiting for transfers between devices  11.6 us (28%)
  Pallas kernels  9.29 us (23%)
  between operations  0.83 us (2%)
  other arithmetic  0.74 us (2%)
    ppermute x6, starting transfers between devices, hop_to(): return lax.ppermute(value, ('seq', 'dp'), pairs)  13.7 us
    pallas_call x11, Pallas kernels, call(): pl.pallas_call(body, out_shape=[jax.ShapeDtypeStruct(shape, dtype) for sh...  9.29 us
    ppermute x6, waiting for transfers between devices, hop_to(): return lax.ppermute(value, ('seq', 'dp'), pairs)  8.45 us
    ppermute x2, starting transfers between devices, wrapped_device(): parts.append(lax.ppermute(narrow, ('seq', 'dp'), pairs).astype(F32))  3.32 us
    ppermute x2, waiting for transfers between devices, wrapped_device(): parts.append(lax.ppermute(narrow, ('seq', 'dp'), pairs).astype(F32))  1.7 us
    ppermute x5, waiting for transfers between devices, swap(): lax.ppermute(value, axis, [(source, source ^ mask) for source in range(co...  1.47 us
    ppermute x5, starting transfers between devices, swap(): lax.ppermute(value, axis, [(source, source ^ mask) for source in range(co...  1.17 us
  transfers between devices with their start and end apart: 13, of which 9 were waited for; matrix products, arithmetic and copies ran while one was open for 0% of the time, Pallas kernels for 16%

profile of v4, /device:TPU:0, one launch (start us, length us, event | category | flops | bytes accessed | tf_op | source)
XLA Modules:
  0.0 40.7 jit_solution(8897651570503500738)
XLA Ops:
  0.6 0.5 %collective-permute-start.2 = (bf16[2,3,192,384]{3,2,1,0:T(8,128)(2,1)}, bf16[2,3,192,384]{3,2,1,0:T(8,128)(2,1)S(1)}, u32[]{:S(2)}, u32[]{:S(2)}) collective-permute-start(bf16[2,3,192,384]{3,2,1,0:T(8,128)(2,1)} %bitcast.2), channel_id=1, source_target_pairs={{0,1},{1,0},{2,3},{3,2},{4,5},{5,4},{6,7},{7,6},{8,9},{9,8},{10,11... | collective-permute-start | bytes 2654216 | tf_op jit(solution)/shard_map/ppermute | solution.py:687
  1.2 0.1 collective-permute-start.1
  1.3 0.4 collective-permute-start.4
  1.7 1.1 %shard_map.121.first_ref = bf16[1,8,896]{2,1,0:T(8,128)(2,1)S(1)} custom-call(bf16[1,128,768]{2,1,0:T(8,128)(2,1)} %cot_ref.1, f32[1,128]{1,0:T(1,128)} %keep_ref.3, f32[4]{0:T(128)} %decay_ref.3), custom_call_target="tpu_custom_call" | custom-call | flops 1300000000 | bytes 5078125 | tf_op jit(solution)/shard_map/pallas_call | solution.py:362
  2.8 3.8 %collective-permute-start = (bf16[1,8,896]{2,1,0:T(8,128)(2,1)S(1)}, bf16[1,8,896]{2,1,0:T(8,128)(2,1)S(1)}, u32[]{:S(2)}, u32[]{:S(2)}) collective-permute-start(bf16[1,8,896]{2,1,0:T(8,128)(2,1)S(1)} %shard_map.121.first_ref), channel_id=1, source_target_pairs={{0,8},{1,9},{2,10},{3,11},{4,12},{5,13},{6,14},{7,15},{8,0},{9,1},... | collective-permute-start | bytes 43016 | tf_op jit(solution)/shard_map/ppermute | solution.py:695
  6.5 0.0 copy-done.9
  6.6 1.7 %collective-permute-done.second_ref = bf16[1,8,896]{2,1,0:T(8,128)(2,1)S(1)} collective-permute-done((bf16[1,8,896]{2,1,0:T(8,128)(2,1)S(1)}, bf16[1,8,896]{2,1,0:T(8,128)(2,1)S(1)}, u32[]{:S(2)}, u32[]{:S(2)}) %collective-permute-start) | collective-permute-done | bytes 14368 | tf_op jit(solution)/shard_map/ppermute | solution.py:695
  8.3 0.0 copy-start.2
  8.3 0.0 copy-start.3
  8.3 0.0 copy-start.6
  8.3 0.0 collective-permute-done.1.down_far_ref
  8.3 0.0 collective-permute-done.2.tap_far_ref
  8.3 0.0 copy-done
  8.3 0.0 copy-done.1
  8.3 0.3 shard_map.122
  8.6 0.0 copy-start.7
  8.6 0.0 copy-start.4
  8.6 0.0 copy-start.5
  8.6 0.0 copy-start.8
  8.6 2.0 %collective-permute-start.3 = (bf16[2,8,896]{2,1,0:T(8,128)(2,1)S(1)}, bf16[2,8,896]{2,1,0:T(8,128)(2,1)S(1)}, u32[]{:S(2)}, u32[]{:S(2)}) collective-permute-start(bf16[2,8,896]{2,1,0:T(8,128)(2,1)S(1)} %pad_maximum_fusion.2), channel_id=1, source_target_pairs={{0,4},{1,3},{2,6},{3,1},{4,0},{5,7},{6,2},{7,5},{8,12},{9,11},{10,... | collective-permute-start | bytes 86024 | tf_op jit(solution)/shard_map/ppermute | solution.py:695
  10.6 0.0 collective-permute-done.4.up_far_ref
  10.6 0.0 copy-done.2
  10.6 1.8 %shard_map.123 = (f32[3,128,768]{2,1,0:T(8,128)S(1)}, f32[2,128,1]{2,1,0:T(8,128)S(1)}, bf16[256,384]{1,0:T(8,128)(2,1)S(1)}, f32[2,128,384]{2,1,0:T(8,128)S(1)}) custom-call(bf16[1,128,768]{2,1,0:T(8,128)(2,1)S(1)} %copy-done.3, s32[1,128]{1,0:T(1,128)S(1)} %copy-done.6, f32[1,768]{1,0:T(1,128)S(1)} %broadcast_in_dim.3.weight_ref, ...), custom_call_target="tpu_custom_call" | custom-call | flops 1800000000 | bytes 7031250 | tf_op jit(solution)/shard_map/pallas_call | solution.py:362
  12.5 0.1 collective-permute-done.3.third_ref
  12.6 0.1 collective-permute-start.5
  12.7 0.0 copy-done.7
  12.7 1.9 %collective-permute-start.6 = (bf16[4,8,896]{2,1,0:T(8,128)(2,1)S(1)}, bf16[4,8,896]{2,1,0:T(8,128)(2,1)S(1)}, u32[]{:S(2)}, u32[]{:S(2)}) collective-permute-start(bf16[4,8,896]{2,1,0:T(8,128)(2,1)S(1)} %pad_maximum_fusion.1), channel_id=1, source_target_pairs={{0,2},{1,5},{2,0},{3,7},{4,6},{5,1},{6,4},{7,3},{8,10},{9,13},{10,... | collective-permute-start | bytes 172040 | tf_op jit(solution)/shard_map/ppermute | solution.py:695
  14.6 0.0 copy-done.8
  14.6 1.5 %shard_map.124 = (f32[128,768]{1,0:T(8,128)S(1)}, f32[8,768]{1,0:T(8,128)S(1)}, f32[8,768]{1,0:T(8,128)S(1)}) custom-call(f32[4]{0:T(128)S(1)} %copy-done.7, f32[4]{0:T(128)S(1)} %negate_sqrt_fusion.scale_ref, bf16[1,128,768]{2,1,0:T(8,128)(2,1)S(1)} %copy-done.4, f32[1,128]{1,0:T(1,128)S(1)} %copy-done.8, f32[2,4,768]{2,1,0:T(4,128)S(1)} %copy-done.5, ...), custom_call_target="tpu_custom_call" | custom-call | flops 1600000000 | bytes 6250000 | tf_op jit(solution)/shard_map/pallas_call | solution.py:362
  16.1 0.0 collective-permute-done.5.reduced_far_ref
  16.1 0.8 %collective-permute-done.6.fourth_ref = bf16[4,8,896]{2,1,0:T(8,128)(2,1)S(1)} collective-permute-done((bf16[4,8,896]{2,1,0:T(8,128)(2,1)S(1)}, bf16[4,8,896]{2,1,0:T(8,128)(2,1)S(1)}, u32[]{:S(2)}, u32[]{:S(2)}) %collective-permute-start.6) | collective-permute-done | bytes 57376 | tf_op jit(solution)/shard_map/ppermute | solution.py:695
  16.9 2.1 %shard_map.125 = (f32[128,768]{1,0:T(8,128)S(1)}, bf16[288,384]{1,0:T(8,128)(2,1)S(1)}, f32[16,384]{1,0:T(8,128)S(1)}) custom-call(f32[4]{0:T(128)S(1)} %copy-done.7, f32[4]{0:T(128)S(1)} %negate_sqrt_fusion.scale_ref, bf16[1,8,896]{2,1,0:T(8,128)(2,1)S(1)} %shard_map.121.first_ref, bf16[1,8,896]{2,1,0:T(8,128)(2,1)S(1)} %collective-permute-done.second_ref, ...), custom_call_target="tpu_custom_call" | custom-call | flops 2100000000 | bytes 8203125 | tf_op jit(solution)/shard_map/pallas_call | solution.py:362
  19.1 0.1 collective-permute-start.7
  19.1 1.5 %collective-permute-done.7.mixed_far_ref = bf16[288,384]{1,0:T(8,128)(2,1)S(1)} collective-permute-done((bf16[288,384]{1,0:T(8,128)(2,1)S(1)}, bf16[288,384]{1,0:T(8,128)(2,1)S(1)}, u32[]{:S(2)}, u32[]{:S(2)}) %collective-permute-start.7) | collective-permute-done | bytes 221216 | tf_op jit(solution)/shard_map/ppermute | solution.py:687
  20.6 0.4 %shard_map.126 = (f32[192,384]{1,0:T(8,128)S(1)}, bf16[208,384]{1,0:T(8,128)(2,1)S(1)}, f32[16,384]{1,0:T(8,128)S(1)}) custom-call(bf16[256,384]{1,0:T(8,128)(2,1)S(1)} %get-tuple-element.43.reduced_ref, bf16[256,384]{1,0:T(8,128)(2,1)S(1)} %collective-permute-done.5.reduced_far_ref, bf16[288,384]{1,0:T(8,128)(2,1)S(1)} %get-tuple-element.53.mixed_ref, ...), custom_call_target="tpu_custom_call" | custom-call | flops 500000000 | bytes 1953125 | tf_op jit(solution)/shard_map/pallas_call | solution.py:362
  21.0 1.6 %collective-permute-start.8 = (bf16[208,384]{1,0:T(8,128)(2,1)S(1)}, bf16[208,384]{1,0:T(8,128)(2,1)S(1)}, u32[]{:S(2)}, u32[]{:S(2)}) collective-permute-start(bf16[208,384]{1,0:T(8,128)(2,1)S(1)} %get-tuple-element.56), channel_id=1, source_target_pairs={{0,3},{1,4},{2,7},{3,0},{4,1},{5,6},{6,5},{7,2},{8,13},{9,10},{10,... | collective-permute-start | bytes 479240 | tf_op jit(solution)/shard_map/ppermute | solution.py:695
  22.7 1.3 %shard_map.128 = bf16[1,128,768]{2,1,0:T(8,128)(2,1)} custom-call(f32[128,768]{1,0:T(8,128)S(1)} %get-tuple-element.59.gradient_ref, bf16[288,384]{1,0:T(8,128)(2,1)S(1)} %get-tuple-element.53.mixed_ref, f32[3,128,768]{2,1,0:T(8,128)S(1)} %get-tuple-element.44.stream_ref, f32[2,128,1]{2,1,0:T(8,128)S(1)} %get-tuple-element.51.inverse_ref, ...), custom_call_target="tpu_custom_call" | custom-call | flops 1300000000 | bytes 5078125 | tf_op jit(solution)/shard_map/pallas_call | solution.py:362
  24.0 1.8 %collective-permute-done.8.got_ref = bf16[208,384]{1,0:T(8,128)(2,1)S(1)} collective-permute-done((bf16[208,384]{1,0:T(8,128)(2,1)S(1)}, bf16[208,384]{1,0:T(8,128)(2,1)S(1)}, u32[]{:S(2)}, u32[]{:S(2)}) %collective-permute-start.8) | collective-permute-done | bytes 159776 | tf_op jit(solution)/shard_map/ppermute | solution.py:695
  25.9 1.7 %collective-permute-start.9 = (bf16[112,384]{1,0:T(8,128)(2,1)S(1)}, bf16[112,384]{1,0:T(8,128)(2,1)S(1)}, u32[]{:S(2)}, u32[]{:S(2)}) collective-permute-start(bf16[112,384]{1,0:T(8,128)(2,1)S(1)} %get-tuple-element.62), channel_id=1, source_target_pairs={{0,5},{1,2},{2,1},{3,6},{4,7},{5,0},{6,3},{7,4},{8,11},{9,12},{10,... | collective-permute-start | bytes 258056 | tf_op jit(solution)/shard_map/ppermute | solution.py:695
  27.6 2.3 %collective-permute-done.9.got_ref = bf16[112,384]{1,0:T(8,128)(2,1)S(1)} collective-permute-done((bf16[112,384]{1,0:T(8,128)(2,1)S(1)}, bf16[112,384]{1,0:T(8,128)(2,1)S(1)}, u32[]{:S(2)}, u32[]{:S(2)}) %collective-permute-start.9) | collective-permute-done | bytes 86048 | tf_op jit(solution)/shard_map/ppermute | solution.py:695
  29.9 2.7 %collective-permute-start.10 = (bf16[56,384]{1,0:T(8,128)(2,1)S(1)}, bf16[56,384]{1,0:T(8,128)(2,1)S(1)}, u32[]{:S(2)}, u32[]{:S(2)}) collective-permute-start(bf16[56,384]{1,0:T(8,128)(2,1)S(1)} %get-tuple-element.65), channel_id=1, source_target_pairs={{0,9},{1,8},{2,11},{3,10},{4,13},{5,12},{6,15},{7,14},{8,1},{9,0},... | collective-permute-start | bytes 129032 | tf_op jit(solution)/shard_map/ppermute | solution.py:695
  32.6 1.7 %collective-permute-done.10.got_ref = bf16[56,384]{1,0:T(8,128)(2,1)S(1)} collective-permute-done((bf16[56,384]{1,0:T(8,128)(2,1)S(1)}, bf16[56,384]{1,0:T(8,128)(2,1)S(1)}, u32[]{:S(2)}, u32[]{:S(2)}) %collective-permute-start.10) | collective-permute-done | bytes 43040 | tf_op jit(solution)/shard_map/ppermute | solution.py:695
  34.3 2.0 %collective-permute-start.12 = (bf16[48,384]{1,0:T(8,128)(2,1)S(1)}, bf16[48,384]{1,0:T(8,128)(2,1)S(1)}, u32[]{:S(2)}, u32[]{:S(2)}) collective-permute-start(bf16[48,384]{1,0:T(8,128)(2,1)S(1)} %get-tuple-element.67), channel_id=1, source_target_pairs={{6,0},{7,1},{0,2},{1,3},{2,4},{3,5},{4,6},{5,7},{14,8},{15,9},{8,1... | collective-permute-start | bytes 110600 | tf_op jit(solution)/shard_map/ppermute | solution.py:807
  36.3 1.3 %collective-permute-start.11 = (bf16[48,384]{1,0:T(8,128)(2,1)S(1)}, bf16[48,384]{1,0:T(8,128)(2,1)S(1)}, u32[]{:S(2)}, u32[]{:S(2)}) collective-permute-start(bf16[48,384]{1,0:T(8,128)(2,1)S(1)} %get-tuple-element.67), channel_id=1, source_target_pairs={{3,0},{4,1},{5,2},{6,3},{7,4},{0,5},{1,6},{2,7},{11,8},{12,9},{13,... | collective-permute-start | bytes 110600 | tf_op jit(solution)/shard_map/ppermute | solution.py:807
  37.6 0.7 %shard_map.131 = f32[8,48]{1,0:T(8,128)} custom-call(bf16[56,384]{1,0:T(8,128)(2,1)S(1)} %collective-permute-done.10.got_ref, f32[8,384]{1,0:T(8,128)S(1)} %get-tuple-element.68.partial_ref), custom_call_target="tpu_custom_call" | custom-call | tf_op jit(solution)/shard_map/pallas_call | solution.py:362
  38.3 1.3 %collective-permute-done.12 = bf16[48,384]{1,0:T(8,128)(2,1)S(1)} collective-permute-done((bf16[48,384]{1,0:T(8,128)(2,1)S(1)}, bf16[48,384]{1,0:T(8,128)(2,1)S(1)}, u32[]{:S(2)}, u32[]{:S(2)}) %collective-permute-start.12) | collective-permute-done | bytes 36896 | tf_op jit(solution)/shard_map/ppermute | solution.py:807
  39.6 0.4 collective-permute-done.11
  40.0 0.7 %pad_maximum_fusion = f32[144,384]{1,0:T(8,128)} fusion(f32[48,384]{1,0:T(8,128)S(1)} %convert_element_type.7, f32[48,384]{1,0:T(8,128)S(1)} %convert_element_type.6, f32[48,384]{1,0:T(8,128)S(1)} %get-tuple-element.66), kind=kLoop, calls=%fused_computation | loop fusion | flops 110592 | bytes 442368 | tf_op jit(solution)/shard_map/concatenate | solution.py:811
  (16 shorter events, 0.1 us)
Async XLA Ops:
  0.6 7.7 %collective-permute-start.2 = (bf16[2,3,192,384]{3,2,1,0:T(8,128)(2,1)}, bf16[2,3,192,384]{3,2,1,0:T(8,128)(2,1)S(1)}, u32[]{:S(2)}, u32[]{:S(2)}) collective-permute-start(bf16[2,3,192,384]{3,2,1,0:T(8,128)(2,1)} %bitcast.2), channel_id=1, source_target_pairs={{0,1},{1,0},{2,3},{3,2},{4,5},{5,4},{6,7},{7,6},{8,9},{9,8},{10,11... | collective-permute-start | bytes 2654216 | tf_op jit(solution)/shard_map/ppermute | solution.py:687
  1.1 5.4 %copy-start.9 = (f32[768]{0:T(1024)S(1)}, f32[768]{0:T(1024)}, u32[]{:S(2)}) copy-start(f32[768]{0:T(1024)} %param.13) | copy-start | bytes 9220
  1.2 7.2 %copy-start = (bf16[2,3,384,192]{2,3,1,0:T(8,128)(2,1)S(1)}, bf16[2,3,384,192]{2,3,1,0:T(8,128)(2,1)}, u32[]{:S(2)}) copy-start(bf16[2,3,384,192]{2,3,1,0:T(8,128)(2,1)} %param.15) | copy-start | bytes 2654212
  1.2 7.2 %copy-start.1 = (bf16[2,768,192]{1,2,0:T(8,128)(2,1)S(1)}, bf16[2,768,192]{1,2,0:T(8,128)(2,1)}, u32[]{:S(2)}) copy-start(bf16[2,768,192]{1,2,0:T(8,128)(2,1)} %param.14) | copy-start | bytes 1769476
  1.2 7.1 %collective-permute-start.1 = (bf16[2,192,768]{2,1,0:T(8,128)(2,1)}, bf16[2,192,768]{2,1,0:T(8,128)(2,1)S(1)}, u32[]{:S(2)}, u32[]{:S(2)}) collective-permute-start(bf16[2,192,768]{2,1,0:T(8,128)(2,1)} %bitcast.4), channel_id=1, source_target_pairs={{0,1},{1,0},{2,3},{3,2},{4,5},{5,4},{6,7},{7,6},{8,9},{9,8},{10,11... | collective-permute-start | bytes 1769480 | tf_op jit(solution)/shard_map/ppermute | solution.py:687
  1.3 9.4 %collective-permute-start.4 = (bf16[2,384,384]{2,1,0:T(8,128)(2,1)}, bf16[2,384,384]{2,1,0:T(8,128)(2,1)S(1)}, u32[]{:S(2)}, u32[]{:S(2)}) collective-permute-start(bf16[2,384,384]{2,1,0:T(8,128)(2,1)} %up_ref.3), channel_id=1, source_target_pairs={{0,1},{1,0},{2,3},{3,2},{4,5},{5,4},{6,7},{7,6},{8,9},{9,8},{10,11... | collective-permute-start | bytes 1769480 | tf_op jit(solution)/shard_map/ppermute | solution.py:687
  2.8 5.4 %collective-permute-start = (bf16[1,8,896]{2,1,0:T(8,128)(2,1)S(1)}, bf16[1,8,896]{2,1,0:T(8,128)(2,1)S(1)}, u32[]{:S(2)}, u32[]{:S(2)}) collective-permute-start(bf16[1,8,896]{2,1,0:T(8,128)(2,1)S(1)} %shard_map.121.first_ref), channel_id=1, source_target_pairs={{0,8},{1,9},{2,10},{3,11},{4,12},{5,13},{6,14},{7,15},{8,0},{9,1},... | collective-permute-start | bytes 43016 | tf_op jit(solution)/shard_map/ppermute | solution.py:695
  8.3 2.4 %copy-start.2 = (bf16[2,384,384]{2,1,0:T(8,128)(2,1)S(1)}, bf16[2,384,384]{2,1,0:T(8,128)(2,1)}, u32[]{:S(2)}) copy-start(bf16[2,384,384]{2,1,0:T(8,128)(2,1)} %up_ref.3) | copy-start | bytes 1769476
  8.3 2.4 %copy-start.3 = (bf16[1,128,768]{2,1,0:T(8,128)(2,1)S(1)}, bf16[1,128,768]{2,1,0:T(8,128)(2,1)}, u32[]{:S(2)}) copy-start(bf16[1,128,768]{2,1,0:T(8,128)(2,1)} %feature_ref.1) | copy-start | bytes 589828
  8.3 2.3 %copy-start.6 = (s32[1,128]{1,0:T(1,128)S(1)}, s32[1,128]{1,0:T(1,128)}, u32[]{:S(2)}) copy-start(s32[1,128]{1,0:T(1,128)} %count_ref.1) | copy-start | bytes 1540
  8.6 4.1 %copy-start.7 = (f32[4]{0:T(128)S(1)}, f32[4]{0:T(128)}, u32[]{:S(2)}) copy-start(f32[4]{0:T(128)} %decay_ref.3) | copy-start | bytes 52
  8.6 6.0 %copy-start.4 = (bf16[1,128,768]{2,1,0:T(8,128)(2,1)S(1)}, bf16[1,128,768]{2,1,0:T(8,128)(2,1)}, u32[]{:S(2)}) copy-start(bf16[1,128,768]{2,1,0:T(8,128)(2,1)} %cot_ref.1) | copy-start | bytes 589828
  8.6 6.0 %copy-start.5 = (f32[2,4,768]{2,1,0:T(4,128)S(1)}, f32[2,4,768]{2,1,0:T(4,128)}, u32[]{:S(2)}) copy-start(f32[2,4,768]{2,1,0:T(4,128)} %mode_ref.3) | copy-start | bytes 73732
  8.6 6.0 %copy-start.8 = (f32[1,128]{1,0:T(1,128)S(1)}, f32[1,128]{1,0:T(1,128)}, u32[]{:S(2)}) copy-start(f32[1,128]{1,0:T(1,128)} %keep_ref.3) | copy-start | bytes 1540
  8.6 3.9 %collective-permute-start.3 = (bf16[2,8,896]{2,1,0:T(8,128)(2,1)S(1)}, bf16[2,8,896]{2,1,0:T(8,128)(2,1)S(1)}, u32[]{:S(2)}, u32[]{:S(2)}) collective-permute-start(bf16[2,8,896]{2,1,0:T(8,128)(2,1)S(1)} %pad_maximum_fusion.2), channel_id=1, source_target_pairs={{0,4},{1,3},{2,6},{3,1},{4,0},{5,7},{6,2},{7,5},{8,12},{9,11},{10,... | collective-permute-start | bytes 86024 | tf_op jit(solution)/shard_map/ppermute | solution.py:695
  12.6 3.5 %collective-permute-start.5 = (bf16[256,384]{1,0:T(8,128)(2,1)S(1)}, bf16[256,384]{1,0:T(8,128)(2,1)S(1)}, u32[]{:S(2)}, u32[]{:S(2)}) collective-permute-start(bf16[256,384]{1,0:T(8,128)(2,1)S(1)} %get-tuple-element.43.reduced_ref), channel_id=1, source_target_pairs={{0,1},{1,0},{2,3},{3,2},{4,5},{5,4},{6,7},{7,6},{8,9},{9,8},{10,11... | collective-permute-start | bytes 589832 | tf_op jit(solution)/shard_map/ppermute | solution.py:687
  12.7 4.2 %collective-permute-start.6 = (bf16[4,8,896]{2,1,0:T(8,128)(2,1)S(1)}, bf16[4,8,896]{2,1,0:T(8,128)(2,1)S(1)}, u32[]{:S(2)}, u32[]{:S(2)}) collective-permute-start(bf16[4,8,896]{2,1,0:T(8,128)(2,1)S(1)} %pad_maximum_fusion.1), channel_id=1, source_target_pairs={{0,2},{1,5},{2,0},{3,7},{4,6},{5,1},{6,4},{7,3},{8,10},{9,13},{10,... | collective-permute-start | bytes 172040 | tf_op jit(solution)/shard_map/ppermute | solution.py:695
  19.1 1.5 %collective-permute-start.7 = (bf16[288,384]{1,0:T(8,128)(2,1)S(1)}, bf16[288,384]{1,0:T(8,128)(2,1)S(1)}, u32[]{:S(2)}, u32[]{:S(2)}) collective-permute-start(bf16[288,384]{1,0:T(8,128)(2,1)S(1)} %get-tuple-element.53.mixed_ref), channel_id=1, source_target_pairs={{0,1},{1,0},{2,3},{3,2},{4,5},{5,4},{6,7},{7,6},{8,9},{9,8},{10,11... | collective-permute-start | bytes 663560 | tf_op jit(solution)/shard_map/ppermute | solution.py:687
  21.0 4.8 %collective-permute-start.8 = (bf16[208,384]{1,0:T(8,128)(2,1)S(1)}, bf16[208,384]{1,0:T(8,128)(2,1)S(1)}, u32[]{:S(2)}, u32[]{:S(2)}) collective-permute-start(bf16[208,384]{1,0:T(8,128)(2,1)S(1)} %get-tuple-element.56), channel_id=1, source_target_pairs={{0,3},{1,4},{2,7},{3,0},{4,1},{5,6},{6,5},{7,2},{8,13},{9,10},{10,... | collective-permute-start | bytes 479240 | tf_op jit(solution)/shard_map/ppermute | solution.py:695
  25.9 4.0 %collective-permute-start.9 = (bf16[112,384]{1,0:T(8,128)(2,1)S(1)}, bf16[112,384]{1,0:T(8,128)(2,1)S(1)}, u32[]{:S(2)}, u32[]{:S(2)}) collective-permute-start(bf16[112,384]{1,0:T(8,128)(2,1)S(1)} %get-tuple-element.62), channel_id=1, source_target_pairs={{0,5},{1,2},{2,1},{3,6},{4,7},{5,0},{6,3},{7,4},{8,11},{9,12},{10,... | collective-permute-start | bytes 258056 | tf_op jit(solution)/shard_map/ppermute | solution.py:695
  29.9 4.4 %collective-permute-start.10 = (bf16[56,384]{1,0:T(8,128)(2,1)S(1)}, bf16[56,384]{1,0:T(8,128)(2,1)S(1)}, u32[]{:S(2)}, u32[]{:S(2)}) collective-permute-start(bf16[56,384]{1,0:T(8,128)(2,1)S(1)} %get-tuple-element.65), channel_id=1, source_target_pairs={{0,9},{1,8},{2,11},{3,10},{4,13},{5,12},{6,15},{7,14},{8,1},{9,0},... | collective-permute-start | bytes 129032 | tf_op jit(solution)/shard_map/ppermute | solution.py:695
  34.3 5.3 %collective-permute-start.12 = (bf16[48,384]{1,0:T(8,128)(2,1)S(1)}, bf16[48,384]{1,0:T(8,128)(2,1)S(1)}, u32[]{:S(2)}, u32[]{:S(2)}) collective-permute-start(bf16[48,384]{1,0:T(8,128)(2,1)S(1)} %get-tuple-element.67), channel_id=1, source_target_pairs={{6,0},{7,1},{0,2},{1,3},{2,4},{3,5},{4,6},{5,7},{14,8},{15,9},{8,1... | collective-permute-start | bytes 110600 | tf_op jit(solution)/shard_map/ppermute | solution.py:807
  36.3 3.7 %collective-permute-start.11 = (bf16[48,384]{1,0:T(8,128)(2,1)S(1)}, bf16[48,384]{1,0:T(8,128)(2,1)S(1)}, u32[]{:S(2)}, u32[]{:S(2)}) collective-permute-start(bf16[48,384]{1,0:T(8,128)(2,1)S(1)} %get-tuple-element.67), channel_id=1, source_target_pairs={{3,0},{4,1},{5,2},{6,3},{7,4},{0,5},{1,6},{2,7},{11,8},{12,9},{13,... | collective-permute-start | bytes 110600 | tf_op jit(solution)/shard_map/ppermute | solution.py:807

commit v5 on v4

--- a/solution.py
+++ b/solution.py
@@ -479,7 +479,7 @@
     stream_ref[LAYERS] = stream
 
 
-def local_body(decay_ref, scale_ref, cot_ref, keep_ref, mode_ref, stream_ref, grad_ref, mark_ref, reach_ref):
+def local_body(decay_ref, scale_ref, cot_ref, keep_ref, mode_ref, stream_ref, grad_ref, mark_ref, reach_ref, edge_ref, rate_ref):
     rows, width = cot_ref.shape[1:]
     column, row, total = log_sums(keep_ref[...])
     below = iota2((rows, rows), 0)
@@ -497,6 +497,13 @@
     _, edges = mode_terms(row, total, decay_ref, rows)
     high = edges.astype(BF16).astype(F32)
     both = jnp.concatenate([high, edges - high], axis=0).astype(BF16)
+    edge_ref[...] = jnp.concatenate([high, high, edges - high, jnp.zeros_like(high)], axis=0).astype(BF16)
+    row8 = iota2((8, 128), 0)
+    for side, values_ref in enumerate((decay_ref, scale_ref)):
+        value8 = jnp.zeros((8, 128), F32)
+        for index in range(2 * M):
+            value8 = jnp.where(row8 == index, values_ref[index % M], value8)
+        rate_ref[side] = value8
     span = 256
     for start in range(0, width, span):
         part = slice(start, start + span)
@@ -519,14 +526,13 @@
 
 
 def backward_body(
-    decay_ref, scale_ref, first_ref, second_ref, third_ref, fourth_ref, keep_ref, mode_ref,
-    local_ref, mark_ref, reach_ref, stream_ref, inverse_ref, slope_ref, down_ref, tap_ref, up_ref,
+    first_ref, second_ref, third_ref, fourth_ref, mode_ref,
+    local_ref, mark_ref, reach_ref, edge_ref, rate_ref, stream_ref, inverse_ref, slope_ref, down_ref, tap_ref, up_ref,
     up_far_ref, grads_ref, mixed_ref, partial_ref,
 ):
     core = lax.axis_index("dp")
     place = lax.axis_index("seq")
-    rows = keep_ref.shape[-1]
-    width = local_ref.shape[-1]
+    rows, width = local_ref.shape
     wide = up_ref.shape[-1]
 
     masks = [0]
@@ -535,31 +541,25 @@
     pieces = []
     for ref in (first_ref, second_ref, third_ref, fourth_ref):
         pieces = pieces + [ref[index].astype(F32) for index in range(ref.shape[0])]
-    totals = [jnp.sum(piece[:, width:], axis=0, keepdims=True) for piece in pieces]
+    totals = jnp.concatenate([jnp.sum(piece[:, width:], axis=0, keepdims=True) for piece in pieces], axis=0)
     row8 = iota2((8, 128), 0)
-    decay8 = jnp.zeros((8, 128), F32)
-    gain8 = jnp.zeros((8, 128), F32)
-    for index in range(2 * M):
-        decay8 = jnp.where(row8 == index, decay_ref[index % M], decay8)
-        gain8 = jnp.where(row8 == index, scale_ref[index % M], gain8)
-    gain8 = gain8[:, 0:1]
-    everything = totals[0]
-    for value in totals[1:]:
-        everything = everything + value
-    loop = 1.0 - jnp.exp(jnp.broadcast_to(everything, (8, 128)) - (RING * rows) * decay8)
-    others = [lax.bitwise_xor(place, mask) for mask in masks]
-    ahead = [lax.rem(place - other + (RING - 1), RING) for other in others]
-    after = [lax.rem(other - place + (RING - 1), RING) for other in others]
+    decay8 = rate_ref[0]
+    gain8 = rate_ref[1, :, 0:1]
+    everything = jnp.sum(totals, axis=0, keepdims=True)
+    loop = 1.0 / (1.0 - jnp.exp(everything - (RING * rows) * decay8))
+    spots = jnp.zeros((8, 128), jnp.int32)
+    for index in range(RING):
+        spots = jnp.where(row8 == index, lax.bitwise_xor(place, masks[index]), spots)
+    ahead = lax.bitwise_and(place - spots + (RING - 1), RING - 1)
+    after = lax.bitwise_and(spots - place + (RING - 1), RING - 1)
     entering = jnp.zeros((8, width), F32)
     for index in range(RING):
-        fore = jnp.zeros((1, 128), F32)
-        back = jnp.zeros((1, 128), F32)
-        for other in range(RING):
-            fore = fore + jnp.where(ahead[other] < ahead[index], totals[other], 0.0)
-            back = back + jnp.where(after[other] < after[index], totals[other], 0.0)
-        fore = jnp.broadcast_to(fore, (8, 128)) - (ahead[index] * rows).astype(F32) * decay8
-        back = jnp.broadcast_to(back, (8, 128)) - (after[index] * rows).astype(F32) * decay8
-        share = jnp.exp(jnp.where(row8 < M, back, fore)) / loop
+        here = slice(index, index + 1)
+        fore = jnp.sum(jnp.where(ahead < ahead[here], totals, 0.0), axis=0, keepdims=True)
+        back = jnp.sum(jnp.where(after < after[here], totals, 0.0), axis=0, keepdims=True)
+        fore = fore - (ahead[here] * rows).astype(F32) * decay8
+        back = back - (after[here] * rows).astype(F32) * decay8
+        share = jnp.exp(jnp.where(row8 < M, back, fore)) * loop
         entering = entering + share[:, 0:1] * pieces[index][:, :width]
     whole = gain8 * (mark_ref[...] + entering * reach_ref[...])
     partial = jnp.concatenate([whole[:, :wide], whole[:, wide:]], axis=0)
@@ -567,16 +567,11 @@
     high, low = split_pair(partial)
     mixed_ref[LAYERS * rows : LAYERS * rows + 16, :] = high
     mixed_ref[LAYERS * rows + 16 : LAYERS * rows + 32, :] = low
-    _, sums, total = log_sums(keep_ref[...])
-    _, edges = mode_terms(sums, total, decay_ref, rows)
     weighted = entering * gain8 * jnp.concatenate([mode_ref[0], mode_ref[1]], axis=0)
-    edge_high = edges.astype(BF16).astype(F32)
-    edge_low = edges - edge_high
     in_high = weighted.astype(BF16).astype(F32)
     in_low = weighted - in_high
-    left = jnp.concatenate([edge_high, edge_high, edge_low, jnp.zeros_like(edges)], axis=0).astype(BF16)
     right = jnp.concatenate([in_high, in_low, in_high, jnp.zeros_like(in_high)], axis=0).astype(BF16)
-    gradient = local_ref[...] + dot_tn(left, right)
+    gradient = local_ref[...] + dot_tn(edge_ref[...], right)
 
     for layer in reversed(range(LAYERS)):
         narrow = gradient.astype(BF16)
@@ -746,20 +741,20 @@
     four, stream, reduced = lax.optimization_barrier((four, stream, reduced))
     got_four = hop_to(four, lambda core, place: (0, HOPS[2 - core]))
     reduced_far = swap(reduced, "dp", 1)
-    local, mark, reach = call(
+    local, mark, reach, edge, rate = call(
         local_body,
         (decay_rate, scale, cotangent, keep_share, mode_weight, stream),
         (SMEM, SMEM) + (VMEM,) * 4,
-        (((rows, width), F32), ((8, width), F32), ((8, width), F32)), size=1600 * GIGA
+        (((rows, width), F32), ((8, width), F32), ((8, width), F32), ((32, rows), BF16), ((2, 8, 128), F32)), size=1600 * GIGA
     )
     local, reduced_far = lax.optimization_barrier((local, reduced_far))
     gradient, mixed, partial = call(
         backward_body,
         (
-            decay_rate, scale, pay, got, got_two, got_four, keep_share, mode_weight, local, mark, reach,
+            pay, got, got_two, got_four, mode_weight, local, mark, reach, edge, rate,
             stream, inverse, slope, down_full, tap_full, up_weight, up_far,
         ),
-        (SMEM, SMEM) + (VMEM,) * 16,
+        (VMEM,) * 17,
         (((rows, width), F32), ((LAYERS * rows + 32, B), BF16), ((16, B), F32)), size=2100 * GIGA
     )
     mixed_far = swap(mixed, "dp", 1)

time: 41.2 us -> 40.5 us (0.983)
  Pallas kernels: 9.29 us -> 8.69 us
    pallas_call x11, Pallas kernels: 9.29 us -> 8.69 us  [call(): pl.pallas_call(body, out_shape=[jax.ShapeDtypeStruct(shape, dtype) for sh...]
  transfers between devices with their start and end apart: 13 -> 13, of which waited for: 9 -> 9; matrix products, arithmetic and copies ran while one was open for 0% -> 0% of each run, Pallas kernels for 16% -> 17%
where the time goes in v5:
time: 40.5 us; the launch traced here: 40.1 us
  starting transfers between devices  18.2 us (45%)
  waiting for transfers between devices  11.6 us (29%)
  Pallas kernels  8.69 us (21%)
  between operations  0.83 us (2%)
  other arithmetic  0.74 us (2%)
    ppermute x6, starting transfers between devices, hop_to(): return lax.ppermute(value, ('seq', 'dp'), pairs)  13.7 us
    pallas_call x11, Pallas kernels, call(): pl.pallas_call(body, out_shape=[jax.ShapeDtypeStruct(shape, dtype) for sh...  8.69 us
    ppermute x6, waiting for transfers between devices, hop_to(): return lax.ppermute(value, ('seq', 'dp'), pairs)  8.43 us
    ppermute x2, starting transfers between devices, wrapped_device(): parts.append(lax.ppermute(narrow, ('seq', 'dp'), pairs).astype(F32))  3.32 us
    ppermute x2, waiting for transfers between devices, wrapped_device(): parts.append(lax.ppermute(narrow, ('seq', 'dp'), pairs).astype(F32))  1.7 us
    ppermute x5, waiting for transfers between devices, swap(): lax.ppermute(value, axis, [(source, source ^ mask) for source in range(co...  1.47 us
    ppermute x5, starting transfers between devices, swap(): lax.ppermute(value, axis, [(source, source ^ mask) for source in range(co...  1.17 us
  transfers between devices with their start and end apart: 13, of which 9 were waited for; matrix products, arithmetic and copies ran while one was open for 0% of the time, Pallas kernels for 17%

profile of v5, /device:TPU:0, one launch (start us, length us, event | category | flops | bytes accessed | tf_op | source)
XLA Modules:
  0.0 40.1 jit_solution(1209546018776103475)
XLA Ops:
  0.6 0.5 %collective-permute-start.2 = (bf16[2,3,192,384]{3,2,1,0:T(8,128)(2,1)}, bf16[2,3,192,384]{3,2,1,0:T(8,128)(2,1)S(1)}, u32[]{:S(2)}, u32[]{:S(2)}) collective-permute-start(bf16[2,3,192,384]{3,2,1,0:T(8,128)(2,1)} %bitcast.2), channel_id=1, source_target_pairs={{0,1},{1,0},{2,3},{3,2},{4,5},{5,4},{6,7},{7,6},{8,9},{9,8},{10,11... | collective-permute-start | bytes 2654216 | tf_op jit(solution)/shard_map/ppermute | solution.py:682
  1.2 0.1 collective-permute-start.1
  1.3 0.4 %collective-permute-start.4 = (bf16[2,384,384]{2,1,0:T(8,128)(2,1)}, bf16[2,384,384]{2,1,0:T(8,128)(2,1)S(1)}, u32[]{:S(2)}, u32[]{:S(2)}) collective-permute-start(bf16[2,384,384]{2,1,0:T(8,128)(2,1)} %up_ref.3), channel_id=1, source_target_pairs={{0,1},{1,0},{2,3},{3,2},{4,5},{5,4},{6,7},{7,6},{8,9},{9,8},{10,11... | collective-permute-start | bytes 1769480 | tf_op jit(solution)/shard_map/ppermute | solution.py:682
  1.7 1.1 %shard_map.121.first_ref = bf16[1,8,896]{2,1,0:T(8,128)(2,1)S(1)} custom-call(bf16[1,128,768]{2,1,0:T(8,128)(2,1)} %cot_ref.1, f32[1,128]{1,0:T(1,128)} %keep_ref.1, f32[4]{0:T(128)} %decay_ref.1), custom_call_target="tpu_custom_call" | custom-call | flops 1300000000 | bytes 5078125 | tf_op jit(solution)/shard_map/pallas_call | solution.py:362
  2.8 3.8 %collective-permute-start = (bf16[1,8,896]{2,1,0:T(8,128)(2,1)S(1)}, bf16[1,8,896]{2,1,0:T(8,128)(2,1)S(1)}, u32[]{:S(2)}, u32[]{:S(2)}) collective-permute-start(bf16[1,8,896]{2,1,0:T(8,128)(2,1)S(1)} %shard_map.121.first_ref), channel_id=1, source_target_pairs={{0,8},{1,9},{2,10},{3,11},{4,12},{5,13},{6,14},{7,15},{8,0},{9,1},... | collective-permute-start | bytes 43016 | tf_op jit(solution)/shard_map/ppermute | solution.py:690
  6.5 0.0 copy-done.9
  6.6 1.7 %collective-permute-done.second_ref = bf16[1,8,896]{2,1,0:T(8,128)(2,1)S(1)} collective-permute-done((bf16[1,8,896]{2,1,0:T(8,128)(2,1)S(1)}, bf16[1,8,896]{2,1,0:T(8,128)(2,1)S(1)}, u32[]{:S(2)}, u32[]{:S(2)}) %collective-permute-start) | collective-permute-done | bytes 14368 | tf_op jit(solution)/shard_map/ppermute | solution.py:690
  8.3 0.0 copy-start.2
  8.3 0.0 copy-start.3
  8.3 0.0 copy-start.6
  8.3 0.0 collective-permute-done.1.down_far_ref
  8.3 0.0 collective-permute-done.2.tap_far_ref
  8.3 0.0 copy-done
  8.3 0.0 copy-done.1
  8.3 0.3 shard_map.122
  8.6 0.0 copy-start.8
  8.6 0.0 copy-start.4
  8.6 0.0 copy-start.5
  8.6 0.0 copy-start.7
  8.6 2.0 %collective-permute-start.3 = (bf16[2,8,896]{2,1,0:T(8,128)(2,1)S(1)}, bf16[2,8,896]{2,1,0:T(8,128)(2,1)S(1)}, u32[]{:S(2)}, u32[]{:S(2)}) collective-permute-start(bf16[2,8,896]{2,1,0:T(8,128)(2,1)S(1)} %pad_maximum_fusion.2), channel_id=1, source_target_pairs={{0,4},{1,3},{2,6},{3,1},{4,0},{5,7},{6,2},{7,5},{8,12},{9,11},{10,... | collective-permute-start | bytes 86024 | tf_op jit(solution)/shard_map/ppermute | solution.py:690
  10.6 0.0 collective-permute-done.4.up_far_ref
  10.6 0.0 copy-done.2
  10.6 0.0 copy-done.3
  10.6 0.0 copy-done.6
  10.6 1.8 %shard_map.123 = (f32[3,128,768]{2,1,0:T(8,128)S(1)}, f32[2,128,1]{2,1,0:T(8,128)S(1)}, bf16[256,384]{1,0:T(8,128)(2,1)S(1)}, f32[2,128,384]{2,1,0:T(8,128)S(1)}) custom-call(bf16[1,128,768]{2,1,0:T(8,128)(2,1)S(1)} %copy-done.3, s32[1,128]{1,0:T(1,128)S(1)} %copy-done.6, f32[1,768]{1,0:T(1,128)S(1)} %broadcast_in_dim.3.weight_ref, ...), custom_call_target="tpu_custom_call" | custom-call | flops 1800000000 | bytes 7031250 | tf_op jit(solution)/shard_map/pallas_call | solution.py:362
  12.5 0.1 collective-permute-done.3.third_ref
  12.6 0.1 collective-permute-start.5
  12.7 1.9 %collective-permute-start.6 = (bf16[4,8,896]{2,1,0:T(8,128)(2,1)S(1)}, bf16[4,8,896]{2,1,0:T(8,128)(2,1)S(1)}, u32[]{:S(2)}, u32[]{:S(2)}) collective-permute-start(bf16[4,8,896]{2,1,0:T(8,128)(2,1)S(1)} %pad_maximum_fusion.1), channel_id=1, source_target_pairs={{0,2},{1,5},{2,0},{3,7},{4,6},{5,1},{6,4},{7,3},{8,10},{9,13},{10,... | collective-permute-start | bytes 172040 | tf_op jit(solution)/shard_map/ppermute | solution.py:690
  14.6 1.5 %shard_map.124 = (f32[128,768]{1,0:T(8,128)S(1)}, f32[8,768]{1,0:T(8,128)S(1)}, f32[8,768]{1,0:T(8,128)S(1)}, bf16[32,128]{1,0:T(8,128)(2,1)S(1)}, f32[2,8,128]{2,1,0:T(8,128)S(1)}) custom-call(f32[4]{0:T(128)S(1)} %copy-done.8, f32[4]{0:T(128)S(1)} %negate_sqrt_fusion.scale_ref, bf16[1,128,768]{2,1,0:T(8,128)(2,1)S(1)} %copy-done.4, ...), custom_call_target="tpu_custom_call" | custom-call | flops 1600000000 | bytes 6250000 | tf_op jit(solution)/shard_map/pallas_call | solution.py:362
  16.1 0.0 collective-permute-done.5.reduced_far_ref
  16.1 0.8 %collective-permute-done.6.fourth_ref = bf16[4,8,896]{2,1,0:T(8,128)(2,1)S(1)} collective-permute-done((bf16[4,8,896]{2,1,0:T(8,128)(2,1)S(1)}, bf16[4,8,896]{2,1,0:T(8,128)(2,1)S(1)}, u32[]{:S(2)}, u32[]{:S(2)}) %collective-permute-start.6) | collective-permute-done | bytes 57376 | tf_op jit(solution)/shard_map/ppermute | solution.py:690
  16.9 1.5 %shard_map.125 = (f32[128,768]{1,0:T(8,128)S(1)}, bf16[288,384]{1,0:T(8,128)(2,1)S(1)}, f32[16,384]{1,0:T(8,128)S(1)}) custom-call(bf16[1,8,896]{2,1,0:T(8,128)(2,1)S(1)} %shard_map.121.first_ref, bf16[1,8,896]{2,1,0:T(8,128)(2,1)S(1)} %collective-permute-done.second_ref, bf16[2,8,896]{2,1,0:T(8,128)(2,1)S(1)} %collective-permute-done.3.third_ref, ...), custom_call_target="tpu_custom_call" | custom-call | flops 2100000000 | bytes 8203125 | tf_op jit(solution)/shard_map/pallas_call | solution.py:362
  18.4 0.1 collective-permute-start.7
  18.5 1.5 %collective-permute-done.7.mixed_far_ref = bf16[288,384]{1,0:T(8,128)(2,1)S(1)} collective-permute-done((bf16[288,384]{1,0:T(8,128)(2,1)S(1)}, bf16[288,384]{1,0:T(8,128)(2,1)S(1)}, u32[]{:S(2)}, u32[]{:S(2)}) %collective-permute-start.7) | collective-permute-done | bytes 221216 | tf_op jit(solution)/shard_map/ppermute | solution.py:682
  20.0 0.4 %shard_map.126 = (f32[192,384]{1,0:T(8,128)S(1)}, bf16[208,384]{1,0:T(8,128)(2,1)S(1)}, f32[16,384]{1,0:T(8,128)S(1)}) custom-call(bf16[256,384]{1,0:T(8,128)(2,1)S(1)} %get-tuple-element.45.reduced_ref, bf16[256,384]{1,0:T(8,128)(2,1)S(1)} %collective-permute-done.5.reduced_far_ref, bf16[288,384]{1,0:T(8,128)(2,1)S(1)} %get-tuple-element.57.mixed_ref, ...), custom_call_target="tpu_custom_call" | custom-call | flops 500000000 | bytes 1953125 | tf_op jit(solution)/shard_map/pallas_call | solution.py:362
  20.4 1.6 %collective-permute-start.8 = (bf16[208,384]{1,0:T(8,128)(2,1)S(1)}, bf16[208,384]{1,0:T(8,128)(2,1)S(1)}, u32[]{:S(2)}, u32[]{:S(2)}) collective-permute-start(bf16[208,384]{1,0:T(8,128)(2,1)S(1)} %get-tuple-element.60), channel_id=1, source_target_pairs={{0,3},{1,4},{2,7},{3,0},{4,1},{5,6},{6,5},{7,2},{8,13},{9,10},{10,... | collective-permute-start | bytes 479240 | tf_op jit(solution)/shard_map/ppermute | solution.py:690
  22.1 1.3 %shard_map.128 = bf16[1,128,768]{2,1,0:T(8,128)(2,1)} custom-call(f32[128,768]{1,0:T(8,128)S(1)} %get-tuple-element.63.gradient_ref, bf16[288,384]{1,0:T(8,128)(2,1)S(1)} %get-tuple-element.57.mixed_ref, f32[3,128,768]{2,1,0:T(8,128)S(1)} %get-tuple-element.46.stream_ref, f32[2,128,1]{2,1,0:T(8,128)S(1)} %get-tuple-element.55.inverse_ref, ...), custom_call_target="tpu_custom_call" | custom-call | flops 1300000000 | bytes 5078125 | tf_op jit(solution)/shard_map/pallas_call | solution.py:362
  23.4 1.8 %collective-permute-done.8.got_ref = bf16[208,384]{1,0:T(8,128)(2,1)S(1)} collective-permute-done((bf16[208,384]{1,0:T(8,128)(2,1)S(1)}, bf16[208,384]{1,0:T(8,128)(2,1)S(1)}, u32[]{:S(2)}, u32[]{:S(2)}) %collective-permute-start.8) | collective-permute-done | bytes 159776 | tf_op jit(solution)/shard_map/ppermute | solution.py:690
  25.2 1.7 %collective-permute-start.9 = (bf16[112,384]{1,0:T(8,128)(2,1)S(1)}, bf16[112,384]{1,0:T(8,128)(2,1)S(1)}, u32[]{:S(2)}, u32[]{:S(2)}) collective-permute-start(bf16[112,384]{1,0:T(8,128)(2,1)S(1)} %get-tuple-element.66), channel_id=1, source_target_pairs={{0,5},{1,2},{2,1},{3,6},{4,7},{5,0},{6,3},{7,4},{8,11},{9,12},{10,... | collective-permute-start | bytes 258056 | tf_op jit(solution)/shard_map/ppermute | solution.py:690
  27.0 2.3 %collective-permute-done.9.got_ref = bf16[112,384]{1,0:T(8,128)(2,1)S(1)} collective-permute-done((bf16[112,384]{1,0:T(8,128)(2,1)S(1)}, bf16[112,384]{1,0:T(8,128)(2,1)S(1)}, u32[]{:S(2)}, u32[]{:S(2)}) %collective-permute-start.9) | collective-permute-done | bytes 86048 | tf_op jit(solution)/shard_map/ppermute | solution.py:690
  29.2 2.7 %collective-permute-start.10 = (bf16[56,384]{1,0:T(8,128)(2,1)S(1)}, bf16[56,384]{1,0:T(8,128)(2,1)S(1)}, u32[]{:S(2)}, u32[]{:S(2)}) collective-permute-start(bf16[56,384]{1,0:T(8,128)(2,1)S(1)} %get-tuple-element.69), channel_id=1, source_target_pairs={{0,9},{1,8},{2,11},{3,10},{4,13},{5,12},{6,15},{7,14},{8,1},{9,0},... | collective-permute-start | bytes 129032 | tf_op jit(solution)/shard_map/ppermute | solution.py:690
  32.0 1.7 %collective-permute-done.10.got_ref = bf16[56,384]{1,0:T(8,128)(2,1)S(1)} collective-permute-done((bf16[56,384]{1,0:T(8,128)(2,1)S(1)}, bf16[56,384]{1,0:T(8,128)(2,1)S(1)}, u32[]{:S(2)}, u32[]{:S(2)}) %collective-permute-start.10) | collective-permute-done | bytes 43040 | tf_op jit(solution)/shard_map/ppermute | solution.py:690
  33.7 2.0 %collective-permute-start.12 = (bf16[48,384]{1,0:T(8,128)(2,1)S(1)}, bf16[48,384]{1,0:T(8,128)(2,1)S(1)}, u32[]{:S(2)}, u32[]{:S(2)}) collective-permute-start(bf16[48,384]{1,0:T(8,128)(2,1)S(1)} %get-tuple-element.71), channel_id=1, source_target_pairs={{6,0},{7,1},{0,2},{1,3},{2,4},{3,5},{4,6},{5,7},{14,8},{15,9},{8,1... | collective-permute-start | bytes 110600 | tf_op jit(solution)/shard_map/ppermute | solution.py:802
  35.7 1.3 %collective-permute-start.11 = (bf16[48,384]{1,0:T(8,128)(2,1)S(1)}, bf16[48,384]{1,0:T(8,128)(2,1)S(1)}, u32[]{:S(2)}, u32[]{:S(2)}) collective-permute-start(bf16[48,384]{1,0:T(8,128)(2,1)S(1)} %get-tuple-element.71), channel_id=1, source_target_pairs={{3,0},{4,1},{5,2},{6,3},{7,4},{0,5},{1,6},{2,7},{11,8},{12,9},{13,... | collective-permute-start | bytes 110600 | tf_op jit(solution)/shard_map/ppermute | solution.py:802
  37.0 0.7 %shard_map.131 = f32[8,48]{1,0:T(8,128)} custom-call(bf16[56,384]{1,0:T(8,128)(2,1)S(1)} %collective-permute-done.10.got_ref, f32[8,384]{1,0:T(8,128)S(1)} %get-tuple-element.72.partial_ref), custom_call_target="tpu_custom_call" | custom-call | tf_op jit(solution)/shard_map/pallas_call | solution.py:362
  37.7 1.3 %collective-permute-done.12 = bf16[48,384]{1,0:T(8,128)(2,1)S(1)} collective-permute-done((bf16[48,384]{1,0:T(8,128)(2,1)S(1)}, bf16[48,384]{1,0:T(8,128)(2,1)S(1)}, u32[]{:S(2)}, u32[]{:S(2)}) %collective-permute-start.12) | collective-permute-done | bytes 36896 | tf_op jit(solution)/shard_map/ppermute | solution.py:802
  39.0 0.4 collective-permute-done.11
  39.4 0.7 %pad_maximum_fusion = f32[144,384]{1,0:T(8,128)} fusion(f32[48,384]{1,0:T(8,128)S(1)} %convert_element_type.7, f32[48,384]{1,0:T(8,128)S(1)} %convert_element_type.6, f32[48,384]{1,0:T(8,128)S(1)} %get-tuple-element.70), kind=kLoop, calls=%fused_computation | loop fusion | flops 110592 | bytes 442368 | tf_op jit(solution)/shard_map/concatenate | solution.py:806
  (16 shorter events, 0.1 us)
Async XLA Ops:
  0.6 7.7 %collective-permute-start.2 = (bf16[2,3,192,384]{3,2,1,0:T(8,128)(2,1)}, bf16[2,3,192,384]{3,2,1,0:T(8,128)(2,1)S(1)}, u32[]{:S(2)}, u32[]{:S(2)}) collective-permute-start(bf16[2,3,192,384]{3,2,1,0:T(8,128)(2,1)} %bitcast.2), channel_id=1, source_target_pairs={{0,1},{1,0},{2,3},{3,2},{4,5},{5,4},{6,7},{7,6},{8,9},{9,8},{10,11... | collective-permute-start | bytes 2654216 | tf_op jit(solution)/shard_map/ppermute | solution.py:682
  1.1 5.4 %copy-start.9 = (f32[768]{0:T(1024)S(1)}, f32[768]{0:T(1024)}, u32[]{:S(2)}) copy-start(f32[768]{0:T(1024)} %param.13) | copy-start | bytes 9220
  1.2 7.2 %copy-start = (bf16[2,3,384,192]{2,3,1,0:T(8,128)(2,1)S(1)}, bf16[2,3,384,192]{2,3,1,0:T(8,128)(2,1)}, u32[]{:S(2)}) copy-start(bf16[2,3,384,192]{2,3,1,0:T(8,128)(2,1)} %param.15) | copy-start | bytes 2654212
  1.2 7.2 %copy-start.1 = (bf16[2,768,192]{1,2,0:T(8,128)(2,1)S(1)}, bf16[2,768,192]{1,2,0:T(8,128)(2,1)}, u32[]{:S(2)}) copy-start(bf16[2,768,192]{1,2,0:T(8,128)(2,1)} %param.14) | copy-start | bytes 1769476
  1.2 7.1 %collective-permute-start.1 = (bf16[2,192,768]{2,1,0:T(8,128)(2,1)}, bf16[2,192,768]{2,1,0:T(8,128)(2,1)S(1)}, u32[]{:S(2)}, u32[]{:S(2)}) collective-permute-start(bf16[2,192,768]{2,1,0:T(8,128)(2,1)} %bitcast.4), channel_id=1, source_target_pairs={{0,1},{1,0},{2,3},{3,2},{4,5},{5,4},{6,7},{7,6},{8,9},{9,8},{10,11... | collective-permute-start | bytes 1769480 | tf_op jit(solution)/shard_map/ppermute | solution.py:682
  1.3 9.4 %collective-permute-start.4 = (bf16[2,384,384]{2,1,0:T(8,128)(2,1)}, bf16[2,384,384]{2,1,0:T(8,128)(2,1)S(1)}, u32[]{:S(2)}, u32[]{:S(2)}) collective-permute-start(bf16[2,384,384]{2,1,0:T(8,128)(2,1)} %up_ref.3), channel_id=1, source_target_pairs={{0,1},{1,0},{2,3},{3,2},{4,5},{5,4},{6,7},{7,6},{8,9},{9,8},{10,11... | collective-permute-start | bytes 1769480 | tf_op jit(solution)/shard_map/ppermute | solution.py:682
  2.8 5.4 %collective-permute-start = (bf16[1,8,896]{2,1,0:T(8,128)(2,1)S(1)}, bf16[1,8,896]{2,1,0:T(8,128)(2,1)S(1)}, u32[]{:S(2)}, u32[]{:S(2)}) collective-permute-start(bf16[1,8,896]{2,1,0:T(8,128)(2,1)S(1)} %shard_map.121.first_ref), channel_id=1, source_target_pairs={{0,8},{1,9},{2,10},{3,11},{4,12},{5,13},{6,14},{7,15},{8,0},{9,1},... | collective-permute-start | bytes 43016 | tf_op jit(solution)/shard_map/ppermute | solution.py:690
  8.3 2.4 %copy-start.2 = (bf16[2,384,384]{2,1,0:T(8,128)(2,1)S(1)}, bf16[2,384,384]{2,1,0:T(8,128)(2,1)}, u32[]{:S(2)}) copy-start(bf16[2,384,384]{2,1,0:T(8,128)(2,1)} %up_ref.3) | copy-start | bytes 1769476
  8.3 2.4 %copy-start.3 = (bf16[1,128,768]{2,1,0:T(8,128)(2,1)S(1)}, bf16[1,128,768]{2,1,0:T(8,128)(2,1)}, u32[]{:S(2)}) copy-start(bf16[1,128,768]{2,1,0:T(8,128)(2,1)} %feature_ref.1) | copy-start | bytes 589828
  8.3 2.4 %copy-start.6 = (s32[1,128]{1,0:T(1,128)S(1)}, s32[1,128]{1,0:T(1,128)}, u32[]{:S(2)}) copy-start(s32[1,128]{1,0:T(1,128)} %count_ref.1) | copy-start | bytes 1540
  8.6 4.1 %copy-start.8 = (f32[4]{0:T(128)S(1)}, f32[4]{0:T(128)}, u32[]{:S(2)}) copy-start(f32[4]{0:T(128)} %decay_ref.1) | copy-start | bytes 52
  8.6 6.0 %copy-start.4 = (bf16[1,128,768]{2,1,0:T(8,128)(2,1)S(1)}, bf16[1,128,768]{2,1,0:T(8,128)(2,1)}, u32[]{:S(2)}) copy-start(bf16[1,128,768]{2,1,0:T(8,128)(2,1)} %cot_ref.1) | copy-start | bytes 589828
  8.6 6.0 %copy-start.5 = (f32[2,4,768]{2,1,0:T(4,128)S(1)}, f32[2,4,768]{2,1,0:T(4,128)}, u32[]{:S(2)}) copy-start(f32[2,4,768]{2,1,0:T(4,128)} %mode_ref.3) | copy-start | bytes 73732
  8.6 6.0 %copy-start.7 = (f32[1,128]{1,0:T(1,128)S(1)}, f32[1,128]{1,0:T(1,128)}, u32[]{:S(2)}) copy-start(f32[1,128]{1,0:T(1,128)} %keep_ref.1) | copy-start | bytes 1540
  8.6 3.9 %collective-permute-start.3 = (bf16[2,8,896]{2,1,0:T(8,128)(2,1)S(1)}, bf16[2,8,896]{2,1,0:T(8,128)(2,1)S(1)}, u32[]{:S(2)}, u32[]{:S(2)}) collective-permute-start(bf16[2,8,896]{2,1,0:T(8,128)(2,1)S(1)} %pad_maximum_fusion.2), channel_id=1, source_target_pairs={{0,4},{1,3},{2,6},{3,1},{4,0},{5,7},{6,2},{7,5},{8,12},{9,11},{10,... | collective-permute-start | bytes 86024 | tf_op jit(solution)/shard_map/ppermute | solution.py:690
  12.6 3.5 %collective-permute-start.5 = (bf16[256,384]{1,0:T(8,128)(2,1)S(1)}, bf16[256,384]{1,0:T(8,128)(2,1)S(1)}, u32[]{:S(2)}, u32[]{:S(2)}) collective-permute-start(bf16[256,384]{1,0:T(8,128)(2,1)S(1)} %get-tuple-element.45.reduced_ref), channel_id=1, source_target_pairs={{0,1},{1,0},{2,3},{3,2},{4,5},{5,4},{6,7},{7,6},{8,9},{9,8},{10,11... | collective-permute-start | bytes 589832 | tf_op jit(solution)/shard_map/ppermute | solution.py:682
  12.7 4.2 %collective-permute-start.6 = (bf16[4,8,896]{2,1,0:T(8,128)(2,1)S(1)}, bf16[4,8,896]{2,1,0:T(8,128)(2,1)S(1)}, u32[]{:S(2)}, u32[]{:S(2)}) collective-permute-start(bf16[4,8,896]{2,1,0:T(8,128)(2,1)S(1)} %pad_maximum_fusion.1), channel_id=1, source_target_pairs={{0,2},{1,5},{2,0},{3,7},{4,6},{5,1},{6,4},{7,3},{8,10},{9,13},{10,... | collective-permute-start | bytes 172040 | tf_op jit(solution)/shard_map/ppermute | solution.py:690
  18.4 1.5 %collective-permute-start.7 = (bf16[288,384]{1,0:T(8,128)(2,1)S(1)}, bf16[288,384]{1,0:T(8,128)(2,1)S(1)}, u32[]{:S(2)}, u32[]{:S(2)}) collective-permute-start(bf16[288,384]{1,0:T(8,128)(2,1)S(1)} %get-tuple-element.57.mixed_ref), channel_id=1, source_target_pairs={{0,1},{1,0},{2,3},{3,2},{4,5},{5,4},{6,7},{7,6},{8,9},{9,8},{10,11... | collective-permute-start | bytes 663560 | tf_op jit(solution)/shard_map/ppermute | solution.py:682
  20.4 4.8 %collective-permute-start.8 = (bf16[208,384]{1,0:T(8,128)(2,1)S(1)}, bf16[208,384]{1,0:T(8,128)(2,1)S(1)}, u32[]{:S(2)}, u32[]{:S(2)}) collective-permute-start(bf16[208,384]{1,0:T(8,128)(2,1)S(1)} %get-tuple-element.60), channel_id=1, source_target_pairs={{0,3},{1,4},{2,7},{3,0},{4,1},{5,6},{6,5},{7,2},{8,13},{9,10},{10,... | collective-permute-start | bytes 479240 | tf_op jit(solution)/shard_map/ppermute | solution.py:690
  25.2 4.0 %collective-permute-start.9 = (bf16[112,384]{1,0:T(8,128)(2,1)S(1)}, bf16[112,384]{1,0:T(8,128)(2,1)S(1)}, u32[]{:S(2)}, u32[]{:S(2)}) collective-permute-start(bf16[112,384]{1,0:T(8,128)(2,1)S(1)} %get-tuple-element.66), channel_id=1, source_target_pairs={{0,5},{1,2},{2,1},{3,6},{4,7},{5,0},{6,3},{7,4},{8,11},{9,12},{10,... | collective-permute-start | bytes 258056 | tf_op jit(solution)/shard_map/ppermute | solution.py:690
  29.2 4.4 %collective-permute-start.10 = (bf16[56,384]{1,0:T(8,128)(2,1)S(1)}, bf16[56,384]{1,0:T(8,128)(2,1)S(1)}, u32[]{:S(2)}, u32[]{:S(2)}) collective-permute-start(bf16[56,384]{1,0:T(8,128)(2,1)S(1)} %get-tuple-element.69), channel_id=1, source_target_pairs={{0,9},{1,8},{2,11},{3,10},{4,13},{5,12},{6,15},{7,14},{8,1},{9,0},... | collective-permute-start | bytes 129032 | tf_op jit(solution)/shard_map/ppermute | solution.py:690
  33.7 5.3 %collective-permute-start.12 = (bf16[48,384]{1,0:T(8,128)(2,1)S(1)}, bf16[48,384]{1,0:T(8,128)(2,1)S(1)}, u32[]{:S(2)}, u32[]{:S(2)}) collective-permute-start(bf16[48,384]{1,0:T(8,128)(2,1)S(1)} %get-tuple-element.71), channel_id=1, source_target_pairs={{6,0},{7,1},{0,2},{1,3},{2,4},{3,5},{4,6},{5,7},{14,8},{15,9},{8,1... | collective-permute-start | bytes 110600 | tf_op jit(solution)/shard_map/ppermute | solution.py:802
  35.7 3.7 %collective-permute-start.11 = (bf16[48,384]{1,0:T(8,128)(2,1)S(1)}, bf16[48,384]{1,0:T(8,128)(2,1)S(1)}, u32[]{:S(2)}, u32[]{:S(2)}) collective-permute-start(bf16[48,384]{1,0:T(8,128)(2,1)S(1)} %get-tuple-element.71), channel_id=1, source_target_pairs={{3,0},{4,1},{5,2},{6,3},{7,4},{0,5},{1,6},{2,7},{11,8},{12,9},{13,... | collective-permute-start | bytes 110600 | tf_op jit(solution)/shard_map/ppermute | solution.py:802

commit v6 on v5

--- a/solution.py
+++ b/solution.py
@@ -355,6 +355,8 @@
 RING = 8
 HOPS = (4, 2, 1)
 BLOCK = 48
+OWNED = (0, 5, 7, 3, 4, 1, 2, 6)
+SOURCES = ((6, 3, 7, 5, 1, 0, 4, 2), (5, 4, 0, 6, 7, 2, 3, 1))
 GIGA = 10**6
 
 
@@ -602,9 +604,14 @@
     grad_ref[0] = gradient.astype(BF16)
 
 
+def entry_of(table, index):
+    packed = sum(value << (3 * place) for place, value in enumerate(table))
+    return lax.bitwise_and(lax.shift_right_logical(jnp.int32(packed), jnp.int32(3) * index), jnp.int32(7))
+
+
 def held_block(parity, bit_x, bit_z, layer):
     core = lax.bitwise_xor(lax.bitwise_xor(parity, bit_x), lax.bitwise_xor(bit_z, layer))
-    return pl.multiple_of(lax.rem(3 * core + 6 * bit_x + 4 * bit_z, RING) * BLOCK, BLOCK)
+    return pl.multiple_of(entry_of(OWNED, 4 * bit_z + 2 * bit_x + core) * BLOCK, BLOCK)
 
 
 def taps_body(
@@ -669,6 +676,14 @@
     send_out[...] = block.astype(BF16)
 
 
+def place_body(own_ref, first_ref, second_ref, out_ref):
+    number = lax.rem(2 * lax.axis_index("seq") + lax.axis_index("dp"), 8)
+    held = (range(8),) + SOURCES
+    for table, ref in zip(held, (own_ref, first_ref, second_ref)):
+        spots = [(OWNED[table[j]] - 3 * j) % 8 for j in range(8)]
+        out_ref[pl.ds(pl.multiple_of(entry_of(spots, number) * BLOCK, BLOCK), BLOCK), :] = ref[...].astype(F32)
+
+
 def modes_body(scale, got_ref, partial_ref, mode_out):
     rows = got_ref.shape[0] - 8
     full = (partial_ref[...] + got_ref[rows : rows + 8, :].astype(F32)) * scale
@@ -796,14 +811,15 @@
         (VMEM,) * 2,
         (((BLOCK, B), F32), ((BLOCK, B), BF16)),
     )
-    parts = [block]
-    for step in (3, 6):
-        pairs = [(8 * layer + (j + step) % 8, 8 * layer + j) for layer in range(LAYERS) for j in range(8)]
-        parts.append(lax.ppermute(narrow, ("seq", "dp"), pairs).astype(F32))
+    parts = []
+    for table in SOURCES:
+        pairs = [(8 * layer + table[j], 8 * layer + j) for layer in range(LAYERS) for j in range(8)]
+        parts.append(lax.ppermute(narrow, ("seq", "dp"), pairs))
     (mode_sum,) = call(
         functools.partial(modes_body, report), (got, partial), (VMEM,) * 2, (((8, BLOCK), F32),)
     )
-    return grad, jnp.concatenate(parts, axis=0), mode_sum
+    (taps_sum,) = call(place_body, (block, *parts), (VMEM,) * 3, (((3 * BLOCK, B), F32),))
+    return grad, taps_sum, mode_sum
 
 
 def solution(mesh):

time: 40.5 us -> 40.1 us (level)
  Pallas kernels: 8.69 us -> 9.41 us
  other arithmetic: 0.74 us -> 0.03 us
  waiting for transfers between devices: 11.6 us -> 11.1 us
    pallas_call x11 -> x12, Pallas kernels: 8.69 us -> 9.41 us  [call(): pl.pallas_call(body, out_shape=[jax.ShapeDtypeStruct(shape, dtype) for sh...]
    concatenate x1 -> x0, other arithmetic: 0.7 us -> none  [wrapped_device(): return (grad, jnp.concatenate(parts, axis=0), mode_sum)]
    ppermute x2, waiting for transfers between devices: 1.7 us -> 1.23 us  [wrapped_device(): parts.append(lax.ppermute(narrow, ('seq', 'dp'), pairs))]
where the time goes in v6:
time: 40.1 us; the launch traced here: 39.9 us
  starting transfers between devices  18.4 us (46%)
  waiting for transfers between devices  11.1 us (28%)
  Pallas kernels  9.41 us (23%)
  between operations  0.83 us (2%)
    ppermute x6, starting transfers between devices, hop_to(): return lax.ppermute(value, ('seq', 'dp'), pairs)  13.7 us
    pallas_call x12, Pallas kernels, call(): pl.pallas_call(body, out_shape=[jax.ShapeDtypeStruct(shape, dtype) for sh...  9.41 us
    ppermute x6, waiting for transfers between devices, hop_to(): return lax.ppermute(value, ('seq', 'dp'), pairs)  8.42 us
    ppermute x2, starting transfers between devices, wrapped_device(): parts.append(lax.ppermute(narrow, ('seq', 'dp'), pairs))  3.6 us
    ppermute x5, waiting for transfers between devices, swap(): lax.ppermute(value, axis, [(source, source ^ mask) for source in range(co...  1.47 us
    ppermute x2, waiting for transfers between devices, wrapped_device(): parts.append(lax.ppermute(narrow, ('seq', 'dp'), pairs))  1.23 us
    ppermute x5, starting transfers between devices, swap(): lax.ppermute(value, axis, [(source, source ^ mask) for source in range(co...  1.17 us
  transfers between devices with their start and end apart: 13, of which 9 were waited for; matrix products, arithmetic and copies ran while one was open for 0% of the time, Pallas kernels for 17%

profile of v6, /device:TPU:0, one launch (start us, length us, event | category | flops | bytes accessed | tf_op | source)
XLA Modules:
  0.0 39.9 jit_solution(12912736857779676335)
XLA Ops:
  0.6 0.5 %collective-permute-start.2 = (bf16[2,3,192,384]{3,2,1,0:T(8,128)(2,1)}, bf16[2,3,192,384]{3,2,1,0:T(8,128)(2,1)S(1)}, u32[]{:S(2)}, u32[]{:S(2)}) collective-permute-start(bf16[2,3,192,384]{3,2,1,0:T(8,128)(2,1)} %bitcast.2), channel_id=1, source_target_pairs={{0,1},{1,0},{2,3},{3,2},{4,5},{5,4},{6,7},{7,6},{8,9},{9,8},{10,11... | collective-permute-start | bytes 2654216 | tf_op jit(solution)/shard_map/ppermute | solution.py:697
  1.2 0.1 collective-permute-start.1
  1.3 0.4 %collective-permute-start.4 = (bf16[2,384,384]{2,1,0:T(8,128)(2,1)}, bf16[2,384,384]{2,1,0:T(8,128)(2,1)S(1)}, u32[]{:S(2)}, u32[]{:S(2)}) collective-permute-start(bf16[2,384,384]{2,1,0:T(8,128)(2,1)} %up_ref.3), channel_id=1, source_target_pairs={{0,1},{1,0},{2,3},{3,2},{4,5},{5,4},{6,7},{7,6},{8,9},{9,8},{10,11... | collective-permute-start | bytes 1769480 | tf_op jit(solution)/shard_map/ppermute | solution.py:697
  1.7 1.1 %shard_map.121.first_ref = bf16[1,8,896]{2,1,0:T(8,128)(2,1)S(1)} custom-call(bf16[1,128,768]{2,1,0:T(8,128)(2,1)} %cot_ref.1, f32[1,128]{1,0:T(1,128)} %keep_ref.1, f32[4]{0:T(128)} %decay_ref.1), custom_call_target="tpu_custom_call" | custom-call | flops 1300000000 | bytes 5078125 | tf_op jit(solution)/shard_map/pallas_call | solution.py:364
  2.8 3.8 %collective-permute-start = (bf16[1,8,896]{2,1,0:T(8,128)(2,1)S(1)}, bf16[1,8,896]{2,1,0:T(8,128)(2,1)S(1)}, u32[]{:S(2)}, u32[]{:S(2)}) collective-permute-start(bf16[1,8,896]{2,1,0:T(8,128)(2,1)S(1)} %shard_map.121.first_ref), channel_id=1, source_target_pairs={{0,8},{1,9},{2,10},{3,11},{4,12},{5,13},{6,14},{7,15},{8,0},{9,1},... | collective-permute-start | bytes 43016 | tf_op jit(solution)/shard_map/ppermute | solution.py:705
  6.5 0.0 copy-done.9
  6.6 1.7 %collective-permute-done.second_ref = bf16[1,8,896]{2,1,0:T(8,128)(2,1)S(1)} collective-permute-done((bf16[1,8,896]{2,1,0:T(8,128)(2,1)S(1)}, bf16[1,8,896]{2,1,0:T(8,128)(2,1)S(1)}, u32[]{:S(2)}, u32[]{:S(2)}) %collective-permute-start) | collective-permute-done | bytes 14368 | tf_op jit(solution)/shard_map/ppermute | solution.py:705
  8.3 0.0 copy-start.2
  8.3 0.0 copy-start.3
  8.3 0.0 copy-start.6
  8.3 0.0 collective-permute-done.1.down_far_ref
  8.3 0.0 collective-permute-done.2.tap_far_ref
  8.3 0.0 copy-done
  8.3 0.0 copy-done.1
  8.3 0.3 shard_map.122
  8.6 0.0 copy-start.8
  8.6 0.0 copy-start.4
  8.6 0.0 copy-start.5
  8.6 0.0 copy-start.7
  8.6 2.0 %collective-permute-start.3 = (bf16[2,8,896]{2,1,0:T(8,128)(2,1)S(1)}, bf16[2,8,896]{2,1,0:T(8,128)(2,1)S(1)}, u32[]{:S(2)}, u32[]{:S(2)}) collective-permute-start(bf16[2,8,896]{2,1,0:T(8,128)(2,1)S(1)} %pad_maximum_fusion.1), channel_id=1, source_target_pairs={{0,4},{1,3},{2,6},{3,1},{4,0},{5,7},{6,2},{7,5},{8,12},{9,11},{10,... | collective-permute-start | bytes 86024 | tf_op jit(solution)/shard_map/ppermute | solution.py:705
  10.6 0.0 collective-permute-done.4.up_far_ref
  10.6 0.0 copy-done.2
  10.6 0.0 copy-done.3
  10.6 0.0 copy-done.6
  10.6 1.8 %shard_map.123 = (f32[3,128,768]{2,1,0:T(8,128)S(1)}, f32[2,128,1]{2,1,0:T(8,128)S(1)}, bf16[256,384]{1,0:T(8,128)(2,1)S(1)}, f32[2,128,384]{2,1,0:T(8,128)S(1)}) custom-call(bf16[1,128,768]{2,1,0:T(8,128)(2,1)S(1)} %copy-done.3, s32[1,128]{1,0:T(1,128)S(1)} %copy-done.6, f32[1,768]{1,0:T(1,128)S(1)} %broadcast_in_dim.3.weight_ref, ...), custom_call_target="tpu_custom_call" | custom-call | flops 1800000000 | bytes 7031250 | tf_op jit(solution)/shard_map/pallas_call | solution.py:364
  12.5 0.1 collective-permute-done.3.third_ref
  12.6 0.1 collective-permute-start.5
  12.7 1.9 %collective-permute-start.6 = (bf16[4,8,896]{2,1,0:T(8,128)(2,1)S(1)}, bf16[4,8,896]{2,1,0:T(8,128)(2,1)S(1)}, u32[]{:S(2)}, u32[]{:S(2)}) collective-permute-start(bf16[4,8,896]{2,1,0:T(8,128)(2,1)S(1)} %pad_maximum_fusion), channel_id=1, source_target_pairs={{0,2},{1,5},{2,0},{3,7},{4,6},{5,1},{6,4},{7,3},{8,10},{9,13},{10,... | collective-permute-start | bytes 172040 | tf_op jit(solution)/shard_map/ppermute | solution.py:705
  14.6 1.5 %shard_map.124 = (f32[128,768]{1,0:T(8,128)S(1)}, f32[8,768]{1,0:T(8,128)S(1)}, f32[8,768]{1,0:T(8,128)S(1)}, bf16[32,128]{1,0:T(8,128)(2,1)S(1)}, f32[2,8,128]{2,1,0:T(8,128)S(1)}) custom-call(f32[4]{0:T(128)S(1)} %copy-done.8, f32[4]{0:T(128)S(1)} %negate_sqrt_fusion.scale_ref, bf16[1,128,768]{2,1,0:T(8,128)(2,1)S(1)} %copy-done.4, ...), custom_call_target="tpu_custom_call" | custom-call | flops 1600000000 | bytes 6250000 | tf_op jit(solution)/shard_map/pallas_call | solution.py:364
  16.1 0.0 collective-permute-done.5.reduced_far_ref
  16.1 0.8 %collective-permute-done.6.fourth_ref = bf16[4,8,896]{2,1,0:T(8,128)(2,1)S(1)} collective-permute-done((bf16[4,8,896]{2,1,0:T(8,128)(2,1)S(1)}, bf16[4,8,896]{2,1,0:T(8,128)(2,1)S(1)}, u32[]{:S(2)}, u32[]{:S(2)}) %collective-permute-start.6) | collective-permute-done | bytes 57376 | tf_op jit(solution)/shard_map/ppermute | solution.py:705
  16.9 1.5 %shard_map.125 = (f32[128,768]{1,0:T(8,128)S(1)}, bf16[288,384]{1,0:T(8,128)(2,1)S(1)}, f32[16,384]{1,0:T(8,128)S(1)}) custom-call(bf16[1,8,896]{2,1,0:T(8,128)(2,1)S(1)} %shard_map.121.first_ref, bf16[1,8,896]{2,1,0:T(8,128)(2,1)S(1)} %collective-permute-done.second_ref, bf16[2,8,896]{2,1,0:T(8,128)(2,1)S(1)} %collective-permute-done.3.third_ref, ...), custom_call_target="tpu_custom_call" | custom-call | flops 2100000000 | bytes 8203125 | tf_op jit(solution)/shard_map/pallas_call | solution.py:364
  18.4 0.1 collective-permute-start.7
  18.5 1.5 %collective-permute-done.7.mixed_far_ref = bf16[288,384]{1,0:T(8,128)(2,1)S(1)} collective-permute-done((bf16[288,384]{1,0:T(8,128)(2,1)S(1)}, bf16[288,384]{1,0:T(8,128)(2,1)S(1)}, u32[]{:S(2)}, u32[]{:S(2)}) %collective-permute-start.7) | collective-permute-done | bytes 221216 | tf_op jit(solution)/shard_map/ppermute | solution.py:697
  20.0 0.4 %shard_map.126 = (f32[192,384]{1,0:T(8,128)S(1)}, bf16[208,384]{1,0:T(8,128)(2,1)S(1)}, f32[16,384]{1,0:T(8,128)S(1)}) custom-call(bf16[256,384]{1,0:T(8,128)(2,1)S(1)} %get-tuple-element.45.reduced_ref, bf16[256,384]{1,0:T(8,128)(2,1)S(1)} %collective-permute-done.5.reduced_far_ref, bf16[288,384]{1,0:T(8,128)(2,1)S(1)} %get-tuple-element.57.mixed_ref, ...), custom_call_target="tpu_custom_call" | custom-call | flops 500000000 | bytes 1953125 | tf_op jit(solution)/shard_map/pallas_call | solution.py:364
  20.4 1.6 %collective-permute-start.8 = (bf16[208,384]{1,0:T(8,128)(2,1)S(1)}, bf16[208,384]{1,0:T(8,128)(2,1)S(1)}, u32[]{:S(2)}, u32[]{:S(2)}) collective-permute-start(bf16[208,384]{1,0:T(8,128)(2,1)S(1)} %get-tuple-element.60), channel_id=1, source_target_pairs={{0,3},{1,4},{2,7},{3,0},{4,1},{5,6},{6,5},{7,2},{8,13},{9,10},{10,... | collective-permute-start | bytes 479240 | tf_op jit(solution)/shard_map/ppermute | solution.py:705
  22.1 1.3 %shard_map.128 = bf16[1,128,768]{2,1,0:T(8,128)(2,1)} custom-call(f32[128,768]{1,0:T(8,128)S(1)} %get-tuple-element.63.gradient_ref, bf16[288,384]{1,0:T(8,128)(2,1)S(1)} %get-tuple-element.57.mixed_ref, f32[3,128,768]{2,1,0:T(8,128)S(1)} %get-tuple-element.46.stream_ref, f32[2,128,1]{2,1,0:T(8,128)S(1)} %get-tuple-element.55.inverse_ref, ...), custom_call_target="tpu_custom_call" | custom-call | flops 1300000000 | bytes 5078125 | tf_op jit(solution)/shard_map/pallas_call | solution.py:364
  23.4 1.8 %collective-permute-done.8.got_ref = bf16[208,384]{1,0:T(8,128)(2,1)S(1)} collective-permute-done((bf16[208,384]{1,0:T(8,128)(2,1)S(1)}, bf16[208,384]{1,0:T(8,128)(2,1)S(1)}, u32[]{:S(2)}, u32[]{:S(2)}) %collective-permute-start.8) | collective-permute-done | bytes 159776 | tf_op jit(solution)/shard_map/ppermute | solution.py:705
  25.2 1.7 %collective-permute-start.9 = (bf16[112,384]{1,0:T(8,128)(2,1)S(1)}, bf16[112,384]{1,0:T(8,128)(2,1)S(1)}, u32[]{:S(2)}, u32[]{:S(2)}) collective-permute-start(bf16[112,384]{1,0:T(8,128)(2,1)S(1)} %get-tuple-element.66), channel_id=1, source_target_pairs={{0,5},{1,2},{2,1},{3,6},{4,7},{5,0},{6,3},{7,4},{8,11},{9,12},{10,... | collective-permute-start | bytes 258056 | tf_op jit(solution)/shard_map/ppermute | solution.py:705
  27.0 2.3 %collective-permute-done.9.got_ref = bf16[112,384]{1,0:T(8,128)(2,1)S(1)} collective-permute-done((bf16[112,384]{1,0:T(8,128)(2,1)S(1)}, bf16[112,384]{1,0:T(8,128)(2,1)S(1)}, u32[]{:S(2)}, u32[]{:S(2)}) %collective-permute-start.9) | collective-permute-done | bytes 86048 | tf_op jit(solution)/shard_map/ppermute | solution.py:705
  29.2 2.7 %collective-permute-start.10 = (bf16[56,384]{1,0:T(8,128)(2,1)S(1)}, bf16[56,384]{1,0:T(8,128)(2,1)S(1)}, u32[]{:S(2)}, u32[]{:S(2)}) collective-permute-start(bf16[56,384]{1,0:T(8,128)(2,1)S(1)} %get-tuple-element.69), channel_id=1, source_target_pairs={{0,9},{1,8},{2,11},{3,10},{4,13},{5,12},{6,15},{7,14},{8,1},{9,0},... | collective-permute-start | bytes 129032 | tf_op jit(solution)/shard_map/ppermute | solution.py:705
  32.0 1.7 %collective-permute-done.10.got_ref = bf16[56,384]{1,0:T(8,128)(2,1)S(1)} collective-permute-done((bf16[56,384]{1,0:T(8,128)(2,1)S(1)}, bf16[56,384]{1,0:T(8,128)(2,1)S(1)}, u32[]{:S(2)}, u32[]{:S(2)}) %collective-permute-start.10) | collective-permute-done | bytes 43040 | tf_op jit(solution)/shard_map/ppermute | solution.py:705
  33.7 2.1 %collective-permute-start.11 = (bf16[48,384]{1,0:T(8,128)(2,1)S(1)}, bf16[48,384]{1,0:T(8,128)(2,1)S(1)}, u32[]{:S(2)}, u32[]{:S(2)}) collective-permute-start(bf16[48,384]{1,0:T(8,128)(2,1)S(1)} %get-tuple-element.71), channel_id=1, source_target_pairs={{6,0},{3,1},{7,2},{5,3},{1,4},{0,5},{4,6},{2,7},{14,8},{11,9},{15,... | collective-permute-start | bytes 110600 | tf_op jit(solution)/shard_map/ppermute | solution.py:817
  35.8 1.5 %collective-permute-start.12 = (bf16[48,384]{1,0:T(8,128)(2,1)S(1)}, bf16[48,384]{1,0:T(8,128)(2,1)S(1)}, u32[]{:S(2)}, u32[]{:S(2)}) collective-permute-start(bf16[48,384]{1,0:T(8,128)(2,1)S(1)} %get-tuple-element.71), channel_id=1, source_target_pairs={{5,0},{4,1},{0,2},{6,3},{7,4},{2,5},{3,6},{1,7},{13,8},{12,9},{8,1... | collective-permute-start | bytes 110600 | tf_op jit(solution)/shard_map/ppermute | solution.py:817
  37.3 0.7 %shard_map.132 = f32[8,48]{1,0:T(8,128)} custom-call(bf16[56,384]{1,0:T(8,128)(2,1)S(1)} %collective-permute-done.10.got_ref, f32[8,384]{1,0:T(8,128)S(1)} %get-tuple-element.72.partial_ref), custom_call_target="tpu_custom_call" | custom-call | tf_op jit(solution)/shard_map/pallas_call | solution.py:364
  38.0 1.0 %collective-permute-done.11.first_ref = bf16[48,384]{1,0:T(8,128)(2,1)S(1)} collective-permute-done((bf16[48,384]{1,0:T(8,128)(2,1)S(1)}, bf16[48,384]{1,0:T(8,128)(2,1)S(1)}, u32[]{:S(2)}, u32[]{:S(2)}) %collective-permute-start.11) | collective-permute-done | bytes 36896 | tf_op jit(solution)/shard_map/ppermute | solution.py:817
  39.0 0.2 collective-permute-done.12.second_ref
  39.2 0.7 %shard_map.131 = f32[144,384]{1,0:T(8,128)} custom-call(f32[48,384]{1,0:T(8,128)S(1)} %get-tuple-element.70.own_ref, bf16[48,384]{1,0:T(8,128)(2,1)S(1)} %collective-permute-done.11.first_ref, bf16[48,384]{1,0:T(8,128)(2,1)S(1)} %collective-permute-done.12.second_ref), custom_call_target="tpu_custom_call" | custom-call | tf_op jit(solution)/shard_map/pallas_call | solution.py:364
  (14 shorter events, 0.1 us)
Async XLA Ops:
  0.6 7.7 %collective-permute-start.2 = (bf16[2,3,192,384]{3,2,1,0:T(8,128)(2,1)}, bf16[2,3,192,384]{3,2,1,0:T(8,128)(2,1)S(1)}, u32[]{:S(2)}, u32[]{:S(2)}) collective-permute-start(bf16[2,3,192,384]{3,2,1,0:T(8,128)(2,1)} %bitcast.2), channel_id=1, source_target_pairs={{0,1},{1,0},{2,3},{3,2},{4,5},{5,4},{6,7},{7,6},{8,9},{9,8},{10,11... | collective-permute-start | bytes 2654216 | tf_op jit(solution)/shard_map/ppermute | solution.py:697
  1.1 5.4 %copy-start.9 = (f32[768]{0:T(1024)S(1)}, f32[768]{0:T(1024)}, u32[]{:S(2)}) copy-start(f32[768]{0:T(1024)} %param.13) | copy-start | bytes 9220
  1.2 7.2 %copy-start = (bf16[2,3,384,192]{2,3,1,0:T(8,128)(2,1)S(1)}, bf16[2,3,384,192]{2,3,1,0:T(8,128)(2,1)}, u32[]{:S(2)}) copy-start(bf16[2,3,384,192]{2,3,1,0:T(8,128)(2,1)} %param.15) | copy-start | bytes 2654212
  1.2 7.2 %copy-start.1 = (bf16[2,768,192]{1,2,0:T(8,128)(2,1)S(1)}, bf16[2,768,192]{1,2,0:T(8,128)(2,1)}, u32[]{:S(2)}) copy-start(bf16[2,768,192]{1,2,0:T(8,128)(2,1)} %param.14) | copy-start | bytes 1769476
  1.2 7.1 %collective-permute-start.1 = (bf16[2,192,768]{2,1,0:T(8,128)(2,1)}, bf16[2,192,768]{2,1,0:T(8,128)(2,1)S(1)}, u32[]{:S(2)}, u32[]{:S(2)}) collective-permute-start(bf16[2,192,768]{2,1,0:T(8,128)(2,1)} %bitcast.4), channel_id=1, source_target_pairs={{0,1},{1,0},{2,3},{3,2},{4,5},{5,4},{6,7},{7,6},{8,9},{9,8},{10,11... | collective-permute-start | bytes 1769480 | tf_op jit(solution)/shard_map/ppermute | solution.py:697
  1.3 9.4 %collective-permute-start.4 = (bf16[2,384,384]{2,1,0:T(8,128)(2,1)}, bf16[2,384,384]{2,1,0:T(8,128)(2,1)S(1)}, u32[]{:S(2)}, u32[]{:S(2)}) collective-permute-start(bf16[2,384,384]{2,1,0:T(8,128)(2,1)} %up_ref.3), channel_id=1, source_target_pairs={{0,1},{1,0},{2,3},{3,2},{4,5},{5,4},{6,7},{7,6},{8,9},{9,8},{10,11... | collective-permute-start | bytes 1769480 | tf_op jit(solution)/shard_map/ppermute | solution.py:697
  2.8 5.4 %collective-permute-start = (bf16[1,8,896]{2,1,0:T(8,128)(2,1)S(1)}, bf16[1,8,896]{2,1,0:T(8,128)(2,1)S(1)}, u32[]{:S(2)}, u32[]{:S(2)}) collective-permute-start(bf16[1,8,896]{2,1,0:T(8,128)(2,1)S(1)} %shard_map.121.first_ref), channel_id=1, source_target_pairs={{0,8},{1,9},{2,10},{3,11},{4,12},{5,13},{6,14},{7,15},{8,0},{9,1},... | collective-permute-start | bytes 43016 | tf_op jit(solution)/shard_map/ppermute | solution.py:705
  8.3 2.4 %copy-start.2 = (bf16[2,384,384]{2,1,0:T(8,128)(2,1)S(1)}, bf16[2,384,384]{2,1,0:T(8,128)(2,1)}, u32[]{:S(2)}) copy-start(bf16[2,384,384]{2,1,0:T(8,128)(2,1)} %up_ref.3) | copy-start | bytes 1769476
  8.3 2.4 %copy-start.3 = (bf16[1,128,768]{2,1,0:T(8,128)(2,1)S(1)}, bf16[1,128,768]{2,1,0:T(8,128)(2,1)}, u32[]{:S(2)}) copy-start(bf16[1,128,768]{2,1,0:T(8,128)(2,1)} %feature_ref.1) | copy-start | bytes 589828
  8.3 2.4 %copy-start.6 = (s32[1,128]{1,0:T(1,128)S(1)}, s32[1,128]{1,0:T(1,128)}, u32[]{:S(2)}) copy-start(s32[1,128]{1,0:T(1,128)} %count_ref.1) | copy-start | bytes 1540
  8.6 4.1 %copy-start.8 = (f32[4]{0:T(128)S(1)}, f32[4]{0:T(128)}, u32[]{:S(2)}) copy-start(f32[4]{0:T(128)} %decay_ref.1) | copy-start | bytes 52
  8.6 6.0 %copy-start.4 = (bf16[1,128,768]{2,1,0:T(8,128)(2,1)S(1)}, bf16[1,128,768]{2,1,0:T(8,128)(2,1)}, u32[]{:S(2)}) copy-start(bf16[1,128,768]{2,1,0:T(8,128)(2,1)} %cot_ref.1) | copy-start | bytes 589828
  8.6 6.0 %copy-start.5 = (f32[2,4,768]{2,1,0:T(4,128)S(1)}, f32[2,4,768]{2,1,0:T(4,128)}, u32[]{:S(2)}) copy-start(f32[2,4,768]{2,1,0:T(4,128)} %mode_ref.3) | copy-start | bytes 73732
  8.6 6.0 %copy-start.7 = (f32[1,128]{1,0:T(1,128)S(1)}, f32[1,128]{1,0:T(1,128)}, u32[]{:S(2)}) copy-start(f32[1,128]{1,0:T(1,128)} %keep_ref.1) | copy-start | bytes 1540
  8.6 3.9 %collective-permute-start.3 = (bf16[2,8,896]{2,1,0:T(8,128)(2,1)S(1)}, bf16[2,8,896]{2,1,0:T(8,128)(2,1)S(1)}, u32[]{:S(2)}, u32[]{:S(2)}) collective-permute-start(bf16[2,8,896]{2,1,0:T(8,128)(2,1)S(1)} %pad_maximum_fusion.1), channel_id=1, source_target_pairs={{0,4},{1,3},{2,6},{3,1},{4,0},{5,7},{6,2},{7,5},{8,12},{9,11},{10,... | collective-permute-start | bytes 86024 | tf_op jit(solution)/shard_map/ppermute | solution.py:705
  12.6 3.5 %collective-permute-start.5 = (bf16[256,384]{1,0:T(8,128)(2,1)S(1)}, bf16[256,384]{1,0:T(8,128)(2,1)S(1)}, u32[]{:S(2)}, u32[]{:S(2)}) collective-permute-start(bf16[256,384]{1,0:T(8,128)(2,1)S(1)} %get-tuple-element.45.reduced_ref), channel_id=1, source_target_pairs={{0,1},{1,0},{2,3},{3,2},{4,5},{5,4},{6,7},{7,6},{8,9},{9,8},{10,11... | collective-permute-start | bytes 589832 | tf_op jit(solution)/shard_map/ppermute | solution.py:697
  12.7 4.2 %collective-permute-start.6 = (bf16[4,8,896]{2,1,0:T(8,128)(2,1)S(1)}, bf16[4,8,896]{2,1,0:T(8,128)(2,1)S(1)}, u32[]{:S(2)}, u32[]{:S(2)}) collective-permute-start(bf16[4,8,896]{2,1,0:T(8,128)(2,1)S(1)} %pad_maximum_fusion), channel_id=1, source_target_pairs={{0,2},{1,5},{2,0},{3,7},{4,6},{5,1},{6,4},{7,3},{8,10},{9,13},{10,... | collective-permute-start | bytes 172040 | tf_op jit(solution)/shard_map/ppermute | solution.py:705
  18.4 1.5 %collective-permute-start.7 = (bf16[288,384]{1,0:T(8,128)(2,1)S(1)}, bf16[288,384]{1,0:T(8,128)(2,1)S(1)}, u32[]{:S(2)}, u32[]{:S(2)}) collective-permute-start(bf16[288,384]{1,0:T(8,128)(2,1)S(1)} %get-tuple-element.57.mixed_ref), channel_id=1, source_target_pairs={{0,1},{1,0},{2,3},{3,2},{4,5},{5,4},{6,7},{7,6},{8,9},{9,8},{10,11... | collective-permute-start | bytes 663560 | tf_op jit(solution)/shard_map/ppermute | solution.py:697
  20.4 4.8 %collective-permute-start.8 = (bf16[208,384]{1,0:T(8,128)(2,1)S(1)}, bf16[208,384]{1,0:T(8,128)(2,1)S(1)}, u32[]{:S(2)}, u32[]{:S(2)}) collective-permute-start(bf16[208,384]{1,0:T(8,128)(2,1)S(1)} %get-tuple-element.60), channel_id=1, source_target_pairs={{0,3},{1,4},{2,7},{3,0},{4,1},{5,6},{6,5},{7,2},{8,13},{9,10},{10,... | collective-permute-start | bytes 479240 | tf_op jit(solution)/shard_map/ppermute | solution.py:705
  25.2 4.0 %collective-permute-start.9 = (bf16[112,384]{1,0:T(8,128)(2,1)S(1)}, bf16[112,384]{1,0:T(8,128)(2,1)S(1)}, u32[]{:S(2)}, u32[]{:S(2)}) collective-permute-start(bf16[112,384]{1,0:T(8,128)(2,1)S(1)} %get-tuple-element.66), channel_id=1, source_target_pairs={{0,5},{1,2},{2,1},{3,6},{4,7},{5,0},{6,3},{7,4},{8,11},{9,12},{10,... | collective-permute-start | bytes 258056 | tf_op jit(solution)/shard_map/ppermute | solution.py:705
  29.2 4.4 %collective-permute-start.10 = (bf16[56,384]{1,0:T(8,128)(2,1)S(1)}, bf16[56,384]{1,0:T(8,128)(2,1)S(1)}, u32[]{:S(2)}, u32[]{:S(2)}) collective-permute-start(bf16[56,384]{1,0:T(8,128)(2,1)S(1)} %get-tuple-element.69), channel_id=1, source_target_pairs={{0,9},{1,8},{2,11},{3,10},{4,13},{5,12},{6,15},{7,14},{8,1},{9,0},... | collective-permute-start | bytes 129032 | tf_op jit(solution)/shard_map/ppermute | solution.py:705
  33.7 5.3 %collective-permute-start.11 = (bf16[48,384]{1,0:T(8,128)(2,1)S(1)}, bf16[48,384]{1,0:T(8,128)(2,1)S(1)}, u32[]{:S(2)}, u32[]{:S(2)}) collective-permute-start(bf16[48,384]{1,0:T(8,128)(2,1)S(1)} %get-tuple-element.71), channel_id=1, source_target_pairs={{6,0},{3,1},{7,2},{5,3},{1,4},{0,5},{4,6},{2,7},{14,8},{11,9},{15,... | collective-permute-start | bytes 110600 | tf_op jit(solution)/shard_map/ppermute | solution.py:817
  35.8 3.4 %collective-permute-start.12 = (bf16[48,384]{1,0:T(8,128)(2,1)S(1)}, bf16[48,384]{1,0:T(8,128)(2,1)S(1)}, u32[]{:S(2)}, u32[]{:S(2)}) collective-permute-start(bf16[48,384]{1,0:T(8,128)(2,1)S(1)} %get-tuple-element.71), channel_id=1, source_target_pairs={{5,0},{4,1},{0,2},{6,3},{7,4},{2,5},{3,6},{1,7},{13,8},{12,9},{8,1... | collective-permute-start | bytes 110600 | tf_op jit(solution)/shard_map/ppermute | solution.py:817

commit v7 on v6

--- a/solution.py
+++ b/solution.py
@@ -614,26 +614,33 @@
     return pl.multiple_of(entry_of(OWNED, 4 * bit_z + 2 * bit_x + core) * BLOCK, BLOCK)
 
 
-def taps_body(
-    reduced_ref, reduced_far_ref, mixed_ref, mixed_far_ref, partial_ref,
-    kept_ref, send_ref, partial_out, block_ref,
-):
+def select_body(reduced_ref, reduced_far_ref, left_ref, turned_ref):
     bits, parity = position_bits()
     bit = pick(parity, bits[0], bits[1])
     rows = reduced_ref.shape[0] // LAYERS
     for layer in range(LAYERS):
         part = slice(layer * rows, (layer + 1) * rows)
-        left = jnp.concatenate([reduced_ref[part, :], reduced_far_ref[part, :]], axis=0)
+        turned_ref[layer, :, :rows] = reduced_ref[part, :].T
+        turned_ref[layer, :, rows:] = reduced_far_ref[part, :].T
+        for side in range(2):
+            first = bit if side == 0 else 1 - bit
+            for turn in range(2):
+                block = held_block(parity, pick(parity, first, turn), pick(parity, turn, first), layer)
+                to = (2 * side + turn) * BLOCK
+                left_ref[layer, to : to + BLOCK, :] = turned_ref[layer, pl.ds(block, BLOCK), :]
+
+
+def taps_body(left_ref, mixed_ref, mixed_far_ref, partial_ref, kept_ref, send_ref, partial_out):
+    rows = left_ref.shape[-1] // 2
+    kept_rows = kept_ref.shape[0]
+    for layer in range(LAYERS):
+        part = slice(layer * rows, (layer + 1) * rows)
         right = jnp.concatenate([mixed_ref[part, :], mixed_far_ref[part, :]], axis=0)
-        block_ref[layer] = dot_tn(left, right)
-    kept_rows = kept_ref.shape[0]
-    for turn in range(2):
-        for layer in range(LAYERS):
+        blocks = dot(left_ref[layer], right)
+        for turn in range(2):
             to = (2 * turn + layer) * BLOCK
-            kept = held_block(parity, pick(parity, bit, turn), pick(parity, turn, bit), layer)
-            sent = held_block(parity, pick(parity, 1 - bit, turn), pick(parity, turn, 1 - bit), layer)
-            kept_ref[to : to + BLOCK, :] = block_ref[layer, pl.ds(kept, BLOCK), :]
-            send_ref[to : to + BLOCK, :] = block_ref[layer, pl.ds(sent, BLOCK), :].astype(BF16)
+            kept_ref[to : to + BLOCK, :] = blocks[turn * BLOCK : (turn + 1) * BLOCK]
+            send_ref[to : to + BLOCK, :] = blocks[(2 + turn) * BLOCK : (3 + turn) * BLOCK].astype(BF16)
     high = mixed_far_ref[LAYERS * rows : LAYERS * rows + 16, :].astype(F32)
     low = mixed_far_ref[LAYERS * rows + 16 : LAYERS * rows + 32, :].astype(F32)
     partial = partial_ref[...] + (high + low)
@@ -780,12 +787,20 @@
         (((1, rows, width), BF16),), size=1300 * GIGA
     )
     kept_rows = RING * BLOCK // 2
+    (left,) = call(
+        select_body,
+        (reduced, reduced_far),
+        (VMEM,) * 2,
+        (((LAYERS, kept_rows, 2 * rows), BF16),),
+        (pltpu.VMEM((LAYERS, B, 2 * rows), BF16),),
+        size=500 * GIGA,
+    )
     kept, send, partial = call(
         taps_body,
-        (reduced, reduced_far, mixed, mixed_far, partial),
-        (VMEM,) * 5,
+        (left, mixed, mixed_far, partial),
+        (VMEM,) * 4,
         (((kept_rows, B), F32), ((kept_rows + 16, B), BF16), ((16, B), F32)),
-        (pltpu.VMEM((LAYERS, B, B), F32),), size=500 * GIGA
+        size=300 * GIGA,
     )
     got = hop_to(send, lambda core, place: (1, 1 + class_of(core, place)))
     for stage in (1, 2):

time: 40.1 us -> 39.9 us (level)
    pallas_call x12 -> x13, Pallas kernels: 9.41 us -> 9.39 us  [call(): pl.pallas_call(body, out_shape=[jax.ShapeDtypeStruct(shape, dtype) for sh...]
where the time goes in v7:
time: 39.9 us; the launch traced here: 39.7 us
  starting transfers between devices  18.4 us (46%)
  waiting for transfers between devices  11 us (28%)
  Pallas kernels  9.39 us (24%)
  between operations  0.84 us (2%)
    ppermute x6, starting transfers between devices, hop_to(): return lax.ppermute(value, ('seq', 'dp'), pairs)  13.7 us
    pallas_call x13, Pallas kernels, call(): pl.pallas_call(body, out_shape=[jax.ShapeDtypeStruct(shape, dtype) for sh...  9.39 us
    ppermute x6, waiting for transfers between devices, hop_to(): return lax.ppermute(value, ('seq', 'dp'), pairs)  8.44 us
    ppermute x2, starting transfers between devices, wrapped_device(): parts.append(lax.ppermute(narrow, ('seq', 'dp'), pairs))  3.6 us
    ppermute x5, waiting for transfers between devices, swap(): lax.ppermute(value, axis, [(source, source ^ mask) for source in range(co...  1.3 us
    ppermute x2, waiting for transfers between devices, wrapped_device(): parts.append(lax.ppermute(narrow, ('seq', 'dp'), pairs))  1.23 us
    ppermute x5, starting transfers between devices, swap(): lax.ppermute(value, axis, [(source, source ^ mask) for source in range(co...  1.17 us
  transfers between devices with their start and end apart: 13, of which 9 were waited for; matrix products, arithmetic and copies ran while one was open for 0% of the time, Pallas kernels for 17%

profile of v7, /device:TPU:0, one launch (start us, length us, event | category | flops | bytes accessed | tf_op | source)
XLA Modules:
  0.0 39.7 jit_solution(3897870053898137137)
XLA Ops:
  0.6 0.5 %collective-permute-start.2 = (bf16[2,3,192,384]{3,2,1,0:T(8,128)(2,1)}, bf16[2,3,192,384]{3,2,1,0:T(8,128)(2,1)S(1)}, u32[]{:S(2)}, u32[]{:S(2)}) collective-permute-start(bf16[2,3,192,384]{3,2,1,0:T(8,128)(2,1)} %bitcast.2), channel_id=1, source_target_pairs={{0,1},{1,0},{2,3},{3,2},{4,5},{5,4},{6,7},{7,6},{8,9},{9,8},{10,11... | collective-permute-start | bytes 2654216 | tf_op jit(solution)/shard_map/ppermute | solution.py:704
  1.2 0.1 collective-permute-start.1
  1.3 0.4 %collective-permute-start.4 = (bf16[2,384,384]{2,1,0:T(8,128)(2,1)}, bf16[2,384,384]{2,1,0:T(8,128)(2,1)S(1)}, u32[]{:S(2)}, u32[]{:S(2)}) collective-permute-start(bf16[2,384,384]{2,1,0:T(8,128)(2,1)} %up_ref.3), channel_id=1, source_target_pairs={{0,1},{1,0},{2,3},{3,2},{4,5},{5,4},{6,7},{7,6},{8,9},{9,8},{10,11... | collective-permute-start | bytes 1769480 | tf_op jit(solution)/shard_map/ppermute | solution.py:704
  1.7 1.1 %shard_map.121.first_ref = bf16[1,8,896]{2,1,0:T(8,128)(2,1)S(1)} custom-call(bf16[1,128,768]{2,1,0:T(8,128)(2,1)} %cot_ref.1, f32[1,128]{1,0:T(1,128)} %keep_ref.1, f32[4]{0:T(128)} %decay_ref.1), custom_call_target="tpu_custom_call" | custom-call | flops 1300000000 | bytes 5078125 | tf_op jit(solution)/shard_map/pallas_call | solution.py:364
  2.8 3.8 %collective-permute-start = (bf16[1,8,896]{2,1,0:T(8,128)(2,1)S(1)}, bf16[1,8,896]{2,1,0:T(8,128)(2,1)S(1)}, u32[]{:S(2)}, u32[]{:S(2)}) collective-permute-start(bf16[1,8,896]{2,1,0:T(8,128)(2,1)S(1)} %shard_map.121.first_ref), channel_id=1, source_target_pairs={{0,8},{1,9},{2,10},{3,11},{4,12},{5,13},{6,14},{7,15},{8,0},{9,1},... | collective-permute-start | bytes 43016 | tf_op jit(solution)/shard_map/ppermute | solution.py:712
  6.6 1.7 %collective-permute-done.second_ref = bf16[1,8,896]{2,1,0:T(8,128)(2,1)S(1)} collective-permute-done((bf16[1,8,896]{2,1,0:T(8,128)(2,1)S(1)}, bf16[1,8,896]{2,1,0:T(8,128)(2,1)S(1)}, u32[]{:S(2)}, u32[]{:S(2)}) %collective-permute-start) | collective-permute-done | bytes 14368 | tf_op jit(solution)/shard_map/ppermute | solution.py:712
  8.3 0.0 copy-start.2
  8.3 0.0 copy-start.3
  8.3 0.0 copy-start.6
  8.3 0.0 collective-permute-done.1.down_far_ref
  8.3 0.0 collective-permute-done.2.tap_far_ref
  8.3 0.0 copy-done
  8.3 0.0 copy-done.1
  8.3 0.3 shard_map.122
  8.6 0.0 copy-start.8
  8.6 0.0 copy-start.4
  8.6 0.0 copy-start.5
  8.6 0.0 copy-start.7
  8.6 2.0 %collective-permute-start.3 = (bf16[2,8,896]{2,1,0:T(8,128)(2,1)S(1)}, bf16[2,8,896]{2,1,0:T(8,128)(2,1)S(1)}, u32[]{:S(2)}, u32[]{:S(2)}) collective-permute-start(bf16[2,8,896]{2,1,0:T(8,128)(2,1)S(1)} %pad_maximum_fusion.1), channel_id=1, source_target_pairs={{0,4},{1,3},{2,6},{3,1},{4,0},{5,7},{6,2},{7,5},{8,12},{9,11},{10,... | collective-permute-start | bytes 86024 | tf_op jit(solution)/shard_map/ppermute | solution.py:712
  10.6 0.0 collective-permute-done.4.up_far_ref
  10.6 0.0 copy-done.2
  10.6 1.8 %shard_map.123 = (f32[3,128,768]{2,1,0:T(8,128)S(1)}, f32[2,128,1]{2,1,0:T(8,128)S(1)}, bf16[256,384]{1,0:T(8,128)(2,1)S(1)}, f32[2,128,384]{2,1,0:T(8,128)S(1)}) custom-call(bf16[1,128,768]{2,1,0:T(8,128)(2,1)S(1)} %copy-done.3, s32[1,128]{1,0:T(1,128)S(1)} %copy-done.6, f32[1,768]{1,0:T(1,128)S(1)} %broadcast_in_dim.3.weight_ref, ...), custom_call_target="tpu_custom_call" | custom-call | flops 1800000000 | bytes 7031250 | tf_op jit(solution)/shard_map/pallas_call | solution.py:364
  12.5 0.1 collective-permute-done.3.third_ref
  12.6 0.1 collective-permute-start.5
  12.7 0.0 copy-done.8
  12.7 1.9 %collective-permute-start.6 = (bf16[4,8,896]{2,1,0:T(8,128)(2,1)S(1)}, bf16[4,8,896]{2,1,0:T(8,128)(2,1)S(1)}, u32[]{:S(2)}, u32[]{:S(2)}) collective-permute-start(bf16[4,8,896]{2,1,0:T(8,128)(2,1)S(1)} %pad_maximum_fusion), channel_id=1, source_target_pairs={{0,2},{1,5},{2,0},{3,7},{4,6},{5,1},{6,4},{7,3},{8,10},{9,13},{10,... | collective-permute-start | bytes 172040 | tf_op jit(solution)/shard_map/ppermute | solution.py:712
  14.6 0.0 copy-done.7
  14.6 1.5 %shard_map.124 = (f32[128,768]{1,0:T(8,128)S(1)}, f32[8,768]{1,0:T(8,128)S(1)}, f32[8,768]{1,0:T(8,128)S(1)}, bf16[32,128]{1,0:T(8,128)(2,1)S(1)}, f32[2,8,128]{2,1,0:T(8,128)S(1)}) custom-call(f32[4]{0:T(128)S(1)} %copy-done.8, f32[4]{0:T(128)S(1)} %negate_sqrt_fusion.scale_ref, bf16[1,128,768]{2,1,0:T(8,128)(2,1)S(1)} %copy-done.4, ...), custom_call_target="tpu_custom_call" | custom-call | flops 1600000000 | bytes 6250000 | tf_op jit(solution)/shard_map/pallas_call | solution.py:364
  16.1 0.0 collective-permute-done.5.reduced_far_ref
  16.1 0.8 %collective-permute-done.6.fourth_ref = bf16[4,8,896]{2,1,0:T(8,128)(2,1)S(1)} collective-permute-done((bf16[4,8,896]{2,1,0:T(8,128)(2,1)S(1)}, bf16[4,8,896]{2,1,0:T(8,128)(2,1)S(1)}, u32[]{:S(2)}, u32[]{:S(2)}) %collective-permute-start.6) | collective-permute-done | bytes 57376 | tf_op jit(solution)/shard_map/ppermute | solution.py:712
  16.9 1.5 %shard_map.126 = (f32[128,768]{1,0:T(8,128)S(1)}, bf16[288,384]{1,0:T(8,128)(2,1)S(1)}, f32[16,384]{1,0:T(8,128)S(1)}) custom-call(bf16[1,8,896]{2,1,0:T(8,128)(2,1)S(1)} %shard_map.121.first_ref, bf16[1,8,896]{2,1,0:T(8,128)(2,1)S(1)} %collective-permute-done.second_ref, bf16[2,8,896]{2,1,0:T(8,128)(2,1)S(1)} %collective-permute-done.3.third_ref, ...), custom_call_target="tpu_custom_call" | custom-call | flops 2100000000 | bytes 8203125 | tf_op jit(solution)/shard_map/pallas_call | solution.py:364
  18.4 0.1 collective-permute-start.7
  18.5 0.2 shard_map.125.left_ref
  18.7 1.3 %collective-permute-done.7.mixed_far_ref = bf16[288,384]{1,0:T(8,128)(2,1)S(1)} collective-permute-done((bf16[288,384]{1,0:T(8,128)(2,1)S(1)}, bf16[288,384]{1,0:T(8,128)(2,1)S(1)}, u32[]{:S(2)}, u32[]{:S(2)}) %collective-permute-start.7) | collective-permute-done | bytes 221216 | tf_op jit(solution)/shard_map/ppermute | solution.py:704
  20.0 0.3 shard_map.127
  20.3 1.6 %collective-permute-start.8 = (bf16[208,384]{1,0:T(8,128)(2,1)S(1)}, bf16[208,384]{1,0:T(8,128)(2,1)S(1)}, u32[]{:S(2)}, u32[]{:S(2)}) collective-permute-start(bf16[208,384]{1,0:T(8,128)(2,1)S(1)} %get-tuple-element.60), channel_id=1, source_target_pairs={{0,3},{1,4},{2,7},{3,0},{4,1},{5,6},{6,5},{7,2},{8,13},{9,10},{10,... | collective-permute-start | bytes 479240 | tf_op jit(solution)/shard_map/ppermute | solution.py:712
  21.9 1.3 %shard_map.129 = bf16[1,128,768]{2,1,0:T(8,128)(2,1)} custom-call(f32[128,768]{1,0:T(8,128)S(1)} %get-tuple-element.63.gradient_ref, bf16[288,384]{1,0:T(8,128)(2,1)S(1)} %get-tuple-element.57.mixed_ref, f32[3,128,768]{2,1,0:T(8,128)S(1)} %get-tuple-element.46.stream_ref, f32[2,128,1]{2,1,0:T(8,128)S(1)} %get-tuple-element.55.inverse_ref, ...), custom_call_target="tpu_custom_call" | custom-call | flops 1300000000 | bytes 5078125 | tf_op jit(solution)/shard_map/pallas_call | solution.py:364
  23.2 1.8 %collective-permute-done.8.got_ref = bf16[208,384]{1,0:T(8,128)(2,1)S(1)} collective-permute-done((bf16[208,384]{1,0:T(8,128)(2,1)S(1)}, bf16[208,384]{1,0:T(8,128)(2,1)S(1)}, u32[]{:S(2)}, u32[]{:S(2)}) %collective-permute-start.8) | collective-permute-done | bytes 159776 | tf_op jit(solution)/shard_map/ppermute | solution.py:712
  25.1 1.7 %collective-permute-start.9 = (bf16[112,384]{1,0:T(8,128)(2,1)S(1)}, bf16[112,384]{1,0:T(8,128)(2,1)S(1)}, u32[]{:S(2)}, u32[]{:S(2)}) collective-permute-start(bf16[112,384]{1,0:T(8,128)(2,1)S(1)} %get-tuple-element.66), channel_id=1, source_target_pairs={{0,5},{1,2},{2,1},{3,6},{4,7},{5,0},{6,3},{7,4},{8,11},{9,12},{10,... | collective-permute-start | bytes 258056 | tf_op jit(solution)/shard_map/ppermute | solution.py:712
  26.8 2.3 %collective-permute-done.9.got_ref = bf16[112,384]{1,0:T(8,128)(2,1)S(1)} collective-permute-done((bf16[112,384]{1,0:T(8,128)(2,1)S(1)}, bf16[112,384]{1,0:T(8,128)(2,1)S(1)}, u32[]{:S(2)}, u32[]{:S(2)}) %collective-permute-start.9) | collective-permute-done | bytes 86048 | tf_op jit(solution)/shard_map/ppermute | solution.py:712
  29.1 2.7 %collective-permute-start.10 = (bf16[56,384]{1,0:T(8,128)(2,1)S(1)}, bf16[56,384]{1,0:T(8,128)(2,1)S(1)}, u32[]{:S(2)}, u32[]{:S(2)}) collective-permute-start(bf16[56,384]{1,0:T(8,128)(2,1)S(1)} %get-tuple-element.69), channel_id=1, source_target_pairs={{0,9},{1,8},{2,11},{3,10},{4,13},{5,12},{6,15},{7,14},{8,1},{9,0},... | collective-permute-start | bytes 129032 | tf_op jit(solution)/shard_map/ppermute | solution.py:712
  31.8 1.7 %collective-permute-done.10.got_ref = bf16[56,384]{1,0:T(8,128)(2,1)S(1)} collective-permute-done((bf16[56,384]{1,0:T(8,128)(2,1)S(1)}, bf16[56,384]{1,0:T(8,128)(2,1)S(1)}, u32[]{:S(2)}, u32[]{:S(2)}) %collective-permute-start.10) | collective-permute-done | bytes 43040 | tf_op jit(solution)/shard_map/ppermute | solution.py:712
  33.5 2.1 %collective-permute-start.11 = (bf16[48,384]{1,0:T(8,128)(2,1)S(1)}, bf16[48,384]{1,0:T(8,128)(2,1)S(1)}, u32[]{:S(2)}, u32[]{:S(2)}) collective-permute-start(bf16[48,384]{1,0:T(8,128)(2,1)S(1)} %get-tuple-element.71), channel_id=1, source_target_pairs={{6,0},{3,1},{7,2},{5,3},{1,4},{0,5},{4,6},{2,7},{14,8},{11,9},{15,... | collective-permute-start | bytes 110600 | tf_op jit(solution)/shard_map/ppermute | solution.py:832
  35.6 1.5 %collective-permute-start.12 = (bf16[48,384]{1,0:T(8,128)(2,1)S(1)}, bf16[48,384]{1,0:T(8,128)(2,1)S(1)}, u32[]{:S(2)}, u32[]{:S(2)}) collective-permute-start(bf16[48,384]{1,0:T(8,128)(2,1)S(1)} %get-tuple-element.71), channel_id=1, source_target_pairs={{5,0},{4,1},{0,2},{6,3},{7,4},{2,5},{3,6},{1,7},{13,8},{12,9},{8,1... | collective-permute-start | bytes 110600 | tf_op jit(solution)/shard_map/ppermute | solution.py:832
  37.1 0.7 %shard_map.133 = f32[8,48]{1,0:T(8,128)} custom-call(bf16[56,384]{1,0:T(8,128)(2,1)S(1)} %collective-permute-done.10.got_ref, f32[8,384]{1,0:T(8,128)S(1)} %get-tuple-element.72.partial_ref), custom_call_target="tpu_custom_call" | custom-call | tf_op jit(solution)/shard_map/pallas_call | solution.py:364
  37.8 1.0 %collective-permute-done.11.first_ref = bf16[48,384]{1,0:T(8,128)(2,1)S(1)} collective-permute-done((bf16[48,384]{1,0:T(8,128)(2,1)S(1)}, bf16[48,384]{1,0:T(8,128)(2,1)S(1)}, u32[]{:S(2)}, u32[]{:S(2)}) %collective-permute-start.11) | collective-permute-done | bytes 36896 | tf_op jit(solution)/shard_map/ppermute | solution.py:832
  38.8 0.2 collective-permute-done.12.second_ref
  39.0 0.7 %shard_map.132 = f32[144,384]{1,0:T(8,128)} custom-call(f32[48,384]{1,0:T(8,128)S(1)} %get-tuple-element.70.own_ref, bf16[48,384]{1,0:T(8,128)(2,1)S(1)} %collective-permute-done.11.first_ref, bf16[48,384]{1,0:T(8,128)(2,1)S(1)} %collective-permute-done.12.second_ref), custom_call_target="tpu_custom_call" | custom-call | tf_op jit(solution)/shard_map/pallas_call | solution.py:364
  (15 shorter events, 0.1 us)
Async XLA Ops:
  0.6 7.7 %collective-permute-start.2 = (bf16[2,3,192,384]{3,2,1,0:T(8,128)(2,1)}, bf16[2,3,192,384]{3,2,1,0:T(8,128)(2,1)S(1)}, u32[]{:S(2)}, u32[]{:S(2)}) collective-permute-start(bf16[2,3,192,384]{3,2,1,0:T(8,128)(2,1)} %bitcast.2), channel_id=1, source_target_pairs={{0,1},{1,0},{2,3},{3,2},{4,5},{5,4},{6,7},{7,6},{8,9},{9,8},{10,11... | collective-permute-start | bytes 2654216 | tf_op jit(solution)/shard_map/ppermute | solution.py:704
  1.1 5.4 %copy-start.9 = (f32[768]{0:T(1024)S(1)}, f32[768]{0:T(1024)}, u32[]{:S(2)}) copy-start(f32[768]{0:T(1024)} %param.13) | copy-start | bytes 9220
  1.2 7.2 %copy-start = (bf16[2,3,384,192]{2,3,1,0:T(8,128)(2,1)S(1)}, bf16[2,3,384,192]{2,3,1,0:T(8,128)(2,1)}, u32[]{:S(2)}) copy-start(bf16[2,3,384,192]{2,3,1,0:T(8,128)(2,1)} %param.15) | copy-start | bytes 2654212
  1.2 7.2 %copy-start.1 = (bf16[2,768,192]{1,2,0:T(8,128)(2,1)S(1)}, bf16[2,768,192]{1,2,0:T(8,128)(2,1)}, u32[]{:S(2)}) copy-start(bf16[2,768,192]{1,2,0:T(8,128)(2,1)} %param.14) | copy-start | bytes 1769476
  1.2 7.1 %collective-permute-start.1 = (bf16[2,192,768]{2,1,0:T(8,128)(2,1)}, bf16[2,192,768]{2,1,0:T(8,128)(2,1)S(1)}, u32[]{:S(2)}, u32[]{:S(2)}) collective-permute-start(bf16[2,192,768]{2,1,0:T(8,128)(2,1)} %bitcast.4), channel_id=1, source_target_pairs={{0,1},{1,0},{2,3},{3,2},{4,5},{5,4},{6,7},{7,6},{8,9},{9,8},{10,11... | collective-permute-start | bytes 1769480 | tf_op jit(solution)/shard_map/ppermute | solution.py:704
  1.3 9.4 %collective-permute-start.4 = (bf16[2,384,384]{2,1,0:T(8,128)(2,1)}, bf16[2,384,384]{2,1,0:T(8,128)(2,1)S(1)}, u32[]{:S(2)}, u32[]{:S(2)}) collective-permute-start(bf16[2,384,384]{2,1,0:T(8,128)(2,1)} %up_ref.3), channel_id=1, source_target_pairs={{0,1},{1,0},{2,3},{3,2},{4,5},{5,4},{6,7},{7,6},{8,9},{9,8},{10,11... | collective-permute-start | bytes 1769480 | tf_op jit(solution)/shard_map/ppermute | solution.py:704
  2.8 5.4 %collective-permute-start = (bf16[1,8,896]{2,1,0:T(8,128)(2,1)S(1)}, bf16[1,8,896]{2,1,0:T(8,128)(2,1)S(1)}, u32[]{:S(2)}, u32[]{:S(2)}) collective-permute-start(bf16[1,8,896]{2,1,0:T(8,128)(2,1)S(1)} %shard_map.121.first_ref), channel_id=1, source_target_pairs={{0,8},{1,9},{2,10},{3,11},{4,12},{5,13},{6,14},{7,15},{8,0},{9,1},... | collective-permute-start | bytes 43016 | tf_op jit(solution)/shard_map/ppermute | solution.py:712
  8.3 2.4 %copy-start.2 = (bf16[2,384,384]{2,1,0:T(8,128)(2,1)S(1)}, bf16[2,384,384]{2,1,0:T(8,128)(2,1)}, u32[]{:S(2)}) copy-start(bf16[2,384,384]{2,1,0:T(8,128)(2,1)} %up_ref.3) | copy-start | bytes 1769476
  8.3 2.4 %copy-start.3 = (bf16[1,128,768]{2,1,0:T(8,128)(2,1)S(1)}, bf16[1,128,768]{2,1,0:T(8,128)(2,1)}, u32[]{:S(2)}) copy-start(bf16[1,128,768]{2,1,0:T(8,128)(2,1)} %feature_ref.1) | copy-start | bytes 589828
  8.3 2.4 %copy-start.6 = (s32[1,128]{1,0:T(1,128)S(1)}, s32[1,128]{1,0:T(1,128)}, u32[]{:S(2)}) copy-start(s32[1,128]{1,0:T(1,128)} %count_ref.1) | copy-start | bytes 1540
  8.6 4.1 %copy-start.8 = (f32[4]{0:T(128)S(1)}, f32[4]{0:T(128)}, u32[]{:S(2)}) copy-start(f32[4]{0:T(128)} %decay_ref.1) | copy-start | bytes 52
  8.6 6.0 %copy-start.4 = (bf16[1,128,768]{2,1,0:T(8,128)(2,1)S(1)}, bf16[1,128,768]{2,1,0:T(8,128)(2,1)}, u32[]{:S(2)}) copy-start(bf16[1,128,768]{2,1,0:T(8,128)(2,1)} %cot_ref.1) | copy-start | bytes 589828
  8.6 6.0 %copy-start.5 = (f32[2,4,768]{2,1,0:T(4,128)S(1)}, f32[2,4,768]{2,1,0:T(4,128)}, u32[]{:S(2)}) copy-start(f32[2,4,768]{2,1,0:T(4,128)} %mode_ref.3) | copy-start | bytes 73732
  8.6 6.0 %copy-start.7 = (f32[1,128]{1,0:T(1,128)S(1)}, f32[1,128]{1,0:T(1,128)}, u32[]{:S(2)}) copy-start(f32[1,128]{1,0:T(1,128)} %keep_ref.1) | copy-start | bytes 1540
  8.6 3.9 %collective-permute-start.3 = (bf16[2,8,896]{2,1,0:T(8,128)(2,1)S(1)}, bf16[2,8,896]{2,1,0:T(8,128)(2,1)S(1)}, u32[]{:S(2)}, u32[]{:S(2)}) collective-permute-start(bf16[2,8,896]{2,1,0:T(8,128)(2,1)S(1)} %pad_maximum_fusion.1), channel_id=1, source_target_pairs={{0,4},{1,3},{2,6},{3,1},{4,0},{5,7},{6,2},{7,5},{8,12},{9,11},{10,... | collective-permute-start | bytes 86024 | tf_op jit(solution)/shard_map/ppermute | solution.py:712
  12.6 3.5 %collective-permute-start.5 = (bf16[256,384]{1,0:T(8,128)(2,1)S(1)}, bf16[256,384]{1,0:T(8,128)(2,1)S(1)}, u32[]{:S(2)}, u32[]{:S(2)}) collective-permute-start(bf16[256,384]{1,0:T(8,128)(2,1)S(1)} %get-tuple-element.45.reduced_ref), channel_id=1, source_target_pairs={{0,1},{1,0},{2,3},{3,2},{4,5},{5,4},{6,7},{7,6},{8,9},{9,8},{10,11... | collective-permute-start | bytes 589832 | tf_op jit(solution)/shard_map/ppermute | solution.py:704
  12.7 4.2 %collective-permute-start.6 = (bf16[4,8,896]{2,1,0:T(8,128)(2,1)S(1)}, bf16[4,8,896]{2,1,0:T(8,128)(2,1)S(1)}, u32[]{:S(2)}, u32[]{:S(2)}) collective-permute-start(bf16[4,8,896]{2,1,0:T(8,128)(2,1)S(1)} %pad_maximum_fusion), channel_id=1, source_target_pairs={{0,2},{1,5},{2,0},{3,7},{4,6},{5,1},{6,4},{7,3},{8,10},{9,13},{10,... | collective-permute-start | bytes 172040 | tf_op jit(solution)/shard_map/ppermute | solution.py:712
  18.4 1.5 %collective-permute-start.7 = (bf16[288,384]{1,0:T(8,128)(2,1)S(1)}, bf16[288,384]{1,0:T(8,128)(2,1)S(1)}, u32[]{:S(2)}, u32[]{:S(2)}) collective-permute-start(bf16[288,384]{1,0:T(8,128)(2,1)S(1)} %get-tuple-element.57.mixed_ref), channel_id=1, source_target_pairs={{0,1},{1,0},{2,3},{3,2},{4,5},{5,4},{6,7},{7,6},{8,9},{9,8},{10,11... | collective-permute-start | bytes 663560 | tf_op jit(solution)/shard_map/ppermute | solution.py:704
  20.3 4.8 %collective-permute-start.8 = (bf16[208,384]{1,0:T(8,128)(2,1)S(1)}, bf16[208,384]{1,0:T(8,128)(2,1)S(1)}, u32[]{:S(2)}, u32[]{:S(2)}) collective-permute-start(bf16[208,384]{1,0:T(8,128)(2,1)S(1)} %get-tuple-element.60), channel_id=1, source_target_pairs={{0,3},{1,4},{2,7},{3,0},{4,1},{5,6},{6,5},{7,2},{8,13},{9,10},{10,... | collective-permute-start | bytes 479240 | tf_op jit(solution)/shard_map/ppermute | solution.py:712
  25.1 4.0 %collective-permute-start.9 = (bf16[112,384]{1,0:T(8,128)(2,1)S(1)}, bf16[112,384]{1,0:T(8,128)(2,1)S(1)}, u32[]{:S(2)}, u32[]{:S(2)}) collective-permute-start(bf16[112,384]{1,0:T(8,128)(2,1)S(1)} %get-tuple-element.66), channel_id=1, source_target_pairs={{0,5},{1,2},{2,1},{3,6},{4,7},{5,0},{6,3},{7,4},{8,11},{9,12},{10,... | collective-permute-start | bytes 258056 | tf_op jit(solution)/shard_map/ppermute | solution.py:712
  29.1 4.4 %collective-permute-start.10 = (bf16[56,384]{1,0:T(8,128)(2,1)S(1)}, bf16[56,384]{1,0:T(8,128)(2,1)S(1)}, u32[]{:S(2)}, u32[]{:S(2)}) collective-permute-start(bf16[56,384]{1,0:T(8,128)(2,1)S(1)} %get-tuple-element.69), channel_id=1, source_target_pairs={{0,9},{1,8},{2,11},{3,10},{4,13},{5,12},{6,15},{7,14},{8,1},{9,0},... | collective-permute-start | bytes 129032 | tf_op jit(solution)/shard_map/ppermute | solution.py:712
  33.5 5.3 %collective-permute-start.11 = (bf16[48,384]{1,0:T(8,128)(2,1)S(1)}, bf16[48,384]{1,0:T(8,128)(2,1)S(1)}, u32[]{:S(2)}, u32[]{:S(2)}) collective-permute-start(bf16[48,384]{1,0:T(8,128)(2,1)S(1)} %get-tuple-element.71), channel_id=1, source_target_pairs={{6,0},{3,1},{7,2},{5,3},{1,4},{0,5},{4,6},{2,7},{14,8},{11,9},{15,... | collective-permute-start | bytes 110600 | tf_op jit(solution)/shard_map/ppermute | solution.py:832
  35.6 3.4 %collective-permute-start.12 = (bf16[48,384]{1,0:T(8,128)(2,1)S(1)}, bf16[48,384]{1,0:T(8,128)(2,1)S(1)}, u32[]{:S(2)}, u32[]{:S(2)}) collective-permute-start(bf16[48,384]{1,0:T(8,128)(2,1)S(1)} %get-tuple-element.71), channel_id=1, source_target_pairs={{5,0},{4,1},{0,2},{6,3},{7,4},{2,5},{3,6},{1,7},{13,8},{12,9},{8,1... | collective-permute-start | bytes 110600 | tf_op jit(solution)/shard_map/ppermute | solution.py:832

commit v8 on v7

--- a/solution.py
+++ b/solution.py
@@ -440,19 +440,18 @@
     pay_ref[0, :, :width] = (states[0:8] + states[8:16]).astype(BF16)
 
 
-def assemble_body(down_ref, down_far_ref, tap_ref, tap_far_ref, down_out, tap_out):
+def assemble_body(tap_ref, tap_far_ref, tap_out):
     core = lax.axis_index("dp")
-    half = down_ref.shape[1]
-    for down, taps, side in ((down_ref, tap_ref, core), (down_far_ref, tap_far_ref, 1 - core)):
+    half = tap_ref.shape[2]
+    for taps, side in ((tap_ref, core), (tap_far_ref, 1 - core)):
         part = pl.ds(pl.multiple_of(side * half, half), half)
         for layer in range(LAYERS):
-            down_out[layer, part, :] = down[layer]
             total = taps[layer, 0].astype(F32) + taps[layer, 1].astype(F32) + taps[layer, 2].astype(F32)
             tap_out[layer, part, :] = total.astype(BF16)
 
 
 def forward_body(
-    feature_ref, count_ref, weight_ref, down_ref, tap_ref, up_ref, up_far_ref,
+    feature_ref, count_ref, weight_ref, down_ref, down_far_ref, tap_ref, up_ref, up_far_ref,
     stream_ref, inverse_ref, reduced_ref, slope_ref,
 ):
     core = lax.axis_index("dp")
@@ -467,7 +466,10 @@
         inverse = lax.rsqrt(mean + EPSILON)
         inverse_ref[layer] = inverse
         normed = (stream * inverse).astype(BF16)
-        reduced = dot_nt(normed, down_ref[layer]).astype(BF16)
+        near = dot_nt(normed, down_ref[layer])
+        away = dot_nt(normed, down_far_ref[layer])
+        straight = jnp.concatenate([near, away], axis=-1)
+        reduced = jnp.where(core == 0, straight, jnp.concatenate([away, near], axis=-1)).astype(BF16)
         reduced_ref[layer * rows : (layer + 1) * rows, :] = reduced
         mixture = dot_nt(reduced, tap_ref[layer])
         share = 0.5 * (1.0 + lax.erf(mixture * HALF_ROOT))
@@ -481,8 +483,13 @@
     stream_ref[LAYERS] = stream
 
 
-def local_body(decay_ref, scale_ref, cot_ref, keep_ref, mode_ref, stream_ref, grad_ref, mark_ref, reach_ref, edge_ref, rate_ref):
+def local_body(decay_ref, scale_ref, cot_ref, keep_ref, mode_ref, stream_ref, down_ref, down_far_ref, down_out, grad_ref, mark_ref, reach_ref, edge_ref, rate_ref):
     rows, width = cot_ref.shape[1:]
+    core = lax.axis_index("dp")
+    half = down_ref.shape[1]
+    for down, side in ((down_ref, core), (down_far_ref, 1 - core)):
+        for layer in range(LAYERS):
+            down_out[layer, pl.ds(pl.multiple_of(side * half, half), half), :] = down[layer]
     column, row, total = log_sums(keep_ref[...])
     below = iota2((rows, rows), 0)
     across = iota2((rows, rows), 1)
@@ -739,19 +746,16 @@
         size=1300 * GIGA,
     )
     got = hop_to(pay, lambda core, place: (0, HOPS[0]))
-    down_full, tap_full = call(
-        assemble_body,
-        (down, down_far, taps, taps_far),
-        (VMEM,) * 4,
-        (((LAYERS, B, width), BF16), ((LAYERS, B, B), BF16)), size=1200 * GIGA
+    (tap_full,) = call(
+        assemble_body, (taps, taps_far), (VMEM,) * 2, (((LAYERS, B, B), BF16),), size=1200 * GIGA
     )
     two = jnp.concatenate([pay, got], axis=0)
-    two, down_full, tap_full = lax.optimization_barrier((two, down_full, tap_full))
+    two, down_far, tap_full = lax.optimization_barrier((two, down_far, tap_full))
     got_two = hop_to(two, lambda core, place: (0, HOPS[1 + core]))
     stream, inverse, reduced, slope = call(
         forward_body,
-        (features, counts, count_weight[None], down_full, tap_full, up_weight, up_far),
-        (VMEM,) * 7,
+        (features, counts, count_weight[None], down, down_far, tap_full, up_weight, up_far),
+        (VMEM,) * 8,
         (
             ((LAYERS + 1, rows, width), F32),
             ((LAYERS, rows, 1), F32),
@@ -763,11 +767,11 @@
     four, stream, reduced = lax.optimization_barrier((four, stream, reduced))
     got_four = hop_to(four, lambda core, place: (0, HOPS[2 - core]))
     reduced_far = swap(reduced, "dp", 1)
-    local, mark, reach, edge, rate = call(
+    down_full, local, mark, reach, edge, rate = call(
         local_body,
-        (decay_rate, scale, cotangent, keep_share, mode_weight, stream),
-        (SMEM, SMEM) + (VMEM,) * 4,
-        (((rows, width), F32), ((8, width), F32), ((8, width), F32), ((32, rows), BF16), ((2, 8, 128), F32)), size=1600 * GIGA
+        (decay_rate, scale, cotangent, keep_share, mode_weight, stream, down, down_far),
+        (SMEM, SMEM) + (VMEM,) * 6,
+        (((LAYERS, B, width), BF16), ((rows, width), F32), ((8, width), F32), ((8, width), F32), ((32, rows), BF16), ((2, 8, 128), F32)), size=1600 * GIGA
     )
     local, reduced_far = lax.optimization_barrier((local, reduced_far))
     gradient, mixed, partial = call(

time: 39.9 us -> 39.8 us (level)
  transfers between devices with their start and end apart: 13 -> 13, of which waited for: 9 -> 8; matrix products, arithmetic and copies ran while one was open for 0% -> 0% of each run, Pallas kernels for 17% -> 17%
where the time goes in v8:
time: 39.8 us; the launch traced here: 39.7 us
  starting transfers between devices  18.4 us (46%)
  waiting for transfers between devices  10.9 us (27%)
  Pallas kernels  9.43 us (24%)
  between operations  0.85 us (2%)
    ppermute x6, starting transfers between devices, hop_to(): return lax.ppermute(value, ('seq', 'dp'), pairs)  13.7 us
    pallas_call x13, Pallas kernels, call(): pl.pallas_call(body, out_shape=[jax.ShapeDtypeStruct(shape, dtype) for sh...  9.43 us
    ppermute x6, waiting for transfers between devices, hop_to(): return lax.ppermute(value, ('seq', 'dp'), pairs)  8.34 us
    ppermute x2, starting transfers between devices, wrapped_device(): parts.append(lax.ppermute(narrow, ('seq', 'dp'), pairs))  3.61 us
    ppermute x5, waiting for transfers between devices, swap(): lax.ppermute(value, axis, [(source, source ^ mask) for source in range(co...  1.31 us
    ppermute x2, waiting for transfers between devices, wrapped_device(): parts.append(lax.ppermute(narrow, ('seq', 'dp'), pairs))  1.22 us
    ppermute x5, starting transfers between devices, swap(): lax.ppermute(value, axis, [(source, source ^ mask) for source in range(co...  1.17 us
  transfers between devices with their start and end apart: 13, of which 8 were waited for; matrix products, arithmetic and copies ran while one was open for 0% of the time, Pallas kernels for 17%

profile of v8, /device:TPU:0, one launch (start us, length us, event | category | flops | bytes accessed | tf_op | source)
XLA Modules:
  0.0 39.7 jit_solution(2482479842985295501)
XLA Ops:
  0.6 0.5 %collective-permute-start.2 = (bf16[2,3,192,384]{3,2,1,0:T(8,128)(2,1)}, bf16[2,3,192,384]{3,2,1,0:T(8,128)(2,1)S(1)}, u32[]{:S(2)}, u32[]{:S(2)}) collective-permute-start(bf16[2,3,192,384]{3,2,1,0:T(8,128)(2,1)} %bitcast.2), channel_id=1, source_target_pairs={{0,1},{1,0},{2,3},{3,2},{4,5},{5,4},{6,7},{7,6},{8,9},{9,8},{10,11... | collective-permute-start | bytes 2654216 | tf_op jit(solution)/shard_map/ppermute | solution.py:711
  1.2 0.1 collective-permute-start.1
  1.2 0.4 %collective-permute-start.4 = (bf16[2,384,384]{2,1,0:T(8,128)(2,1)}, bf16[2,384,384]{2,1,0:T(8,128)(2,1)S(1)}, u32[]{:S(2)}, u32[]{:S(2)}) collective-permute-start(bf16[2,384,384]{2,1,0:T(8,128)(2,1)} %up_ref.3), channel_id=1, source_target_pairs={{0,1},{1,0},{2,3},{3,2},{4,5},{5,4},{6,7},{7,6},{8,9},{9,8},{10,11... | collective-permute-start | bytes 1769480 | tf_op jit(solution)/shard_map/ppermute | solution.py:711
  1.7 1.1 %shard_map.121.first_ref = bf16[1,8,896]{2,1,0:T(8,128)(2,1)S(1)} custom-call(bf16[1,128,768]{2,1,0:T(8,128)(2,1)} %cot_ref.1, f32[1,128]{1,0:T(1,128)} %keep_ref.1, f32[4]{0:T(128)} %decay_ref.1), custom_call_target="tpu_custom_call" | custom-call | flops 1300000000 | bytes 5078125 | tf_op jit(solution)/shard_map/pallas_call | solution.py:364
  2.8 3.7 %collective-permute-start = (bf16[1,8,896]{2,1,0:T(8,128)(2,1)S(1)}, bf16[1,8,896]{2,1,0:T(8,128)(2,1)S(1)}, u32[]{:S(2)}, u32[]{:S(2)}) collective-permute-start(bf16[1,8,896]{2,1,0:T(8,128)(2,1)S(1)} %shard_map.121.first_ref), channel_id=1, source_target_pairs={{0,8},{1,9},{2,10},{3,11},{4,12},{5,13},{6,14},{7,15},{8,0},{9,1},... | collective-permute-start | bytes 43016 | tf_op jit(solution)/shard_map/ppermute | solution.py:719
  6.5 1.7 %collective-permute-done.second_ref = bf16[1,8,896]{2,1,0:T(8,128)(2,1)S(1)} collective-permute-done((bf16[1,8,896]{2,1,0:T(8,128)(2,1)S(1)}, bf16[1,8,896]{2,1,0:T(8,128)(2,1)S(1)}, u32[]{:S(2)}, u32[]{:S(2)}) %collective-permute-start) | collective-permute-done | bytes 14368 | tf_op jit(solution)/shard_map/ppermute | solution.py:719
  8.2 0.0 copy-start.1
  8.3 0.0 copy-start.2
  8.3 0.0 copy-start.3
  8.3 0.0 copy-start.6
  8.3 0.0 collective-permute-done.2.tap_far_ref
  8.3 0.2 shard_map.122.tap_ref
  8.5 0.0 copy-start.8
  8.6 0.0 copy-start.4
  8.6 0.0 copy-start.5
  8.6 0.0 copy-start.7
  8.6 0.0 collective-permute-done.1.down_far_ref
  8.6 2.0 %collective-permute-start.3 = (bf16[2,8,896]{2,1,0:T(8,128)(2,1)S(1)}, bf16[2,8,896]{2,1,0:T(8,128)(2,1)S(1)}, u32[]{:S(2)}, u32[]{:S(2)}) collective-permute-start(bf16[2,8,896]{2,1,0:T(8,128)(2,1)S(1)} %pad_maximum_fusion.1), channel_id=1, source_target_pairs={{0,4},{1,3},{2,6},{3,1},{4,0},{5,7},{6,2},{7,5},{8,12},{9,11},{10,... | collective-permute-start | bytes 86024 | tf_op jit(solution)/shard_map/ppermute | solution.py:719
  10.6 0.0 collective-permute-done.4.up_far_ref
  10.6 0.0 copy-done.2
  10.6 0.0 copy-done.3
  10.6 0.0 copy-done.6
  10.6 1.9 %shard_map.123 = (f32[3,128,768]{2,1,0:T(8,128)S(1)}, f32[2,128,1]{2,1,0:T(8,128)S(1)}, bf16[256,384]{1,0:T(8,128)(2,1)S(1)}, f32[2,128,384]{2,1,0:T(8,128)S(1)}) custom-call(bf16[1,128,768]{2,1,0:T(8,128)(2,1)S(1)} %copy-done.3, s32[1,128]{1,0:T(1,128)S(1)} %copy-done.6, f32[1,768]{1,0:T(1,128)S(1)} %broadcast_in_dim.3.weight_ref, ...), custom_call_target="tpu_custom_call" | custom-call | flops 1800000000 | bytes 7031250 | tf_op jit(solution)/shard_map/pallas_call | solution.py:364
  12.5 0.0 collective-permute-done.3.third_ref
  12.5 0.1 collective-permute-start.5
  12.7 1.9 %collective-permute-start.6 = (bf16[4,8,896]{2,1,0:T(8,128)(2,1)S(1)}, bf16[4,8,896]{2,1,0:T(8,128)(2,1)S(1)}, u32[]{:S(2)}, u32[]{:S(2)}) collective-permute-start(bf16[4,8,896]{2,1,0:T(8,128)(2,1)S(1)} %pad_maximum_fusion), channel_id=1, source_target_pairs={{0,2},{1,5},{2,0},{3,7},{4,6},{5,1},{6,4},{7,3},{8,10},{9,13},{10,... | collective-permute-start | bytes 172040 | tf_op jit(solution)/shard_map/ppermute | solution.py:719
  14.5 0.0 copy-done.4
  14.5 1.5 %shard_map.124 = (bf16[2,384,768]{2,1,0:T(8,128)(2,1)S(1)}, f32[128,768]{1,0:T(8,128)S(1)}, f32[8,768]{1,0:T(8,128)S(1)}, f32[8,768]{1,0:T(8,128)S(1)}, bf16[32,...) custom-call(f32[4]{0:T(128)S(1)} %copy-done.8, f32[4]{0:T(128)S(1)} %negate_sqrt_fusion.scale_ref, ...), custom_call_target="tpu_custom_call" | custom-call | flops 1600000000 | bytes 6250000 | tf_op jit(solution)/shard_map/pallas_call | solution.py:364
  16.1 0.0 collective-permute-done.5.reduced_far_ref
  16.1 0.8 %collective-permute-done.6.fourth_ref = bf16[4,8,896]{2,1,0:T(8,128)(2,1)S(1)} collective-permute-done((bf16[4,8,896]{2,1,0:T(8,128)(2,1)S(1)}, bf16[4,8,896]{2,1,0:T(8,128)(2,1)S(1)}, u32[]{:S(2)}, u32[]{:S(2)}) %collective-permute-start.6) | collective-permute-done | bytes 57376 | tf_op jit(solution)/shard_map/ppermute | solution.py:719
  16.9 1.5 %shard_map.126 = (f32[128,768]{1,0:T(8,128)S(1)}, bf16[288,384]{1,0:T(8,128)(2,1)S(1)}, f32[16,384]{1,0:T(8,128)S(1)}) custom-call(bf16[1,8,896]{2,1,0:T(8,128)(2,1)S(1)} %shard_map.121.first_ref, bf16[1,8,896]{2,1,0:T(8,128)(2,1)S(1)} %collective-permute-done.second_ref, bf16[2,8,896]{2,1,0:T(8,128)(2,1)S(1)} %collective-permute-done.3.third_ref, ...), custom_call_target="tpu_custom_call" | custom-call | flops 2100000000 | bytes 8203125 | tf_op jit(solution)/shard_map/pallas_call | solution.py:364
  18.4 0.1 collective-permute-start.7
  18.5 0.2 shard_map.125.left_ref
  18.6 1.3 %collective-permute-done.7.mixed_far_ref = bf16[288,384]{1,0:T(8,128)(2,1)S(1)} collective-permute-done((bf16[288,384]{1,0:T(8,128)(2,1)S(1)}, bf16[288,384]{1,0:T(8,128)(2,1)S(1)}, u32[]{:S(2)}, u32[]{:S(2)}) %collective-permute-start.7) | collective-permute-done | bytes 221216 | tf_op jit(solution)/shard_map/ppermute | solution.py:711
  19.9 0.3 shard_map.127
  20.2 1.6 %collective-permute-start.8 = (bf16[208,384]{1,0:T(8,128)(2,1)S(1)}, bf16[208,384]{1,0:T(8,128)(2,1)S(1)}, u32[]{:S(2)}, u32[]{:S(2)}) collective-permute-start(bf16[208,384]{1,0:T(8,128)(2,1)S(1)} %get-tuple-element.58), channel_id=1, source_target_pairs={{0,3},{1,4},{2,7},{3,0},{4,1},{5,6},{6,5},{7,2},{8,13},{9,10},{10,... | collective-permute-start | bytes 479240 | tf_op jit(solution)/shard_map/ppermute | solution.py:719
  21.8 1.3 %shard_map.129 = bf16[1,128,768]{2,1,0:T(8,128)(2,1)} custom-call(f32[128,768]{1,0:T(8,128)S(1)} %get-tuple-element.61.gradient_ref, bf16[288,384]{1,0:T(8,128)(2,1)S(1)} %get-tuple-element.55.mixed_ref, f32[3,128,768]{2,1,0:T(8,128)S(1)} %get-tuple-element.43.stream_ref, f32[2,128,1]{2,1,0:T(8,128)S(1)} %get-tuple-element.52.inverse_ref, ...), custom_call_target="tpu_custom_call" | custom-call | flops 1300000000 | bytes 5078125 | tf_op jit(solution)/shard_map/pallas_call | solution.py:364
  23.2 1.8 %collective-permute-done.8.got_ref = bf16[208,384]{1,0:T(8,128)(2,1)S(1)} collective-permute-done((bf16[208,384]{1,0:T(8,128)(2,1)S(1)}, bf16[208,384]{1,0:T(8,128)(2,1)S(1)}, u32[]{:S(2)}, u32[]{:S(2)}) %collective-permute-start.8) | collective-permute-done | bytes 159776 | tf_op jit(solution)/shard_map/ppermute | solution.py:719
  25.0 1.7 %collective-permute-start.9 = (bf16[112,384]{1,0:T(8,128)(2,1)S(1)}, bf16[112,384]{1,0:T(8,128)(2,1)S(1)}, u32[]{:S(2)}, u32[]{:S(2)}) collective-permute-start(bf16[112,384]{1,0:T(8,128)(2,1)S(1)} %get-tuple-element.64), channel_id=1, source_target_pairs={{0,5},{1,2},{2,1},{3,6},{4,7},{5,0},{6,3},{7,4},{8,11},{9,12},{10,... | collective-permute-start | bytes 258056 | tf_op jit(solution)/shard_map/ppermute | solution.py:719
  26.7 2.3 %collective-permute-done.9.got_ref = bf16[112,384]{1,0:T(8,128)(2,1)S(1)} collective-permute-done((bf16[112,384]{1,0:T(8,128)(2,1)S(1)}, bf16[112,384]{1,0:T(8,128)(2,1)S(1)}, u32[]{:S(2)}, u32[]{:S(2)}) %collective-permute-start.9) | collective-permute-done | bytes 86048 | tf_op jit(solution)/shard_map/ppermute | solution.py:719
  29.0 2.7 %collective-permute-start.10 = (bf16[56,384]{1,0:T(8,128)(2,1)S(1)}, bf16[56,384]{1,0:T(8,128)(2,1)S(1)}, u32[]{:S(2)}, u32[]{:S(2)}) collective-permute-start(bf16[56,384]{1,0:T(8,128)(2,1)S(1)} %get-tuple-element.67), channel_id=1, source_target_pairs={{0,9},{1,8},{2,11},{3,10},{4,13},{5,12},{6,15},{7,14},{8,1},{9,0},... | collective-permute-start | bytes 129032 | tf_op jit(solution)/shard_map/ppermute | solution.py:719
  31.7 1.7 %collective-permute-done.10.got_ref = bf16[56,384]{1,0:T(8,128)(2,1)S(1)} collective-permute-done((bf16[56,384]{1,0:T(8,128)(2,1)S(1)}, bf16[56,384]{1,0:T(8,128)(2,1)S(1)}, u32[]{:S(2)}, u32[]{:S(2)}) %collective-permute-start.10) | collective-permute-done | bytes 43040 | tf_op jit(solution)/shard_map/ppermute | solution.py:719
  33.5 2.1 %collective-permute-start.11 = (bf16[48,384]{1,0:T(8,128)(2,1)S(1)}, bf16[48,384]{1,0:T(8,128)(2,1)S(1)}, u32[]{:S(2)}, u32[]{:S(2)}) collective-permute-start(bf16[48,384]{1,0:T(8,128)(2,1)S(1)} %get-tuple-element.69), channel_id=1, source_target_pairs={{6,0},{3,1},{7,2},{5,3},{1,4},{0,5},{4,6},{2,7},{14,8},{11,9},{15,... | collective-permute-start | bytes 110600 | tf_op jit(solution)/shard_map/ppermute | solution.py:836
  35.6 1.5 %collective-permute-start.12 = (bf16[48,384]{1,0:T(8,128)(2,1)S(1)}, bf16[48,384]{1,0:T(8,128)(2,1)S(1)}, u32[]{:S(2)}, u32[]{:S(2)}) collective-permute-start(bf16[48,384]{1,0:T(8,128)(2,1)S(1)} %get-tuple-element.69), channel_id=1, source_target_pairs={{5,0},{4,1},{0,2},{6,3},{7,4},{2,5},{3,6},{1,7},{13,8},{12,9},{8,1... | collective-permute-start | bytes 110600 | tf_op jit(solution)/shard_map/ppermute | solution.py:836
  37.1 0.7 %shard_map.133 = f32[8,48]{1,0:T(8,128)} custom-call(bf16[56,384]{1,0:T(8,128)(2,1)S(1)} %collective-permute-done.10.got_ref, f32[8,384]{1,0:T(8,128)S(1)} %get-tuple-element.70.partial_ref), custom_call_target="tpu_custom_call" | custom-call | tf_op jit(solution)/shard_map/pallas_call | solution.py:364
  37.8 1.0 %collective-permute-done.11.first_ref = bf16[48,384]{1,0:T(8,128)(2,1)S(1)} collective-permute-done((bf16[48,384]{1,0:T(8,128)(2,1)S(1)}, bf16[48,384]{1,0:T(8,128)(2,1)S(1)}, u32[]{:S(2)}, u32[]{:S(2)}) %collective-permute-start.11) | collective-permute-done | bytes 36896 | tf_op jit(solution)/shard_map/ppermute | solution.py:836
  38.8 0.2 collective-permute-done.12.second_ref
  39.0 0.7 %shard_map.132 = f32[144,384]{1,0:T(8,128)} custom-call(f32[48,384]{1,0:T(8,128)S(1)} %get-tuple-element.68.own_ref, bf16[48,384]{1,0:T(8,128)(2,1)S(1)} %collective-permute-done.11.first_ref, bf16[48,384]{1,0:T(8,128)(2,1)S(1)} %collective-permute-done.12.second_ref), custom_call_target="tpu_custom_call" | custom-call | tf_op jit(solution)/shard_map/pallas_call | solution.py:364
  (15 shorter events, 0.1 us)
Async XLA Ops:
  0.6 7.7 %collective-permute-start.2 = (bf16[2,3,192,384]{3,2,1,0:T(8,128)(2,1)}, bf16[2,3,192,384]{3,2,1,0:T(8,128)(2,1)S(1)}, u32[]{:S(2)}, u32[]{:S(2)}) collective-permute-start(bf16[2,3,192,384]{3,2,1,0:T(8,128)(2,1)} %bitcast.2), channel_id=1, source_target_pairs={{0,1},{1,0},{2,3},{3,2},{4,5},{5,4},{6,7},{7,6},{8,9},{9,8},{10,11... | collective-permute-start | bytes 2654216 | tf_op jit(solution)/shard_map/ppermute | solution.py:711
  1.1 5.4 %copy-start.9 = (f32[768]{0:T(1024)S(1)}, f32[768]{0:T(1024)}, u32[]{:S(2)}) copy-start(f32[768]{0:T(1024)} %param.13) | copy-start | bytes 9220
  1.2 7.2 %copy-start = (bf16[2,3,384,192]{2,3,1,0:T(8,128)(2,1)S(1)}, bf16[2,3,384,192]{2,3,1,0:T(8,128)(2,1)}, u32[]{:S(2)}) copy-start(bf16[2,3,384,192]{2,3,1,0:T(8,128)(2,1)} %param.15) | copy-start | bytes 2654212
  1.2 7.4 %collective-permute-start.1 = (bf16[2,192,768]{2,1,0:T(8,128)(2,1)}, bf16[2,192,768]{2,1,0:T(8,128)(2,1)S(1)}, u32[]{:S(2)}, u32[]{:S(2)}) collective-permute-start(bf16[2,192,768]{2,1,0:T(8,128)(2,1)} %bitcast.4), channel_id=1, source_target_pairs={{0,1},{1,0},{2,3},{3,2},{4,5},{5,4},{6,7},{7,6},{8,9},{9,8},{10,11... | collective-permute-start | bytes 1769480 | tf_op jit(solution)/shard_map/ppermute | solution.py:711
  1.2 9.3 %collective-permute-start.4 = (bf16[2,384,384]{2,1,0:T(8,128)(2,1)}, bf16[2,384,384]{2,1,0:T(8,128)(2,1)S(1)}, u32[]{:S(2)}, u32[]{:S(2)}) collective-permute-start(bf16[2,384,384]{2,1,0:T(8,128)(2,1)} %up_ref.3), channel_id=1, source_target_pairs={{0,1},{1,0},{2,3},{3,2},{4,5},{5,4},{6,7},{7,6},{8,9},{9,8},{10,11... | collective-permute-start | bytes 1769480 | tf_op jit(solution)/shard_map/ppermute | solution.py:711
  2.8 5.4 %collective-permute-start = (bf16[1,8,896]{2,1,0:T(8,128)(2,1)S(1)}, bf16[1,8,896]{2,1,0:T(8,128)(2,1)S(1)}, u32[]{:S(2)}, u32[]{:S(2)}) collective-permute-start(bf16[1,8,896]{2,1,0:T(8,128)(2,1)S(1)} %shard_map.121.first_ref), channel_id=1, source_target_pairs={{0,8},{1,9},{2,10},{3,11},{4,12},{5,13},{6,14},{7,15},{8,0},{9,1},... | collective-permute-start | bytes 43016 | tf_op jit(solution)/shard_map/ppermute | solution.py:719
  8.2 2.3 %copy-start.1 = (bf16[2,768,192]{1,2,0:T(8,128)(2,1)S(1)}, bf16[2,768,192]{1,2,0:T(8,128)(2,1)}, u32[]{:S(2)}) copy-start(bf16[2,768,192]{1,2,0:T(8,128)(2,1)} %param.14) | copy-start | bytes 1769476
  8.3 2.3 %copy-start.2 = (bf16[2,384,384]{2,1,0:T(8,128)(2,1)S(1)}, bf16[2,384,384]{2,1,0:T(8,128)(2,1)}, u32[]{:S(2)}) copy-start(bf16[2,384,384]{2,1,0:T(8,128)(2,1)} %up_ref.3) | copy-start | bytes 1769476
  8.3 2.3 %copy-start.3 = (bf16[1,128,768]{2,1,0:T(8,128)(2,1)S(1)}, bf16[1,128,768]{2,1,0:T(8,128)(2,1)}, u32[]{:S(2)}) copy-start(bf16[1,128,768]{2,1,0:T(8,128)(2,1)} %feature_ref.1) | copy-start | bytes 589828
  8.3 2.3 %copy-start.6 = (s32[1,128]{1,0:T(1,128)S(1)}, s32[1,128]{1,0:T(1,128)}, u32[]{:S(2)}) copy-start(s32[1,128]{1,0:T(1,128)} %count_ref.1) | copy-start | bytes 1540
  8.5 4.1 %copy-start.8 = (f32[4]{0:T(128)S(1)}, f32[4]{0:T(128)}, u32[]{:S(2)}) copy-start(f32[4]{0:T(128)} %decay_ref.1) | copy-start | bytes 52
  8.6 6.0 %copy-start.4 = (bf16[1,128,768]{2,1,0:T(8,128)(2,1)S(1)}, bf16[1,128,768]{2,1,0:T(8,128)(2,1)}, u32[]{:S(2)}) copy-start(bf16[1,128,768]{2,1,0:T(8,128)(2,1)} %cot_ref.1) | copy-start | bytes 589828
  8.6 6.0 %copy-start.5 = (f32[2,4,768]{2,1,0:T(4,128)S(1)}, f32[2,4,768]{2,1,0:T(4,128)}, u32[]{:S(2)}) copy-start(f32[2,4,768]{2,1,0:T(4,128)} %mode_ref.3) | copy-start | bytes 73732
  8.6 6.0 %copy-start.7 = (f32[1,128]{1,0:T(1,128)S(1)}, f32[1,128]{1,0:T(1,128)}, u32[]{:S(2)}) copy-start(f32[1,128]{1,0:T(1,128)} %keep_ref.1) | copy-start | bytes 1540
  8.6 3.9 %collective-permute-start.3 = (bf16[2,8,896]{2,1,0:T(8,128)(2,1)S(1)}, bf16[2,8,896]{2,1,0:T(8,128)(2,1)S(1)}, u32[]{:S(2)}, u32[]{:S(2)}) collective-permute-start(bf16[2,8,896]{2,1,0:T(8,128)(2,1)S(1)} %pad_maximum_fusion.1), channel_id=1, source_target_pairs={{0,4},{1,3},{2,6},{3,1},{4,0},{5,7},{6,2},{7,5},{8,12},{9,11},{10,... | collective-permute-start | bytes 86024 | tf_op jit(solution)/shard_map/ppermute | solution.py:719
  12.5 3.5 %collective-permute-start.5 = (bf16[256,384]{1,0:T(8,128)(2,1)S(1)}, bf16[256,384]{1,0:T(8,128)(2,1)S(1)}, u32[]{:S(2)}, u32[]{:S(2)}) collective-permute-start(bf16[256,384]{1,0:T(8,128)(2,1)S(1)} %get-tuple-element.42.reduced_ref), channel_id=1, source_target_pairs={{0,1},{1,0},{2,3},{3,2},{4,5},{5,4},{6,7},{7,6},{8,9},{9,8},{10,11... | collective-permute-start | bytes 589832 | tf_op jit(solution)/shard_map/ppermute | solution.py:711
  12.7 4.2 %collective-permute-start.6 = (bf16[4,8,896]{2,1,0:T(8,128)(2,1)S(1)}, bf16[4,8,896]{2,1,0:T(8,128)(2,1)S(1)}, u32[]{:S(2)}, u32[]{:S(2)}) collective-permute-start(bf16[4,8,896]{2,1,0:T(8,128)(2,1)S(1)} %pad_maximum_fusion), channel_id=1, source_target_pairs={{0,2},{1,5},{2,0},{3,7},{4,6},{5,1},{6,4},{7,3},{8,10},{9,13},{10,... | collective-permute-start | bytes 172040 | tf_op jit(solution)/shard_map/ppermute | solution.py:719
  18.4 1.5 %collective-permute-start.7 = (bf16[288,384]{1,0:T(8,128)(2,1)S(1)}, bf16[288,384]{1,0:T(8,128)(2,1)S(1)}, u32[]{:S(2)}, u32[]{:S(2)}) collective-permute-start(bf16[288,384]{1,0:T(8,128)(2,1)S(1)} %get-tuple-element.55.mixed_ref), channel_id=1, source_target_pairs={{0,1},{1,0},{2,3},{3,2},{4,5},{5,4},{6,7},{7,6},{8,9},{9,8},{10,11... | collective-permute-start | bytes 663560 | tf_op jit(solution)/shard_map/ppermute | solution.py:711
  20.2 4.8 %collective-permute-start.8 = (bf16[208,384]{1,0:T(8,128)(2,1)S(1)}, bf16[208,384]{1,0:T(8,128)(2,1)S(1)}, u32[]{:S(2)}, u32[]{:S(2)}) collective-permute-start(bf16[208,384]{1,0:T(8,128)(2,1)S(1)} %get-tuple-element.58), channel_id=1, source_target_pairs={{0,3},{1,4},{2,7},{3,0},{4,1},{5,6},{6,5},{7,2},{8,13},{9,10},{10,... | collective-permute-start | bytes 479240 | tf_op jit(solution)/shard_map/ppermute | solution.py:719
  25.0 4.0 %collective-permute-start.9 = (bf16[112,384]{1,0:T(8,128)(2,1)S(1)}, bf16[112,384]{1,0:T(8,128)(2,1)S(1)}, u32[]{:S(2)}, u32[]{:S(2)}) collective-permute-start(bf16[112,384]{1,0:T(8,128)(2,1)S(1)} %get-tuple-element.64), channel_id=1, source_target_pairs={{0,5},{1,2},{2,1},{3,6},{4,7},{5,0},{6,3},{7,4},{8,11},{9,12},{10,... | collective-permute-start | bytes 258056 | tf_op jit(solution)/shard_map/ppermute | solution.py:719
  29.0 4.4 %collective-permute-start.10 = (bf16[56,384]{1,0:T(8,128)(2,1)S(1)}, bf16[56,384]{1,0:T(8,128)(2,1)S(1)}, u32[]{:S(2)}, u32[]{:S(2)}) collective-permute-start(bf16[56,384]{1,0:T(8,128)(2,1)S(1)} %get-tuple-element.67), channel_id=1, source_target_pairs={{0,9},{1,8},{2,11},{3,10},{4,13},{5,12},{6,15},{7,14},{8,1},{9,0},... | collective-permute-start | bytes 129032 | tf_op jit(solution)/shard_map/ppermute | solution.py:719
  33.5 5.3 %collective-permute-start.11 = (bf16[48,384]{1,0:T(8,128)(2,1)S(1)}, bf16[48,384]{1,0:T(8,128)(2,1)S(1)}, u32[]{:S(2)}, u32[]{:S(2)}) collective-permute-start(bf16[48,384]{1,0:T(8,128)(2,1)S(1)} %get-tuple-element.69), channel_id=1, source_target_pairs={{6,0},{3,1},{7,2},{5,3},{1,4},{0,5},{4,6},{2,7},{14,8},{11,9},{15,... | collective-permute-start | bytes 110600 | tf_op jit(solution)/shard_map/ppermute | solution.py:836
  35.6 3.4 %collective-permute-start.12 = (bf16[48,384]{1,0:T(8,128)(2,1)S(1)}, bf16[48,384]{1,0:T(8,128)(2,1)S(1)}, u32[]{:S(2)}, u32[]{:S(2)}) collective-permute-start(bf16[48,384]{1,0:T(8,128)(2,1)S(1)} %get-tuple-element.69), channel_id=1, source_target_pairs={{5,0},{4,1},{0,2},{6,3},{7,4},{2,5},{3,6},{1,7},{13,8},{12,9},{8,1... | collective-permute-start | bytes 110600 | tf_op jit(solution)/shard_map/ppermute | solution.py:836
